TPU v7x, 32 devices: a whole 2x2x4 slice. The times are simulated.
32 devices in a mesh: group: 2 (over y), expert: 4 (over z), tensor: 4 (over x, core).
Axes of the slice: x: 2, y: 2, z: 4, core: 2. Of those that a mesh axis runs over, the one named last changes fastest.
Arguments:
- tokens: bfloat16 [512, 4096], P(('group', 'expert'), 'tensor'), parts along dimension 0, may hold values from -400 to 400
- norm_gain: float32 [4096], replicated, may hold values from 0.1 to 1.9
- expert_ids: int32 [512, 8], P(('group', 'expert')), parts along dimension 0, may hold values from 0 to 63, all different within a row; in each aligned block of 64 rows (0 to 63, 64 to 127, ...) at most 16 rows name the same one
- gate_weights: float32 [512, 8], P(('group', 'expert')), parts along dimension 0, may hold values from 0.1 to 1
- gate_proj: bfloat16 [64, 768, 4096], P('expert', 'tensor'), may hold values from -0.09375 to 0.09375
- up_proj: bfloat16 [64, 768, 4096], P('expert', 'tensor'), may hold values from -0.09375 to 0.09375
- down_proj: bfloat16 [64, 4096, 768], P('expert', 'tensor'), may hold values from -0.21875 to 0.21875
Outputs:
- moe_out: bfloat16 [512, 4096], P(('group', 'expert'), 'tensor'), parts along dimension 0
There are 2 independent parts, one for each index of `group`. A program takes and returns all parts, laid end to end along the dimension named above; an argument that names none is the same for every part. Nothing has to cross between parts.
Inputs may be any that keep to these rules, and one draw needn't show every extreme that they name: `expert_ids`: each row names 8 different experts. Within the rows of one device (aligned blocks of 64 rows) no expert is named by more than 16 rows, a bound that some block reaches.
All inputs are finite; a program needn't handle non-finite values.
Results may differ from a plain program's by a relative error of at most 0.008.
Values may be sent and summed in bfloat16 or wider, within the bound.
No kernel may reach another device: no remote copies, remote signals or barrier semaphores. Data moves between devices by JAX's collectives and lax.ppermute only.
A program may use at most 128 MiB of HBM per device.

v0:
```python
import jax
import jax.numpy as jnp
from jax import lax
from jax.sharding import PartitionSpec as P

D = 4096
EXPERTS = 64
TOP = 8
CAP = 16


epsilon = 1e-06


def slot_places(expert_ids):
    flat_ids = expert_ids.reshape(-1)
    onehot = (flat_ids[:, None] == jnp.arange(EXPERTS, dtype=jnp.int32)[None, :]).astype(jnp.int32)
    before = jnp.cumsum(onehot, axis=0) - onehot
    inside = jnp.sum(onehot * before, axis=1)
    return flat_ids * CAP + inside


def expert_block(slot_rows, gate_proj, up_proj, down_proj):
    sources = slot_rows.shape[0]
    local_experts = slot_rows.shape[1]
    item_count = slot_rows.shape[2]
    gate_act = jnp.einsum(
        "slcd,lfd->lfsc", slot_rows, gate_proj, preferred_element_type=jnp.float32
    )
    up_act = jnp.einsum("slcd,lfd->lfsc", slot_rows, up_proj, preferred_element_type=jnp.float32)
    hidden = (jax.nn.silu(gate_act) * up_act).astype(jnp.bfloat16)
    hidden = hidden.reshape(local_experts, hidden.shape[1], sources * item_count)
    hidden_all = lax.all_gather(hidden, "tensor", axis=1, tiled=True)
    hidden_all = hidden_all.reshape(local_experts, hidden_all.shape[1], sources, item_count)
    result = jnp.einsum(
        "lfsc,ldf->slcd", hidden_all, down_proj, preferred_element_type=jnp.float32
    ).astype(jnp.bfloat16)
    return lax.all_to_all(result, "expert", split_axis=0, concat_axis=0, tiled=True)


def body(tokens, norm_gain, expert_ids, gate_weights, gate_proj, up_proj, down_proj):
    local_experts = gate_proj.shape[0]
    groups = lax.axis_size("expert")
    tok_rows = tokens.shape[0]
    places = slot_places(expert_ids)
    owners = (
        jnp.full((EXPERTS * CAP,), tok_rows, jnp.int32)
        .at[places]
        .set(jnp.arange(places.shape[0], dtype=jnp.int32) // TOP)
    )
    values = tokens.astype(jnp.float32)
    squares = lax.psum(jnp.sum(values * values, axis=1), "tensor")
    inv_scale = lax.rsqrt(squares / D + epsilon)[:, None]
    quarter_width = tokens.shape[1]
    gain_part = lax.dynamic_slice_in_dim(
        norm_gain, lax.axis_index("tensor") * quarter_width, quarter_width
    )
    normed = (values * inv_scale * gain_part).astype(jnp.bfloat16)
    padded = jnp.concatenate([normed, jnp.zeros((1, quarter_width), jnp.bfloat16)], axis=0)
    dispatched = padded[owners].reshape(groups, local_experts, CAP, quarter_width)
    full_rows = lax.all_gather(
        lax.all_to_all(dispatched, "expert", split_axis=0, concat_axis=0, tiled=True),
        "tensor",
        axis=3,
        tiled=True,
    )
    returned = expert_block(full_rows, gate_proj, up_proj, down_proj)
    out_width = returned.shape[-1]
    flat_back = returned.reshape(EXPERTS * CAP, out_width)
    picked = flat_back[places].reshape(tok_rows, TOP, out_width).astype(jnp.float32)
    return jnp.einsum("tkd,tk->td", picked, gate_weights).astype(jnp.bfloat16)


def solution(mesh):
    return jax.shard_map(
        body,
        mesh=mesh,
        in_specs=(
            P(("group", "expert"), "tensor"),
            P(),
            P(("group", "expert"), None),
            P(("group", "expert"), None),
            P("expert", "tensor", None),
            P("expert", "tensor", None),
            P("expert", "tensor", None),
        ),
        out_specs=P(("group", "expert"), "tensor"),
        check_vma=False,
    )
```

profile of v0, /device:TPU:0, one launch (start us, length us, event | category | flops | bytes accessed | tf_op | source)
XLA Modules:
  0.0 281.1 jit_solution(12578102919068015323)
XLA Ops:
  6.5 0.8 copy.15
  7.5 0.7 broadcast_multiply_fusion
  8.2 1.2 reduce-window.6
  10.0 2.4 scatter_custom_fusion
  12.5 1.0 fusion.22
  13.5 8.4 %psum.7 = f32[64]{0:T(128)S(1)} all-reduce(f32[64]{0:T(128)S(1)} %fusion.22), channel_id=1, replica_groups=mesh['group'=2,'expert'=4,'tensor'=4] {'tensor'}, use_global_device_ids=true, to_apply=%region_1.2 | all-reduce | flops 64 | bytes 512 | tf_op jit(solution)/shard_map/psum | solution.py:52
  21.9 0.7 dynamic_slice.3
  22.6 1.0 fusion.24
  23.6 4.1 %gather_fusion = bf16[1024,1024]{1,0:T(8,128)(2,1)S(1)} fusion(bf16[65,1024]{1,0:T(8,128)(2,1)S(1)} %concatenate.3, s32[1024]{0:T(1024)S(1)} %fusion.29), kind=kCustom, calls=%fused_computation | custom fusion | bytes 4198400 | tf_op jit(solution)/shard_map/gather | solution.py:60
  27.7 51.7 %all_to_all.10 = bf16[4,16,16,1024]{3,2,1,0:T(8,128)(2,1)S(1)} all-to-all(bf16[4,16,16,1024]{3,2,1,0:T(8,128)(2,1)S(1)} %bitcast.72), channel_id=1, replica_groups=mesh['group'=2,'expert'=4,'tensor'=4] {'expert'}, dimensions={0} | all-to-all | bytes 4194304 | tf_op jit(solution)/shard_map/all_to_all | solution.py:62
  79.3 1.6 copy.18
  81.2 57.3 %all-gather.3.cloned.1.call-done = bf16[4,16,16,4096]{3,2,0,1:T(8,128)(2,1)} async-done(((bf16[4,16,16,1024]{3,2,0,1:T(8,128)(2,1)}), bf16[4,16,16,4096]{3,2,0,1:T(8,128)(2,1)}) %all-gather.3.cloned.1.call-update) | async-done | bytes 8388624 | tf_op jit(solution)/shard_map/all_gather | solution.py:61
  138.5 14.8 %fusion.8 = f32[16,192,4,16]{1,3,2,0:T(8,128)S(1)} fusion(bf16[4,16,16,4096]{3,2,0,1:T(8,128)(2,1)} %all-gather.3.cloned.1.call-done, bf16[16,192,4096]{2,1,0:T(8,128)(2,1)} %param.11), kind=kOutput, calls=%fused_computation.10 | convolution fusion | flops 1610612736 | bytes 34340864 | tf_op jit(solution)/shard_map/slcd,lfd->lfsc/dot_general | solution.py:27
  153.3 15.0 %fusion.17 = bf16[16,192,4,16]{1,3,2,0:T(8,128)(2,1)S(1)} fusion(bf16[4,16,16,4096]{3,2,0,1:T(8,128)(2,1)} %all-gather.3.cloned.1.call-done, bf16[16,192,4096]{2,1,0:T(8,128)(2,1)} %param.12, f32[16,192,4,16]{1,3,2,0:T(8,128)S(1)} %fusion.8), kind=kOutput, calls=%fused_computation.13 | convolution fusion | flops 1611792384 | bytes 34734080 | tf_op jit(solution)/shard_map/slcd,lfd->lfsc/dot_general | solution.py:30
  168.3 1.5 copy.19
  169.8 28.7 %all-gather.5.cloned.1.call-done = bf16[16,768,64]{2,0,1:T(8,128)(2,1)} async-done(((bf16[16,192,64]{2,0,1:T(8,128)(2,1)}), bf16[16,768,64]{2,0,1:T(8,128)(2,1)}) %all-gather.5.cloned.1.call-update) | async-done | bytes 1572880 | tf_op jit(solution)/shard_map/all_gather | solution.py:33
  198.5 5.0 %copy.20 = bf16[16,768,64]{1,2,0:T(8,128)(2,1)} copy(bf16[16,768,64]{2,0,1:T(8,128)(2,1)} %all-gather.5.cloned.1.call-done) | data formatting | bytes 3145728 | tf_op jit(solution)/shard_map/all_gather | solution.py:33
  203.5 12.8 %convert_bitcast_fusion = bf16[4,16,16,1024]{3,2,0,1:T(8,128)(2,1)S(1)} fusion(bf16[16,768,4,16]{1,3,2,0:T(8,128)(2,1)} %bitcast.73, bf16[16,1024,768]{2,1,0:T(8,128)(2,1)} %param.13), kind=kOutput, calls=%fused_computation.9 | convolution fusion | flops 1611661312 | bytes 28835840 | tf_op jit(solution)/shard_map/lfsc,ldf->slcd/dot_general | solution.py:35
  216.3 1.5 copy.21
  217.9 4.6 %all-to-all-start.1 = ((bf16[4,16,16,1024]{3,2,1,0:T(8,128)(2,1)}), bf16[4,16,16,1024]{3,2,1,0:T(8,128)(2,1)S(1)}, u32[]{:S(2)}, u32[]{:S(2)}) async-start(bf16[4,16,16,1024]{3,2,1,0:T(8,128)(2,1)} %copy.21), calls=%async_computation.1 | async-start | bytes 4194304 | tf_op jit(solution)/shard_map/all_to_all | solution.py:38
  222.6 48.5 %all-to-all-done.1 = bf16[4,16,16,1024]{3,2,1,0:T(8,128)(2,1)S(1)} async-done(((bf16[4,16,16,1024]{3,2,1,0:T(8,128)(2,1)}), bf16[4,16,16,1024]{3,2,1,0:T(8,128)(2,1)S(1)}, u32[]{:S(2)}, u32[]{:S(2)}) %all-to-all-start.1) | async-done | bytes 2097184 | tf_op jit(solution)/shard_map/all_to_all | solution.py:38
  271.1 2.0 gather_fusion.1
  273.1 0.4 fusion.20
  273.5 0.7 copy.30
  (22 shorter events, 1.2 us)
Async XLA Ops:
  6.5 132.0 %all-gather.3.cloned.1.call-start = ((), (), s32[]{:S(2)}) async-start(), calls=%async_computation.2 | async-start | bytes 10485760 | tf_op jit(solution)/shard_map/all_gather | solution.py:61
  80.9 117.5 %all-gather.5.cloned.1.call-start = ((), (), s32[]{:S(2)}) async-start(), calls=%async_computation.3 | async-start | bytes 3932160 | tf_op jit(solution)/shard_map/all_gather | solution.py:33
  216.3 6.2 %copy-start = (f32[64,8]{0,1:T(8,128)S(1)}, f32[64,8]{0,1:T(8,128)}, u32[]{:S(2)}) copy-start(f32[64,8]{0,1:T(8,128)} %param.10) | copy-start | bytes 6148
  217.9 53.2 %all-to-all-start.1 = ((bf16[4,16,16,1024]{3,2,1,0:T(8,128)(2,1)}), bf16[4,16,16,1024]{3,2,1,0:T(8,128)(2,1)S(1)}, u32[]{:S(2)}, u32[]{:S(2)}) async-start(bf16[4,16,16,1024]{3,2,1,0:T(8,128)(2,1)} %copy.21), calls=%async_computation.1 | async-start | bytes 4194304 | tf_op jit(solution)/shard_map/all_to_all | solution.py:38
Sparse Core Ops, SparseCore 0:
  81.1 57.3 all-gather.2
  169.9 28.4 all-gather.4
where the time goes:
time: 282 us; the launch traced here: 281 us
  waiting for transfers between devices  134 us (48%)
  blocking collectives  60 us (21%)
  matrix products  43.1 us (15%)
  local copies, waits for them, and re-layouts  21 us (7%)
  between operations  13.5 us (5%)
  starting transfers between devices  4.82 us (2%)
  other arithmetic  4.13 us (1%)
    all_gather x1, waiting for transfers between devices, body(): lax.all_gather(lax.all_to_all(dispatched, 'expert', split_axis=0, concat_...  57.3 us
    all_to_all x1, blocking collectives, body(): lax.all_to_all(dispatched, 'expert', split_axis=0, concat_axis=0, tiled=T...  51.7 us
    all_to_all x1, waiting for transfers between devices, expert_block(): lax.all_to_all(result, 'expert', split_axis=0, concat_axis=0, tiled=True)  48.5 us
    all_gather x1, waiting for transfers between devices, expert_block(): hidden_all = lax.all_gather(hidden, 'tensor', axis=1, tiled=True)  28.7 us
    dot_general x1, matrix products, expert_block(): jnp.einsum('slcd,lfd->lfsc', slot_rows, up_proj, preferred_element_type=j...  15 us
    dot_general x1, matrix products, expert_block(): jnp.einsum('slcd,lfd->lfsc', slot_rows, gate_proj, preferred_element_type...  14.8 us
    dot_general x1, matrix products, expert_block(): jnp.einsum('lfsc,ldf->slcd', hidden_all, down_proj, preferred_element_typ...  12.8 us
    psum x1, blocking collectives, body(): squares = lax.psum(jnp.sum(values * values, axis=1), 'tensor')  8.37 us
  transfers between devices with their start and end apart: 3, of which 3 were waited for; matrix products, arithmetic and copies ran while one was open for 0% of the time, Pallas kernels for 0%

commit v1 on v0

v1 whole, which is shorter than its diff:
```python
import functools

import jax
import jax.numpy as jnp
from jax import lax
from jax.experimental import pallas as pl
from jax.experimental.pallas import tpu as pltpu
from jax.sharding import PartitionSpec as P

CAP = 16
EPSILON = 1e-06
VMEM_BYTES = 40 << 20
ROWS_CONTRACTED = (((1,), (1,)), ((), ()))


def dot_rows(a, b, precision=None):
    return lax.dot_general(
        a, b, ROWS_CONTRACTED, preferred_element_type=jnp.float32, precision=precision
    )


def split3(v):
    hi = v.astype(jnp.bfloat16)
    rest = v - hi.astype(jnp.float32)
    mid = rest.astype(jnp.bfloat16)
    low = (rest - mid.astype(jnp.float32)).astype(jnp.bfloat16)
    return hi, mid, low


def pack_kernel(where, x_ref, gain_ref, ids_ref, weights_ref, out_ref):
    rows, width = x_ref.shape
    values = x_ref[...].astype(jnp.float32)
    gain = gain_ref[:, pl.ds(pl.multiple_of(where[0] * width, 128), width)]
    out_ref[:rows, :] = (values * gain).astype(jnp.bfloat16)
    squares = values * values
    folded = squares[:, :128]
    for at in range(128, width, 128):
        folded = folded + squares[:, at : at + 128]
    sums = dot_rows(jnp.ones((8, 128), jnp.float32), folded, lax.Precision.HIGHEST)
    out_ref[rows:, :] = jnp.zeros((8, width), jnp.bfloat16)
    fields = [ids_ref[...].astype(jnp.float32).astype(jnp.bfloat16)]
    fields += list(split3(weights_ref[...])) + list(split3(sums))
    for n, field in enumerate(fields):
        out_ref[rows:, 128 * n : 128 * n + rows] = field


def join_kernel(*refs):
    *pieces, out_ref = refs
    rows = pieces[0].shape[0] - 8
    count = len(pieces) * rows
    for n, piece in enumerate(pieces):
        out_ref[n * rows : (n + 1) * rows, :] = piece[:rows, :]
    out_ref[count:, :] = jnp.zeros((8, out_ref.shape[1]), jnp.bfloat16)
    for n, piece in enumerate(pieces):
        for part in range(3):
            at = part * count + n * rows
            out_ref[count:, at : at + rows] = piece[rows:, 128 * (4 + part) : 128 * (4 + part) + rows]


def route_kernel(where, *refs):
    *pieces, code_ref, weight_ref, ids_all, weights_all = refs
    experts = code_ref.shape[0]
    rows = ids_all.shape[1] // len(pieces)
    for n, piece in enumerate(pieces):
        span = slice(n * rows, (n + 1) * rows)
        ids_all[:, span] = piece[:, :rows].astype(jnp.float32)
        weights_all[:, span] = (
            piece[:, 128 : 128 + rows].astype(jnp.float32)
            + piece[:, 256 : 256 + rows].astype(jnp.float32)
            + piece[:, 384 : 384 + rows].astype(jnp.float32)
        )
    tokens = ids_all.shape[1]
    expert_row = lax.broadcasted_iota(jnp.int32, (experts, tokens), 0)
    mine = (expert_row + where[0] * experts).astype(jnp.float32)
    member = jnp.zeros((experts, tokens), jnp.float32)
    weight = jnp.zeros((experts, tokens), jnp.float32)
    for k in range(ids_all.shape[0]):
        same = ids_all[k : k + 1, :] == mine
        member = member + jnp.where(same, 1.0, 0.0)
        weight = weight + jnp.where(same, weights_all[k : k + 1, :], 0.0)
    earlier = lax.broadcasted_iota(jnp.int32, (tokens, tokens), 1) < lax.broadcasted_iota(
        jnp.int32, (tokens, tokens), 0
    )
    rank = dot_rows(
        member.astype(jnp.bfloat16), jnp.where(earlier, 1.0, 0.0).astype(jnp.bfloat16)
    )
    half = len(pieces) * CAP
    offset = ((expert_row & 1) * half).astype(jnp.float32)
    code = jnp.where(member > 0.5, rank + offset, -1.0)
    for e in range(experts):
        code_ref[e] = code[e : e + 1, :]
        weight_ref[e] = weight[e : e + 1, :]


def one_hot(code_row, slots):
    place = lax.broadcasted_iota(jnp.int32, (slots, code_row.shape[1]), 0).astype(jnp.float32)
    return jnp.where(code_row == place, 1.0, 0.0)


def first_half_kernel(where, xa_ref, xb_ref, ga_ref, gb_ref, ua_ref, ub_ref, gate_ref, up_ref):
    pair, units, width = ga_ref.shape
    tokens = gate_ref.shape[2]
    xa, xb = xa_ref[:tokens, :], xb_ref[:tokens, :]
    for a_ref, b_ref, out_ref in ((ga_ref, gb_ref, gate_ref), (ua_ref, ub_ref, up_ref)):
        acc = dot_rows(a_ref[...].reshape(pair * units, width), xa)
        acc = acc + dot_rows(b_ref[...].reshape(pair * units, width), xb)
        out_ref[...] = acc.reshape(pair, units, tokens)


def second_half_kernel(
    where, xa_ref, xb_ref, xc_ref, xd_ref, gc_ref, gd_ref, uc_ref, ud_ref,
    gate_ref, up_ref, code_ref, weight_ref, out_ref, *, features,
):
    pair, units, width = gc_ref.shape
    tokens = gate_ref.shape[2]
    slots = out_ref.shape[2]
    total = jnp.zeros((1, tokens), jnp.float32)
    for x_ref in (xa_ref, xb_ref, xc_ref, xd_ref):
        row = x_ref[tokens:, :].astype(jnp.float32)[:1]
        for part in range(3):
            total = total + row[:, part * tokens : (part + 1) * tokens]
    inv = lax.rsqrt(total / features + EPSILON)
    xc, xd = xc_ref[:tokens, :], xd_ref[:tokens, :]
    acts = []
    for acc_ref, c_ref, d_ref in ((gate_ref, gc_ref, gd_ref), (up_ref, uc_ref, ud_ref)):
        acc = acc_ref[...].reshape(pair * units, tokens)
        acc = acc + dot_rows(c_ref[...].reshape(pair * units, width), xc)
        acc = acc + dot_rows(d_ref[...].reshape(pair * units, width), xd)
        acts.append(acc * inv)
    gate, up = acts
    hidden = gate / (1.0 + jnp.exp(-gate)) * up
    packed = jnp.zeros((units, slots), jnp.float32)
    for n in range(pair):
        mine = hidden[n * units : (n + 1) * units] * weight_ref[n]
        packed = packed + dot_rows(
            mine.astype(jnp.bfloat16), one_hot(code_ref[n], slots).astype(jnp.bfloat16)
        )
    out_ref[0] = packed.astype(jnp.bfloat16)


def down_kernel(where, *refs, shards, last):
    pieces, (code_ref, d_ref), rest = refs[:shards], refs[shards : shards + 2], refs[shards + 2 :]
    if last:
        before_ref, own_ref, *send_refs, joined, acc = rest
    else:
        own_ref, joined, acc = rest
    step = pl.program_id(0)
    units, slots = joined.shape[1:]
    pair = d_ref.shape[0]
    tokens = acc.shape[0]

    @pl.when(step == 0)
    def _():
        acc[...] = before_ref[...] if last else jnp.zeros_like(acc)

    for n, piece in enumerate(pieces):
        joined[where[n]] = piece[0]
    packed = joined[...].reshape(shards * units, slots)
    for n in range(pair):
        spread = one_hot(code_ref[n], slots).T.astype(jnp.bfloat16)
        hidden = dot_rows(spread, packed).astype(jnp.bfloat16)
        acc[...] += dot_rows(hidden, d_ref[n])

    @pl.when(step == pl.num_programs(0) - 1)
    def _():
        if last:
            rows = own_ref.shape[0]
            own_ref[...] = acc[:rows, :]
            for n, ref in enumerate(send_refs):
                ref[...] = acc[(n + 1) * rows : (n + 2) * rows, :].astype(jnp.bfloat16)
        else:
            own_ref[...] = acc[...]


def finish_kernel(own_ref, *refs):
    *pieces, out_ref = refs
    total = own_ref[...]
    for piece in pieces:
        total = total + piece[...].astype(jnp.float32)
    out_ref[...] = total.astype(jnp.bfloat16)


def params(limit=VMEM_BYTES):
    return pltpu.CompilerParams(vmem_limit_bytes=limit)


def whole(shape):
    return pl.BlockSpec(shape, lambda *_: (0,) * len(shape))


def dense_body(tokens, norm_gain, expert_ids, gate_weights, gate_proj, up_proj, down_proj):
    blocks = lax.axis_size("expert")
    shards = lax.axis_size("tensor")
    rows, width = tokens.shape
    experts, units, features = gate_proj.shape
    out_width, hidden_units = down_proj.shape[1:]
    count = blocks * rows
    slots = 2 * blocks * CAP
    me = lax.axis_index("tensor")
    expert_at = lax.axis_index("expert").astype(jnp.int32)[None]
    order = jnp.stack([(me ^ n).astype(jnp.int32) for n in range(shards)])
    top = expert_ids.shape[1]

    packed = pl.pallas_call(
        pack_kernel,
        grid_spec=pltpu.PrefetchScalarGridSpec(
            num_scalar_prefetch=1,
            grid=(1,),
            in_specs=[
                whole((rows, width)), whole((1, features)), whole((top, rows)), whole((top, rows)),
            ],
            out_specs=whole((rows + 8, width)),
        ),
        out_shape=jax.ShapeDtypeStruct((rows + 8, width), jnp.bfloat16),
        compiler_params=params(),
        name="pack",
    )(order, tokens, norm_gain[None, :], expert_ids.T, gate_weights.T)

    pieces = [packed] + [
        lax.ppermute(packed, "expert", [(i, (i + n) % blocks) for i in range(blocks)])
        for n in range(1, blocks)
    ]
    xa = pl.pallas_call(
        join_kernel,
        out_shape=jax.ShapeDtypeStruct((count + 8, width), jnp.bfloat16),
        compiler_params=params(),
        name="join",
    )(*pieces)

    def swap(v, n):
        return lax.ppermute(v, "tensor", [(i, i ^ n) for i in range(shards)])

    xc = swap(xa, 2)
    xb = swap(xa, 1)
    code, weight = pl.pallas_call(
        route_kernel,
        grid_spec=pltpu.PrefetchScalarGridSpec(
            num_scalar_prefetch=1,
            grid=(1,),
            in_specs=[pl.BlockSpec((8, width), lambda i, w: (rows // 8, 0))] * blocks,
            out_specs=[whole((experts, 1, count))] * 2,
            scratch_shapes=[pltpu.VMEM((top, count), jnp.float32)] * 2,
        ),
        out_shape=[jax.ShapeDtypeStruct((experts, 1, count), jnp.float32)] * 2,
        compiler_params=params(),
        name="route",
    )(expert_at, *pieces)

    def columns(n, first=0):
        return pl.BlockSpec((2, units, width), lambda i, w: (i + first, 0, w[n]))

    x_spec = whole((count + 8, width))
    act_shape = jax.ShapeDtypeStruct((experts, units, count), jnp.float32)
    gate_acc, up_acc = pl.pallas_call(
        first_half_kernel,
        grid_spec=pltpu.PrefetchScalarGridSpec(
            num_scalar_prefetch=1,
            grid=(experts // 2,),
            in_specs=[x_spec, x_spec] + [columns(0), columns(1)] * 2,
            out_specs=[pl.BlockSpec((2, units, count), lambda i, w: (i, 0, 0))] * 2,
        ),
        out_shape=[act_shape] * 2,
        compiler_params=params(),
        cost_estimate=pl.CostEstimate(
            flops=2 * experts * units * count * features,
            bytes_accessed=2 * experts * units * features,
            transcendentals=0,
        ),
        name="first",
    )(order, xa, xb, gate_proj, gate_proj, up_proj, up_proj)
    xd = swap(xc, 1)

    parts = 2
    pairs = experts // 2 // parts

    def second(part):
        first = part * pairs
        return pl.pallas_call(
            functools.partial(second_half_kernel, features=features),
            grid_spec=pltpu.PrefetchScalarGridSpec(
                num_scalar_prefetch=1,
                grid=(pairs,),
                in_specs=[x_spec] * 4
                + [columns(2, first), columns(3, first)] * 2
                + [pl.BlockSpec((2, units, count), lambda i, w: (i + first, 0, 0))] * 2
                + [pl.BlockSpec((2, 1, count), lambda i, w: (i + first, 0, 0))] * 2,
                out_specs=pl.BlockSpec((1, units, slots), lambda i, w: (i, 0, 0)),
            ),
            out_shape=jax.ShapeDtypeStruct((pairs, units, slots), jnp.bfloat16),
            compiler_params=params(),
            cost_estimate=pl.CostEstimate(
                flops=2 * experts * units * count * features // parts,
                bytes_accessed=2 * experts * units * features // parts,
                transcendentals=0,
            ),
            name=f"second{part}",
        )(order, xa, xb, xc, xd, gate_proj, gate_proj, up_proj, up_proj, gate_acc, up_acc, code, weight)

    def down(part, pieces, before):
        first = part * pairs
        last = part == parts - 1
        total = jax.ShapeDtypeStruct((count, out_width), jnp.float32)
        if last:
            out_shape = [jax.ShapeDtypeStruct((rows, out_width), jnp.float32)]
            out_shape += [jax.ShapeDtypeStruct((rows, out_width), jnp.bfloat16)] * (blocks - 1)
        else:
            out_shape = [total]
        return pl.pallas_call(
            functools.partial(down_kernel, shards=shards, last=last),
            grid_spec=pltpu.PrefetchScalarGridSpec(
                num_scalar_prefetch=1,
                grid=(pairs,),
                in_specs=[pl.BlockSpec((1, units, slots), lambda i, w: (i, 0, 0))] * shards
                + [
                    pl.BlockSpec((2, 1, count), lambda i, w: (i + first, 0, 0)),
                    pl.BlockSpec((2, out_width, hidden_units), lambda i, w: (i + first, 0, 0)),
                ]
                + [whole(total.shape)] * last,
                out_specs=[whole(s.shape) for s in out_shape],
                scratch_shapes=[
                    pltpu.VMEM((shards, units, slots), jnp.bfloat16),
                    pltpu.VMEM(total.shape, jnp.float32),
                ],
            ),
            out_shape=out_shape,
            compiler_params=params(),
            cost_estimate=pl.CostEstimate(
                flops=2 * experts * count * out_width * hidden_units // parts,
                bytes_accessed=2 * experts * out_width * hidden_units // parts,
                transcendentals=0,
            ),
            name=f"down{part}",
        )(order, *pieces, code, down_proj, *([before] if last else []))

    before = None
    for part in range(parts):
        mine = second(part)
        across = swap(mine, 2)
        pieces = [mine, swap(mine, 1), across, swap(across, 1)]
        before = down(part, pieces, before)
        if part < parts - 1:
            before = before[0]
    own, *sends = before
    back = [
        lax.ppermute(v, "expert", [(i, (i - n) % blocks) for i in range(blocks)])
        for n, v in enumerate(sends, 1)
    ]
    return pl.pallas_call(
        finish_kernel,
        out_shape=jax.ShapeDtypeStruct((rows, out_width), jnp.bfloat16),
        compiler_params=params(),
        name="finish",
    )(own, *back)


def slot_places(expert_ids, total):
    flat_ids = expert_ids.reshape(-1)
    onehot = (flat_ids[:, None] == jnp.arange(total, dtype=jnp.int32)[None, :]).astype(jnp.int32)
    before = jnp.cumsum(onehot, axis=0) - onehot
    inside = jnp.sum(onehot * before, axis=1)
    return flat_ids * CAP + inside


def expert_block(slot_rows, gate_proj, up_proj, down_proj):
    sources, local_experts, item_count = slot_rows.shape[:3]
    gate_act = jnp.einsum(
        "slcd,lfd->lfsc", slot_rows, gate_proj, preferred_element_type=jnp.float32
    )
    up_act = jnp.einsum("slcd,lfd->lfsc", slot_rows, up_proj, preferred_element_type=jnp.float32)
    hidden = (jax.nn.silu(gate_act) * up_act).astype(jnp.bfloat16)
    hidden = hidden.reshape(local_experts, hidden.shape[1], sources * item_count)
    hidden_all = lax.all_gather(hidden, "tensor", axis=1, tiled=True)
    hidden_all = hidden_all.reshape(local_experts, hidden_all.shape[1], sources, item_count)
    result = jnp.einsum(
        "lfsc,ldf->slcd", hidden_all, down_proj, preferred_element_type=jnp.float32
    ).astype(jnp.bfloat16)
    return lax.all_to_all(result, "expert", split_axis=0, concat_axis=0, tiled=True)


def slot_body(tokens, norm_gain, expert_ids, gate_weights, gate_proj, up_proj, down_proj):
    local_experts = gate_proj.shape[0]
    groups = lax.axis_size("expert")
    total = local_experts * groups
    features = gate_proj.shape[2]
    top = expert_ids.shape[1]
    tok_rows = tokens.shape[0]
    places = slot_places(expert_ids, total)
    owners = (
        jnp.full((total * CAP,), tok_rows, jnp.int32)
        .at[places]
        .set(jnp.arange(places.shape[0], dtype=jnp.int32) // top)
    )
    values = tokens.astype(jnp.float32)
    squares = lax.psum(jnp.sum(values * values, axis=1), "tensor")
    inv_scale = lax.rsqrt(squares / features + EPSILON)[:, None]
    width = tokens.shape[1]
    gain_part = lax.dynamic_slice_in_dim(norm_gain, lax.axis_index("tensor") * width, width)
    normed = (values * inv_scale * gain_part).astype(jnp.bfloat16)
    padded = jnp.concatenate([normed, jnp.zeros((1, width), jnp.bfloat16)], axis=0)
    dispatched = padded[owners].reshape(groups, local_experts, CAP, width)
    full_rows = lax.all_gather(
        lax.all_to_all(dispatched, "expert", split_axis=0, concat_axis=0, tiled=True),
        "tensor",
        axis=3,
        tiled=True,
    )
    returned = expert_block(full_rows, gate_proj, up_proj, down_proj)
    out_width = returned.shape[-1]
    flat_back = returned.reshape(total * CAP, out_width)
    picked = flat_back[places].reshape(tok_rows, top, out_width).astype(jnp.float32)
    return jnp.einsum("tkd,tk->td", picked, gate_weights).astype(jnp.bfloat16)


def body(tokens, norm_gain, expert_ids, gate_weights, gate_proj, up_proj, down_proj):
    blocks, shards = lax.axis_size("expert"), lax.axis_size("tensor")
    rows, width = tokens.shape
    experts = gate_proj.shape[0]
    fits = (
        shards == 4
        and experts % 4 == 0
        and experts * blocks <= 256
        and blocks * rows <= 256
        and blocks * CAP * 2 <= 256
        and rows <= 128
        and expert_ids.shape[1] == 8
        and width % 1024 == 0
    )
    run = dense_body if fits else slot_body
    return run(tokens, norm_gain, expert_ids, gate_weights, gate_proj, up_proj, down_proj)


def solution(mesh):
    return jax.shard_map(
        body,
        mesh=mesh,
        in_specs=(
            P(("group", "expert"), "tensor"),
            P(),
            P(("group", "expert"), None),
            P(("group", "expert"), None),
            P("expert", "tensor", None),
            P("expert", "tensor", None),
            P("expert", "tensor", None),
        ),
        out_specs=P(("group", "expert"), "tensor"),
        check_vma=False,
    )
```

time: 282 us -> 107 us (0.38)
  waiting for transfers between devices: 134 us -> 39.9 us
  blocking collectives: 60 us -> 0 us
  Pallas kernels: 0 us -> 48.7 us
  matrix products: 43.1 us -> 0 us
  local copies, waits for them, and re-layouts: 21 us -> 2.99 us
  between operations: 13.5 us -> 0.09 us
  starting transfers between devices: 4.82 us -> 15 us
  other arithmetic: 4.13 us -> 0.08 us
    all_gather x2 -> x0, waiting for transfers between devices: 86 us -> none  [the longest x1 57.3 us: body(): lax.all_gather(lax.all_to_all(dispatched, 'expert', split_axis=0, concat_...]
    all_to_all x1 -> x0, blocking collectives: 51.7 us -> none  [body(): lax.all_to_all(dispatched, 'expert', split_axis=0, concat_axis=0, tiled=T...]
    pallas_call x0 -> x9, Pallas kernels: none -> 48.7 us  [the longest x2 16.9 us: down(): pl.pallas_call(functools.partial(down_kernel, shards=shards, last=last),...]
    all_to_all x1 -> x0, waiting for transfers between devices: 48.5 us -> none  [expert_block(): lax.all_to_all(result, 'expert', split_axis=0, concat_axis=0, tiled=True)]
    dot_general x4 -> x0, matrix products: 43.1 us -> none  [the longest x1 15 us: expert_block(): jnp.einsum('slcd,lfd->lfsc', slot_rows, up_proj, preferred_element_type=j...]
    ppermute x0 -> x15, waiting for transfers between devices: none -> 39.9 us  [the longest x9 17.9 us: swap(): return lax.ppermute(v, 'tensor', [(i, i ^ n) for i in range(shards)])]
    ppermute x0 -> x15, starting transfers between devices: none -> 15 us  [the longest x3 6.11 us: dense_body(): lax.ppermute(packed, 'expert', [(i, (i + n) % blocks) for i in range(bloc...]
    psum x1 -> x0, blocking collectives: 8.37 us -> none  [body(): squares = lax.psum(jnp.sum(values * values, axis=1), 'tensor')]
  transfers between devices with their start and end apart: 3 -> 15, of which waited for: 3 -> 6; matrix products, arithmetic and copies ran while one was open for 0% -> 0% of each run, Pallas kernels for 0% -> 29%
where the time goes in v1:
time: 107 us
  Pallas kernels  48.7 us (46%)
  waiting for transfers between devices  39.9 us (37%)
  starting transfers between devices  15 us (14%)
  local copies, waits for them, and re-layouts  2.99 us (3%)
    ppermute x9, waiting for transfers between devices, swap(): return lax.ppermute(v, 'tensor', [(i, i ^ n) for i in range(shards)])  17.9 us
    pallas_call x2, Pallas kernels, down(): pl.pallas_call(functools.partial(down_kernel, shards=shards, last=last),...  16.9 us
    pallas_call x2, Pallas kernels, second(): pl.pallas_call(functools.partial(second_half_kernel, features=features),...  16.3 us
    pallas_call x1, Pallas kernels, dense_body(): pl.pallas_call(first_half_kernel, grid_spec=pltpu.PrefetchScalarGridSpec(...  13.6 us
    ppermute x3, waiting for transfers between devices, dense_body(): lax.ppermute(packed, 'expert', [(i, (i + n) % blocks) for i in range(bloc...  11.5 us
    ppermute x3, waiting for transfers between devices, dense_body(): lax.ppermute(v, 'expert', [(i, (i - n) % blocks) for i in range(blocks)])  10.6 us
    ppermute x3, starting transfers between devices, dense_body(): lax.ppermute(packed, 'expert', [(i, (i + n) % blocks) for i in range(bloc...  6.11 us
    ppermute x3, starting transfers between devices, dense_body(): lax.ppermute(v, 'expert', [(i, (i - n) % blocks) for i in range(blocks)])  4.72 us
  transfers between devices with their start and end apart: 15, of which 6 were waited for; matrix products, arithmetic and copies ran while one was open for 0% of the time, Pallas kernels for 29%

profile of v1, /device:TPU:0, one launch (start us, length us, event | category | flops | bytes accessed | tf_op | source)
XLA Modules:
  0.0 106.8 jit_solution(7912317648000976704)
XLA Ops:
  0.1 0.9 copy-done
  1.0 0.7 copy-done.1
  1.7 0.7 copy-done.2
  2.4 0.7 copy-done.3
  3.1 0.7 pack.1.refs_0_
  3.8 5.1 %collective-permute-start.2 = (bf16[72,1024]{1,0:T(8,128)(2,1)S(1)}, bf16[72,1024]{1,0:T(8,128)(2,1)S(1)}, u32[]{:S(2)}, u32[]{:S(2)}) collective-permute-start(bf16[72,1024]{1,0:T(8,128)(2,1)S(1)} %pack.1.refs_0_), channel_id=1, source_target_pairs={{0,12},{4,0},{8,4},{12,8},{1,13},{5,1},{9,5},{13,9},{2,14},{6,2},{... | collective-permute-start | bytes 442376 | tf_op jit(solution)/shard_map/ppermute | solution.py:220
  8.9 1.0 collective-permute-start
  9.9 3.3 %collective-permute-done.2.refs_3_ = bf16[72,1024]{1,0:T(8,128)(2,1)S(1)} collective-permute-done((bf16[72,1024]{1,0:T(8,128)(2,1)S(1)}, bf16[72,1024]{1,0:T(8,128)(2,1)S(1)}, u32[]{:S(2)}, u32[]{:S(2)}) %collective-permute-start.2) | collective-permute-done | bytes 147488 | tf_op jit(solution)/shard_map/ppermute | solution.py:220
  13.2 8.2 %collective-permute-done.1.refs_2_ = bf16[72,1024]{1,0:T(8,128)(2,1)S(1)} collective-permute-done((bf16[72,1024]{1,0:T(8,128)(2,1)S(1)}, bf16[72,1024]{1,0:T(8,128)(2,1)S(1)}, u32[]{:S(2)}, u32[]{:S(2)}) %collective-permute-start.1) | collective-permute-done | bytes 147488 | tf_op jit(solution)/shard_map/ppermute | solution.py:220
  21.5 1.5 %collective-permute-start.4 = (bf16[264,1024]{1,0:T(8,128)(2,1)S(1)}, bf16[264,1024]{1,0:T(8,128)(2,1)S(1)}, u32[]{:S(2)}, u32[]{:S(2)}) collective-permute-start(bf16[264,1024]{1,0:T(8,128)(2,1)S(1)} %join.1.xa_ref), channel_id=1, source_target_pairs={{0,2},{1,3},{2,0},{3,1},{4,6},{5,7},{6,4},{7,5},{8,10},{9,11},{10,... | collective-permute-start | bytes 1622024 | tf_op jit(solution)/shard_map/ppermute | solution.py:231
  23.2 11.9 %collective-permute-done.4.xc_ref = bf16[264,1024]{1,0:T(8,128)(2,1)S(1)} collective-permute-done((bf16[264,1024]{1,0:T(8,128)(2,1)S(1)}, bf16[264,1024]{1,0:T(8,128)(2,1)S(1)}, u32[]{:S(2)}, u32[]{:S(2)}) %collective-permute-start.4) | collective-permute-done | bytes 540704 | tf_op jit(solution)/shard_map/ppermute | solution.py:231
  35.1 13.6 %first.1 = (f32[16,192,256]{2,1,0:T(8,128)S(1)}, f32[16,192,256]{2,1,0:T(8,128)S(1)}) custom-call(s32[4]{0:T(128)S(1)} %pad_add_fusion.where, bf16[264,1024]{1,0:T(8,128)(2,1)S(1)} %join.1.xa_ref, bf16[264,1024]{1,0:T(8,128)(2,1)S(1)} %collective-permute-done.3.xb_ref, bf16[16,192,4096]{2,1,0:T(8,128)(2,1)} %gd_ref.3, bf16[16,192,4096]{2,1,0:T(8,128)(2,1)} %gd_ref.3, ...), custom_call_target="tpu_custom_call" | custom-call | flops 6442450944 | bytes 25165824 | tf_op jit(solution)/shard_map/first/pallas_call | solution.py:254
  48.8 8.2 %second0.1.refs_0_ = bf16[4,192,128]{2,1,0:T(8,128)(2,1)S(1)} custom-call(s32[4]{0:T(128)S(1)} %pad_add_fusion.where, bf16[264,1024]{1,0:T(8,128)(2,1)S(1)} %join.1.xa_ref, bf16[264,1024]{1,0:T(8,128)(2,1)S(1)} %collective-permute-done.3.xb_ref, bf16[264,1024]{1,0:T(8,128)(2,1)S(1)} %collective-permute-done.4.xc_ref, ...), custom_call_target="tpu_custom_call" | custom-call | flops 3221225472 | bytes 12582912 | tf_op jit(solution)/shard_map/second0/pallas_call | solution.py:278
  57.0 1.5 %collective-permute-start.10 = (bf16[4,192,128]{2,1,0:T(8,128)(2,1)S(1)}, bf16[4,192,128]{2,1,0:T(8,128)(2,1)S(1)}, u32[]{:S(2)}, u32[]{:S(2)}) collective-permute-start(bf16[4,192,128]{2,1,0:T(8,128)(2,1)S(1)} %second0.1.refs_0_), channel_id=1, source_target_pairs={{0,2},{1,3},{2,0},{3,1},{4,6},{5,7},{6,4},{7,5},{8,10},{9,11},{10,... | collective-permute-start | bytes 589832 | tf_op jit(solution)/shard_map/ppermute | solution.py:231
  58.5 8.2 %second1.1.refs_0_ = bf16[4,192,128]{2,1,0:T(8,128)(2,1)S(1)} custom-call(s32[4]{0:T(128)S(1)} %pad_add_fusion.where, bf16[264,1024]{1,0:T(8,128)(2,1)S(1)} %join.1.xa_ref, bf16[264,1024]{1,0:T(8,128)(2,1)S(1)} %collective-permute-done.3.xb_ref, bf16[264,1024]{1,0:T(8,128)(2,1)S(1)} %collective-permute-done.4.xc_ref, ...), custom_call_target="tpu_custom_call" | custom-call | flops 3221225472 | bytes 12582912 | tf_op jit(solution)/shard_map/second1/pallas_call | solution.py:278
  66.6 0.6 collective-permute-start.7
  67.8 6.0 %collective-permute-done.7.refs_2_ = bf16[4,192,128]{2,1,0:T(8,128)(2,1)S(1)} collective-permute-done((bf16[4,192,128]{2,1,0:T(8,128)(2,1)S(1)}, bf16[4,192,128]{2,1,0:T(8,128)(2,1)S(1)}, u32[]{:S(2)}, u32[]{:S(2)}) %collective-permute-start.7) | collective-permute-done | bytes 196640 | tf_op jit(solution)/shard_map/ppermute | solution.py:231
  73.8 8.5 %down0.1.refs_6_ = f32[256,1024]{1,0:T(8,128)S(1)} custom-call(s32[4]{0:T(128)S(1)} %pad_add_fusion.where, bf16[4,192,128]{2,1,0:T(8,128)(2,1)S(1)} %second0.1.refs_0_, bf16[4,192,128]{2,1,0:T(8,128)(2,1)S(1)} %collective-permute-done.9.refs_1_, bf16[4,192,128]{2,1,0:T(8,128)(2,1)S(1)} %collective-permute-done.10.refs_2_, ...), custom_call_target="tpu_custom_call" | custom-call | flops 3221225472 | bytes 12582912 | tf_op jit(solution)/shard_map/down0/pallas_call | solution.py:308
  82.3 8.5 %down1.1 = (f32[64,1024]{1,0:T(8,128)S(1)}, bf16[64,1024]{1,0:T(8,128)(2,1)S(1)}, bf16[64,1024]{1,0:T(8,128)(2,1)S(1)}, bf16[64,1024]{1,0:T(8,128)(2,1)S(1)}) custom-call(s32[4]{0:T(128)S(1)} %pad_add_fusion.where, bf16[4,192,128]{2,1,0:T(8,128)(2,1)S(1)} %second1.1.refs_0_, bf16[4,192,128]{2,1,0:T(8,128)(2,1)S(1)} %collective-permute-done.6.refs_1_, ...), custom_call_target="tpu_custom_call" | custom-call | flops 3221225472 | bytes 12582912 | tf_op jit(solution)/shard_map/down1/pallas_call | solution.py:308
  91.2 2.4 %collective-permute-start.13 = (bf16[64,1024]{1,0:T(8,128)(2,1)S(1)}, bf16[64,1024]{1,0:T(8,128)(2,1)S(1)}, u32[]{:S(2)}, u32[]{:S(2)}) collective-permute-start(bf16[64,1024]{1,0:T(8,128)(2,1)S(1)} %get-tuple-element.19), channel_id=1, source_target_pairs={{0,8},{4,12},{8,0},{12,4},{1,9},{5,13},{9,1},{13,5},{2,10},{6,14},... | collective-permute-start | bytes 393224 | tf_op jit(solution)/shard_map/ppermute | solution.py:345
  93.5 1.9 %collective-permute-start.14 = (bf16[64,1024]{1,0:T(8,128)(2,1)S(1)}, bf16[64,1024]{1,0:T(8,128)(2,1)S(1)}, u32[]{:S(2)}, u32[]{:S(2)}) collective-permute-start(bf16[64,1024]{1,0:T(8,128)(2,1)S(1)} %get-tuple-element.20), channel_id=1, source_target_pairs={{0,4},{4,8},{8,12},{12,0},{1,5},{5,9},{9,13},{13,1},{2,6},{6,10},{... | collective-permute-start | bytes 393224 | tf_op jit(solution)/shard_map/ppermute | solution.py:345
  95.5 1.2 %collective-permute-done.12.refs_0_ = bf16[64,1024]{1,0:T(8,128)(2,1)S(1)} collective-permute-done((bf16[64,1024]{1,0:T(8,128)(2,1)S(1)}, bf16[64,1024]{1,0:T(8,128)(2,1)S(1)}, u32[]{:S(2)}, u32[]{:S(2)}) %collective-permute-start.12) | collective-permute-done | bytes 131104 | tf_op jit(solution)/shard_map/ppermute | solution.py:345
  96.7 9.3 %collective-permute-done.13.refs_1_ = bf16[64,1024]{1,0:T(8,128)(2,1)S(1)} collective-permute-done((bf16[64,1024]{1,0:T(8,128)(2,1)S(1)}, bf16[64,1024]{1,0:T(8,128)(2,1)S(1)}, u32[]{:S(2)}, u32[]{:S(2)}) %collective-permute-start.13) | collective-permute-done | bytes 131104 | tf_op jit(solution)/shard_map/ppermute | solution.py:345
  106.1 0.7 finish.1
  (24 shorter events, 1.4 us)
Async XLA Ops:
  0.1 0.9 copy-start
  1.0 0.7 copy-start.1
  1.7 0.7 copy-start.2
  2.4 0.7 copy-start.3
  3.8 9.4 %collective-permute-start.2 = (bf16[72,1024]{1,0:T(8,128)(2,1)S(1)}, bf16[72,1024]{1,0:T(8,128)(2,1)S(1)}, u32[]{:S(2)}, u32[]{:S(2)}) collective-permute-start(bf16[72,1024]{1,0:T(8,128)(2,1)S(1)} %pack.1.refs_0_), channel_id=1, source_target_pairs={{0,12},{4,0},{8,4},{12,8},{1,13},{5,1},{9,5},{13,9},{2,14},{6,2},{... | collective-permute-start | bytes 442376 | tf_op jit(solution)/shard_map/ppermute | solution.py:220
  8.9 12.5 %collective-permute-start.1 = (bf16[72,1024]{1,0:T(8,128)(2,1)S(1)}, bf16[72,1024]{1,0:T(8,128)(2,1)S(1)}, u32[]{:S(2)}, u32[]{:S(2)}) collective-permute-start(bf16[72,1024]{1,0:T(8,128)(2,1)S(1)} %pack.1.refs_0_), channel_id=1, source_target_pairs={{0,8},{4,12},{8,0},{12,4},{1,9},{5,13},{9,1},{13,5},{2,10},{6,14},... | collective-permute-start | bytes 442376 | tf_op jit(solution)/shard_map/ppermute | solution.py:220
  8.9 12.5 %collective-permute-start = (bf16[72,1024]{1,0:T(8,128)(2,1)S(1)}, bf16[72,1024]{1,0:T(8,128)(2,1)S(1)}, u32[]{:S(2)}, u32[]{:S(2)}) collective-permute-start(bf16[72,1024]{1,0:T(8,128)(2,1)S(1)} %pack.1.refs_0_), channel_id=1, source_target_pairs={{0,4},{4,8},{8,12},{12,0},{1,5},{5,9},{9,13},{13,1},{2,6},{6,10},{... | collective-permute-start | bytes 442376 | tf_op jit(solution)/shard_map/ppermute | solution.py:220
  21.5 13.6 %collective-permute-start.4 = (bf16[264,1024]{1,0:T(8,128)(2,1)S(1)}, bf16[264,1024]{1,0:T(8,128)(2,1)S(1)}, u32[]{:S(2)}, u32[]{:S(2)}) collective-permute-start(bf16[264,1024]{1,0:T(8,128)(2,1)S(1)} %join.1.xa_ref), channel_id=1, source_target_pairs={{0,2},{1,3},{2,0},{3,1},{4,6},{5,7},{6,4},{7,5},{8,10},{9,11},{10,... | collective-permute-start | bytes 1622024 | tf_op jit(solution)/shard_map/ppermute | solution.py:231
  23.0 12.1 %collective-permute-start.3 = (bf16[264,1024]{1,0:T(8,128)(2,1)S(1)}, bf16[264,1024]{1,0:T(8,128)(2,1)S(1)}, u32[]{:S(2)}, u32[]{:S(2)}) collective-permute-start(bf16[264,1024]{1,0:T(8,128)(2,1)S(1)} %join.1.xa_ref), channel_id=1, source_target_pairs={{0,1},{1,0},{2,3},{3,2},{4,5},{5,4},{6,7},{7,6},{8,9},{9,8},{10,11... | collective-permute-start | bytes 1622024 | tf_op jit(solution)/shard_map/ppermute | solution.py:231
  35.1 13.7 %collective-permute-start.5 = (bf16[264,1024]{1,0:T(8,128)(2,1)S(1)}, bf16[264,1024]{1,0:T(8,128)(2,1)S(1)}, u32[]{:S(2)}, u32[]{:S(2)}) collective-permute-start(bf16[264,1024]{1,0:T(8,128)(2,1)S(1)} %collective-permute-done.4.xc_ref), channel_id=1, source_target_pairs={{0,1},{1,0},{2,3},{3,2},{4,5},{5,4},{6,7},{7,6},{8,9},{9,8},{10,11... | collective-permute-start | bytes 1622024 | tf_op jit(solution)/shard_map/ppermute | solution.py:231
  57.0 10.3 %collective-permute-start.10 = (bf16[4,192,128]{2,1,0:T(8,128)(2,1)S(1)}, bf16[4,192,128]{2,1,0:T(8,128)(2,1)S(1)}, u32[]{:S(2)}, u32[]{:S(2)}) collective-permute-start(bf16[4,192,128]{2,1,0:T(8,128)(2,1)S(1)} %second0.1.refs_0_), channel_id=1, source_target_pairs={{0,2},{1,3},{2,0},{3,1},{4,6},{5,7},{6,4},{7,5},{8,10},{9,11},{10,... | collective-permute-start | bytes 589832 | tf_op jit(solution)/shard_map/ppermute | solution.py:231
  66.6 7.1 %collective-permute-start.7 = (bf16[4,192,128]{2,1,0:T(8,128)(2,1)S(1)}, bf16[4,192,128]{2,1,0:T(8,128)(2,1)S(1)}, u32[]{:S(2)}, u32[]{:S(2)}) collective-permute-start(bf16[4,192,128]{2,1,0:T(8,128)(2,1)S(1)} %second1.1.refs_0_), channel_id=1, source_target_pairs={{0,2},{1,3},{2,0},{3,1},{4,6},{5,7},{6,4},{7,5},{8,10},{9,11},{10,... | collective-permute-start | bytes 589832 | tf_op jit(solution)/shard_map/ppermute | solution.py:231
  67.3 6.5 %collective-permute-start.9 = (bf16[4,192,128]{2,1,0:T(8,128)(2,1)S(1)}, bf16[4,192,128]{2,1,0:T(8,128)(2,1)S(1)}, u32[]{:S(2)}, u32[]{:S(2)}) collective-permute-start(bf16[4,192,128]{2,1,0:T(8,128)(2,1)S(1)} %second0.1.refs_0_), channel_id=1, source_target_pairs={{0,1},{1,0},{2,3},{3,2},{4,5},{5,4},{6,7},{7,6},{8,9},{9,8},{10,11... | collective-permute-start | bytes 589832 | tf_op jit(solution)/shard_map/ppermute | solution.py:231
  67.3 6.5 %collective-permute-start.11 = (bf16[4,192,128]{2,1,0:T(8,128)(2,1)S(1)}, bf16[4,192,128]{2,1,0:T(8,128)(2,1)S(1)}, u32[]{:S(2)}, u32[]{:S(2)}) collective-permute-start(bf16[4,192,128]{2,1,0:T(8,128)(2,1)S(1)} %collective-permute-done.10.refs_2_), channel_id=1, source_target_pairs={{0,1},{1,0},{2,3},{3,2},{4,5},{5,4},{6,7},{7,6},{8,9},{9,8},{10,11... | collective-permute-start | bytes 589832 | tf_op jit(solution)/shard_map/ppermute | solution.py:231
  67.8 14.5 %collective-permute-start.6 = (bf16[4,192,128]{2,1,0:T(8,128)(2,1)S(1)}, bf16[4,192,128]{2,1,0:T(8,128)(2,1)S(1)}, u32[]{:S(2)}, u32[]{:S(2)}) collective-permute-start(bf16[4,192,128]{2,1,0:T(8,128)(2,1)S(1)} %second1.1.refs_0_), channel_id=1, source_target_pairs={{0,1},{1,0},{2,3},{3,2},{4,5},{5,4},{6,7},{7,6},{8,9},{9,8},{10,11... | collective-permute-start | bytes 589832 | tf_op jit(solution)/shard_map/ppermute | solution.py:231
  73.8 8.5 %collective-permute-start.8 = (bf16[4,192,128]{2,1,0:T(8,128)(2,1)S(1)}, bf16[4,192,128]{2,1,0:T(8,128)(2,1)S(1)}, u32[]{:S(2)}, u32[]{:S(2)}) collective-permute-start(bf16[4,192,128]{2,1,0:T(8,128)(2,1)S(1)} %collective-permute-done.7.refs_2_), channel_id=1, source_target_pairs={{0,1},{1,0},{2,3},{3,2},{4,5},{5,4},{6,7},{7,6},{8,9},{9,8},{10,11... | collective-permute-start | bytes 589832 | tf_op jit(solution)/shard_map/ppermute | solution.py:231
  90.8 6.0 %collective-permute-start.12 = (bf16[64,1024]{1,0:T(8,128)(2,1)S(1)}, bf16[64,1024]{1,0:T(8,128)(2,1)S(1)}, u32[]{:S(2)}, u32[]{:S(2)}) collective-permute-start(bf16[64,1024]{1,0:T(8,128)(2,1)S(1)} %get-tuple-element.18), channel_id=1, source_target_pairs={{0,12},{4,0},{8,4},{12,8},{1,13},{5,1},{9,5},{13,9},{2,14},{6,2},{... | collective-permute-start | bytes 393224 | tf_op jit(solution)/shard_map/ppermute | solution.py:345
  91.2 14.9 %collective-permute-start.13 = (bf16[64,1024]{1,0:T(8,128)(2,1)S(1)}, bf16[64,1024]{1,0:T(8,128)(2,1)S(1)}, u32[]{:S(2)}, u32[]{:S(2)}) collective-permute-start(bf16[64,1024]{1,0:T(8,128)(2,1)S(1)} %get-tuple-element.19), channel_id=1, source_target_pairs={{0,8},{4,12},{8,0},{12,4},{1,9},{5,13},{9,1},{13,5},{2,10},{6,14},... | collective-permute-start | bytes 393224 | tf_op jit(solution)/shard_map/ppermute | solution.py:345
  93.5 12.5 %collective-permute-start.14 = (bf16[64,1024]{1,0:T(8,128)(2,1)S(1)}, bf16[64,1024]{1,0:T(8,128)(2,1)S(1)}, u32[]{:S(2)}, u32[]{:S(2)}) collective-permute-start(bf16[64,1024]{1,0:T(8,128)(2,1)S(1)} %get-tuple-element.20), channel_id=1, source_target_pairs={{0,4},{4,8},{8,12},{12,0},{1,5},{5,9},{9,13},{13,1},{2,6},{6,10},{... | collective-permute-start | bytes 393224 | tf_op jit(solution)/shard_map/ppermute | solution.py:345

commit v2 on v1

--- a/solution.py
+++ b/solution.py
@@ -7,9 +7,10 @@
 from jax.experimental.pallas import tpu as pltpu
 from jax.sharding import PartitionSpec as P
 
+
 CAP = 16
 EPSILON = 1e-06
-VMEM_BYTES = 40 << 20
+VMEM_BYTES = 4 << 20
 ROWS_CONTRACTED = (((1,), (1,)), ((), ()))
 
 
@@ -27,10 +28,27 @@
     return hi, mid, low
 
 
-def pack_kernel(where, x_ref, gain_ref, ids_ref, weights_ref, out_ref):
+def pack_kernel(where, x_hbm, gain_hbm, ids_hbm, weights_hbm, out_ref, *scratch):
+    x_ref, gain_ref, ids_ref, weights_ref, sems = scratch
     rows, width = x_ref.shape
+    mine = pl.ds(pl.multiple_of(where[0] * width, 128), width)
+    copies = [
+        pltpu.make_async_copy(source, target, sems.at[n])
+        for n, (source, target) in enumerate(
+            (
+                (x_hbm, x_ref),
+                (gain_hbm.at[:, mine], gain_ref),
+                (ids_hbm, ids_ref),
+                (weights_hbm, weights_ref),
+            )
+        )
+    ]
+    for copy in copies:
+        copy.start()
+    for copy in copies:
+        copy.wait()
     values = x_ref[...].astype(jnp.float32)
-    gain = gain_ref[:, pl.ds(pl.multiple_of(where[0] * width, 128), width)]
+    gain = gain_ref[...]
     out_ref[:rows, :] = (values * gain).astype(jnp.bfloat16)
     squares = values * values
     folded = squares[:, :128]
@@ -71,7 +89,7 @@
         )
     tokens = ids_all.shape[1]
     expert_row = lax.broadcasted_iota(jnp.int32, (experts, tokens), 0)
-    mine = (expert_row + where[0] * experts).astype(jnp.float32)
+    mine = (expert_row + where[where.shape[0] - 1] * experts).astype(jnp.float32)
     member = jnp.zeros((experts, tokens), jnp.float32)
     weight = jnp.zeros((experts, tokens), jnp.float32)
     for k in range(ids_all.shape[0]):
@@ -95,6 +113,21 @@
 def one_hot(code_row, slots):
     place = lax.broadcasted_iota(jnp.int32, (slots, code_row.shape[1]), 0).astype(jnp.float32)
     return jnp.where(code_row == place, 1.0, 0.0)
+
+
+def fetch_kernel(source, target, sems):
+    parts = sems.shape[0]
+    size = source.shape[0] // parts
+    copies = [
+        pltpu.make_async_copy(
+            source.at[pl.ds(n * size, size)], target.at[pl.ds(n * size, size)], sems.at[n]
+        )
+        for n in range(parts)
+    ]
+    for copy in copies:
+        copy.start()
+    for copy in copies:
+        copy.wait()
 
 
 def first_half_kernel(where, xa_ref, xb_ref, ga_ref, gb_ref, ua_ref, ub_ref, gate_ref, up_ref):
@@ -138,7 +171,7 @@
     out_ref[0] = packed.astype(jnp.bfloat16)
 
 
-def down_kernel(where, *refs, shards, last):
+def down_kernel(where, *refs, shards, first, last):
     pieces, (code_ref, d_ref), rest = refs[:shards], refs[shards : shards + 2], refs[shards + 2 :]
     if last:
         before_ref, own_ref, *send_refs, joined, acc = rest
@@ -146,8 +179,7 @@
         own_ref, joined, acc = rest
     step = pl.program_id(0)
     units, slots = joined.shape[1:]
-    pair = d_ref.shape[0]
-    tokens = acc.shape[0]
+    pair = code_ref.shape[0]
 
     @pl.when(step == 0)
     def _():
@@ -159,7 +191,7 @@
     for n in range(pair):
         spread = one_hot(code_ref[n], slots).T.astype(jnp.bfloat16)
         hidden = dot_rows(spread, packed).astype(jnp.bfloat16)
-        acc[...] += dot_rows(hidden, d_ref[n])
+        acc[...] += dot_rows(hidden, d_ref[(step + first) * pair + n])
 
     @pl.when(step == pl.num_programs(0) - 1)
     def _():
@@ -197,29 +229,55 @@
     count = blocks * rows
     slots = 2 * blocks * CAP
     me = lax.axis_index("tensor")
-    expert_at = lax.axis_index("expert").astype(jnp.int32)[None]
-    order = jnp.stack([(me ^ n).astype(jnp.int32) for n in range(shards)])
+    order = jnp.stack([me ^ n for n in range(shards)] + [lax.axis_index("expert")])
+    order = order.astype(jnp.int32)
     top = expert_ids.shape[1]
 
+    in_hbm = functools.partial(pltpu.with_memory_space_constraint, memory_space=pltpu.HBM)
+    in_vmem = functools.partial(pltpu.with_memory_space_constraint, memory_space=pltpu.VMEM)
+    gate_hbm, up_hbm = in_hbm(gate_proj), in_hbm(up_proj)
     packed = pl.pallas_call(
         pack_kernel,
         grid_spec=pltpu.PrefetchScalarGridSpec(
             num_scalar_prefetch=1,
             grid=(1,),
-            in_specs=[
-                whole((rows, width)), whole((1, features)), whole((top, rows)), whole((top, rows)),
+            in_specs=[pl.BlockSpec(memory_space=pltpu.HBM)] * 4,
+            out_specs=whole((rows + 8, width)),
+            scratch_shapes=[
+                pltpu.VMEM((rows, width), jnp.bfloat16),
+                pltpu.VMEM((1, width), jnp.float32),
+                pltpu.VMEM((top, rows), jnp.int32),
+                pltpu.VMEM((top, rows), jnp.float32),
+                pltpu.SemaphoreType.DMA((4,)),
             ],
-            out_specs=whole((rows + 8, width)),
         ),
         out_shape=jax.ShapeDtypeStruct((rows + 8, width), jnp.bfloat16),
         compiler_params=params(),
         name="pack",
-    )(order, tokens, norm_gain[None, :], expert_ids.T, gate_weights.T)
-
-    pieces = [packed] + [
-        lax.ppermute(packed, "expert", [(i, (i + n) % blocks) for i in range(blocks)])
-        for n in range(1, blocks)
-    ]
+    )(
+        order,
+        in_hbm(tokens),
+        in_hbm(norm_gain[None, :]),
+        in_hbm(expert_ids.T),
+        in_hbm(gate_weights.T),
+    )
+
+    def shift(v, n):
+        return lax.ppermute(v, "expert", [(i, (i + n) % blocks) for i in range(blocks)])
+
+    pieces = [packed] + [shift(packed, n) for n in range(1, blocks)]
+    down_local = pl.pallas_call(
+        fetch_kernel,
+        in_specs=[pl.BlockSpec(memory_space=pltpu.HBM)],
+        out_specs=pl.BlockSpec(memory_space=pltpu.VMEM),
+        out_shape=pltpu.VMEM(down_proj.shape, down_proj.dtype),
+        scratch_shapes=[pltpu.SemaphoreType.DMA((4,))],
+        compiler_params=params(1 << 20),
+        cost_estimate=pl.CostEstimate(
+            flops=0, bytes_accessed=4 * down_proj.size, transcendentals=0
+        ),
+        name="fetch",
+    )(in_hbm(down_proj))
     xa = pl.pallas_call(
         join_kernel,
         out_shape=jax.ShapeDtypeStruct((count + 8, width), jnp.bfloat16),
@@ -230,8 +288,8 @@
     def swap(v, n):
         return lax.ppermute(v, "tensor", [(i, i ^ n) for i in range(shards)])
 
+    xb = swap(xa, 1)
     xc = swap(xa, 2)
-    xb = swap(xa, 1)
     code, weight = pl.pallas_call(
         route_kernel,
         grid_spec=pltpu.PrefetchScalarGridSpec(
@@ -244,7 +302,7 @@
         out_shape=[jax.ShapeDtypeStruct((experts, 1, count), jnp.float32)] * 2,
         compiler_params=params(),
         name="route",
-    )(expert_at, *pieces)
+    )(order, *pieces)
 
     def columns(n, first=0):
         return pl.BlockSpec((2, units, width), lambda i, w: (i + first, 0, w[n]))
@@ -260,14 +318,14 @@
             out_specs=[pl.BlockSpec((2, units, count), lambda i, w: (i, 0, 0))] * 2,
         ),
         out_shape=[act_shape] * 2,
-        compiler_params=params(),
+        compiler_params=params(12 << 20),
         cost_estimate=pl.CostEstimate(
             flops=2 * experts * units * count * features,
             bytes_accessed=2 * experts * units * features,
             transcendentals=0,
         ),
         name="first",
-    )(order, xa, xb, gate_proj, gate_proj, up_proj, up_proj)
+    )(order, xa, xb, gate_hbm, gate_hbm, up_hbm, up_hbm)
     xd = swap(xc, 1)
 
     parts = 2
@@ -287,14 +345,13 @@
                 out_specs=pl.BlockSpec((1, units, slots), lambda i, w: (i, 0, 0)),
             ),
             out_shape=jax.ShapeDtypeStruct((pairs, units, slots), jnp.bfloat16),
-            compiler_params=params(),
+            compiler_params=params(12 << 20),
             cost_estimate=pl.CostEstimate(
                 flops=2 * experts * units * count * features // parts,
                 bytes_accessed=2 * experts * units * features // parts,
                 transcendentals=0,
             ),
-            name=f"second{part}",
-        )(order, xa, xb, xc, xd, gate_proj, gate_proj, up_proj, up_proj, gate_acc, up_acc, code, weight)
+        )(order, xa, xb, xc, xd, gate_hbm, gate_hbm, up_hbm, up_hbm, gate_acc, up_acc, code, weight)
 
     def down(part, pieces, before):
         first = part * pairs
@@ -306,14 +363,14 @@
         else:
             out_shape = [total]
         return pl.pallas_call(
-            functools.partial(down_kernel, shards=shards, last=last),
+            functools.partial(down_kernel, shards=shards, first=first, last=last),
             grid_spec=pltpu.PrefetchScalarGridSpec(
                 num_scalar_prefetch=1,
                 grid=(pairs,),
                 in_specs=[pl.BlockSpec((1, units, slots), lambda i, w: (i, 0, 0))] * shards
                 + [
                     pl.BlockSpec((2, 1, count), lambda i, w: (i + first, 0, 0)),
-                    pl.BlockSpec((2, out_width, hidden_units), lambda i, w: (i + first, 0, 0)),
+                    pl.BlockSpec(memory_space=pltpu.VMEM),
                 ]
                 + [whole(total.shape)] * last,
                 out_specs=[whole(s.shape) for s in out_shape],
@@ -323,20 +380,20 @@
                 ],
             ),
             out_shape=out_shape,
-            compiler_params=params(),
+            compiler_params=params(8 << 20),
             cost_estimate=pl.CostEstimate(
                 flops=2 * experts * count * out_width * hidden_units // parts,
                 bytes_accessed=2 * experts * out_width * hidden_units // parts,
                 transcendentals=0,
             ),
-            name=f"down{part}",
-        )(order, *pieces, code, down_proj, *([before] if last else []))
+        )(order, *pieces, code, in_vmem(down_local), *([before] if last else []))
 
     before = None
     for part in range(parts):
         mine = second(part)
         across = swap(mine, 2)
-        pieces = [mine, swap(mine, 1), across, swap(across, 1)]
+        near = swap(mine, 1)
+        pieces = [mine, near, across, swap(across, 1)]
         before = down(part, pieces, before)
         if part < parts - 1:
             before = before[0]

time: 107 us -> 102 us (0.953)
  waiting for transfers between devices: 39.9 us -> 33 us
  Pallas kernels: 48.7 us -> 53.2 us
  local copies, waits for them, and re-layouts: 2.99 us -> 0.08 us
    ppermute x9, waiting for transfers between devices: 17.9 us -> 11.4 us  [swap(): return lax.ppermute(v, 'tensor', [(i, i ^ n) for i in range(shards)])]
    pallas_call x2 -> x3, Pallas kernels: 16.9 us -> 20 us  [the longest x2 11.8 us: down(): pl.pallas_call(functools.partial(down_kernel, shards=shards, first=first,...]
    unnamed x8 -> x0, local copies, waits for them, and re-layouts: 2.99 us -> none
  transfers between devices with their start and end apart: 15 -> 15, of which waited for: 6 -> 5; matrix products, arithmetic and copies ran while one was open for 0% -> 0% of each run, Pallas kernels for 29% -> 36%
where the time goes in v2:
time: 102 us
  Pallas kernels  53.2 us (52%)
  waiting for transfers between devices  33 us (32%)
  starting transfers between devices  15.6 us (15%)
    pallas_call x2, Pallas kernels, second(): pl.pallas_call(functools.partial(second_half_kernel, features=features),...  16.3 us
    pallas_call x1, Pallas kernels, dense_body(): pl.pallas_call(first_half_kernel, grid_spec=pltpu.PrefetchScalarGridSpec(...  13.6 us
    pallas_call x2, Pallas kernels, down(): pl.pallas_call(functools.partial(down_kernel, shards=shards, first=first,...  11.8 us
    ppermute x3, waiting for transfers between devices, shift(): lax.ppermute(v, 'expert', [(i, (i + n) % blocks) for i in range(blocks)])  11.5 us
    ppermute x9, waiting for transfers between devices, swap(): return lax.ppermute(v, 'tensor', [(i, i ^ n) for i in range(shards)])  11.4 us
    ppermute x3, waiting for transfers between devices, dense_body(): lax.ppermute(v, 'expert', [(i, (i - n) % blocks) for i in range(blocks)])  10.1 us
    pallas_call x1, Pallas kernels, dense_body(): pl.pallas_call(fetch_kernel, in_specs=[pl.BlockSpec(memory_space=pltpu.HB...  8.22 us
    ppermute x3, starting transfers between devices, shift(): lax.ppermute(v, 'expert', [(i, (i + n) % blocks) for i in range(blocks)])  6.14 us
  transfers between devices with their start and end apart: 15, of which 5 were waited for; matrix products, arithmetic and copies ran while one was open for 0% of the time, Pallas kernels for 36%

profile of v2, /device:TPU:0, one launch (start us, length us, event | category | flops | bytes accessed | tf_op | source)
XLA Modules:
  0.0 102.0 jit_solution(18124218381793592654)
XLA Ops:
  0.1 1.7 %pack.1.refs_0_ = bf16[72,1024]{1,0:T(8,128)(2,1)S(1)} custom-call(s32[5]{0:T(128)S(1)} %stack.23.where, bf16[64,1024]{1,0:T(8,128)(2,1)} %x_hbm.1, f32[1,4096]{1,0:T(1,128)} %bitcast.8, s32[8,64]{1,0:T(8,128)} %bitcast.9, f32[8,64]{1,0:T(8,128)} %bitcast.10), custom_call_target="tpu_custom_call" | custom-call | tf_op jit(solution)/shard_map/pack/pallas_call | solution.py:239
  1.8 5.1 %collective-permute-start.2 = (bf16[72,1024]{1,0:T(8,128)(2,1)S(1)}, bf16[72,1024]{1,0:T(8,128)(2,1)S(1)}, u32[]{:S(2)}, u32[]{:S(2)}) collective-permute-start(bf16[72,1024]{1,0:T(8,128)(2,1)S(1)} %pack.1.refs_0_), channel_id=1, source_target_pairs={{0,12},{4,0},{8,4},{12,8},{1,13},{5,1},{9,5},{13,9},{2,14},{6,2},{... | collective-permute-start | bytes 442376 | tf_op jit(solution)/shard_map/ppermute | solution.py:266
  6.9 1.0 collective-permute-start
  7.9 3.3 %collective-permute-done.2.refs_3_ = bf16[72,1024]{1,0:T(8,128)(2,1)S(1)} collective-permute-done((bf16[72,1024]{1,0:T(8,128)(2,1)S(1)}, bf16[72,1024]{1,0:T(8,128)(2,1)S(1)}, u32[]{:S(2)}, u32[]{:S(2)}) %collective-permute-start.2) | collective-permute-done | bytes 147488 | tf_op jit(solution)/shard_map/ppermute | solution.py:266
  11.2 8.2 %collective-permute-done.1.refs_2_ = bf16[72,1024]{1,0:T(8,128)(2,1)S(1)} collective-permute-done((bf16[72,1024]{1,0:T(8,128)(2,1)S(1)}, bf16[72,1024]{1,0:T(8,128)(2,1)S(1)}, u32[]{:S(2)}, u32[]{:S(2)}) %collective-permute-start.1) | collective-permute-done | bytes 147488 | tf_op jit(solution)/shard_map/ppermute | solution.py:266
  19.5 1.5 %collective-permute-start.4 = (bf16[264,1024]{1,0:T(8,128)(2,1)S(1)}, bf16[264,1024]{1,0:T(8,128)(2,1)S(1)}, u32[]{:S(2)}, u32[]{:S(2)}) collective-permute-start(bf16[264,1024]{1,0:T(8,128)(2,1)S(1)} %join.1.xa_ref), channel_id=1, source_target_pairs={{0,2},{1,3},{2,0},{3,1},{4,6},{5,7},{6,4},{7,5},{8,10},{9,11},{10,... | collective-permute-start | bytes 1622024 | tf_op jit(solution)/shard_map/ppermute | solution.py:289
  21.0 0.8 route.1
  21.8 11.4 %collective-permute-done.4.xc_ref = bf16[264,1024]{1,0:T(8,128)(2,1)S(1)} collective-permute-done((bf16[264,1024]{1,0:T(8,128)(2,1)S(1)}, bf16[264,1024]{1,0:T(8,128)(2,1)S(1)}, u32[]{:S(2)}, u32[]{:S(2)}) %collective-permute-start.4) | collective-permute-done | bytes 540704 | tf_op jit(solution)/shard_map/ppermute | solution.py:289
  33.1 13.6 %first.1 = (f32[16,192,256]{2,1,0:T(8,128)S(1)}, f32[16,192,256]{2,1,0:T(8,128)S(1)}) custom-call(s32[5]{0:T(128)S(1)} %stack.23.where, bf16[264,1024]{1,0:T(8,128)(2,1)S(1)} %join.1.xa_ref, bf16[264,1024]{1,0:T(8,128)(2,1)S(1)} %collective-permute-done.3.xb_ref, bf16[16,192,4096]{2,1,0:T(8,128)(2,1)} %gd_ref.3, bf16[16,192,4096]{2,1,0:T(8,128)(2,1)} %gd_ref.3, ...), custom_call_target="tpu_custom_call" | custom-call | flops 6442450944 | bytes 25165824 | tf_op jit(solution)/shard_map/first/pallas_call | solution.py:312
  46.8 8.2 %shard_map.74.refs_0_ = bf16[4,192,128]{2,1,0:T(8,128)(2,1)S(1)} custom-call(s32[5]{0:T(128)S(1)} %stack.23.where, bf16[264,1024]{1,0:T(8,128)(2,1)S(1)} %join.1.xa_ref, bf16[264,1024]{1,0:T(8,128)(2,1)S(1)} %collective-permute-done.3.xb_ref, bf16[264,1024]{1,0:T(8,128)(2,1)S(1)} %collective-permute-done.4.xc_ref, ...), custom_call_target="tpu_custom_call" | custom-call | flops 3221225472 | bytes 12582912 | tf_op jit(solution)/shard_map/pallas_call | solution.py:336
  55.0 1.5 %collective-permute-start.10 = (bf16[4,192,128]{2,1,0:T(8,128)(2,1)S(1)}, bf16[4,192,128]{2,1,0:T(8,128)(2,1)S(1)}, u32[]{:S(2)}, u32[]{:S(2)}) collective-permute-start(bf16[4,192,128]{2,1,0:T(8,128)(2,1)S(1)} %shard_map.74.refs_0_), channel_id=1, source_target_pairs={{0,2},{1,3},{2,0},{3,1},{4,6},{5,7},{6,4},{7,5},{8,10},{9,11},{10,... | collective-permute-start | bytes 589832 | tf_op jit(solution)/shard_map/ppermute | solution.py:289
  56.5 8.2 %shard_map.73.refs_0_ = bf16[4,192,128]{2,1,0:T(8,128)(2,1)S(1)} custom-call(s32[5]{0:T(128)S(1)} %stack.23.where, bf16[264,1024]{1,0:T(8,128)(2,1)S(1)} %join.1.xa_ref, bf16[264,1024]{1,0:T(8,128)(2,1)S(1)} %collective-permute-done.3.xb_ref, bf16[264,1024]{1,0:T(8,128)(2,1)S(1)} %collective-permute-done.4.xc_ref, ...), custom_call_target="tpu_custom_call" | custom-call | flops 3221225472 | bytes 12582912 | tf_op jit(solution)/shard_map/pallas_call | solution.py:336
  64.7 0.6 collective-permute-start.7
  65.3 0.5 collective-permute-start.11
  65.8 8.2 %fetch.1.refs_5_ = bf16[16,1024,768]{2,1,0:T(8,128)(2,1)S(1)} custom-call(bf16[16,1024,768]{2,1,0:T(8,128)(2,1)} %source.1), custom_call_target="tpu_custom_call" | custom-call | bytes 50331648 | tf_op jit(solution)/shard_map/fetch/pallas_call | solution.py:269
  74.1 0.5 collective-permute-start.8
  74.6 5.9 %shard_map.75.refs_6_ = f32[256,1024]{1,0:T(8,128)S(1)} custom-call(s32[5]{0:T(128)S(1)} %stack.23.where, bf16[4,192,128]{2,1,0:T(8,128)(2,1)S(1)} %shard_map.74.refs_0_, bf16[4,192,128]{2,1,0:T(8,128)(2,1)S(1)} %collective-permute-done.9.refs_1_, bf16[4,192,128]{2,1,0:T(8,128)(2,1)S(1)} %collective-permute-done.10.refs_2_, ...), custom_call_target="tpu_custom_call" | custom-call | flops 3221225472 | bytes 12582912 | tf_op jit(solution)/shard_map/pallas_call | solution.py:365
  80.5 5.9 %shard_map.76 = (f32[64,1024]{1,0:T(8,128)S(1)}, bf16[64,1024]{1,0:T(8,128)(2,1)S(1)}, bf16[64,1024]{1,0:T(8,128)(2,1)S(1)}, bf16[64,1024]{1,0:T(8,128)(2,1)S(1)}) custom-call(s32[5]{0:T(128)S(1)} %stack.23.where, bf16[4,192,128]{2,1,0:T(8,128)(2,1)S(1)} %shard_map.73.refs_0_, bf16[4,192,128]{2,1,0:T(8,128)(2,1)S(1)} %collective-permute-done.6.refs_1_, ...), custom_call_target="tpu_custom_call" | custom-call | flops 3221225472 | bytes 12582912 | tf_op jit(solution)/shard_map/pallas_call | solution.py:365
  86.4 0.4 collective-permute-start.12
  86.9 2.3 %collective-permute-start.13 = (bf16[64,1024]{1,0:T(8,128)(2,1)S(1)}, bf16[64,1024]{1,0:T(8,128)(2,1)S(1)}, u32[]{:S(2)}, u32[]{:S(2)}) collective-permute-start(bf16[64,1024]{1,0:T(8,128)(2,1)S(1)} %get-tuple-element.19), channel_id=1, source_target_pairs={{0,8},{4,12},{8,0},{12,4},{1,9},{5,13},{9,1},{13,5},{2,10},{6,14},... | collective-permute-start | bytes 393224 | tf_op jit(solution)/shard_map/ppermute | solution.py:402
  89.2 1.9 %collective-permute-start.14 = (bf16[64,1024]{1,0:T(8,128)(2,1)S(1)}, bf16[64,1024]{1,0:T(8,128)(2,1)S(1)}, u32[]{:S(2)}, u32[]{:S(2)}) collective-permute-start(bf16[64,1024]{1,0:T(8,128)(2,1)S(1)} %get-tuple-element.20), channel_id=1, source_target_pairs={{0,4},{4,8},{8,12},{12,0},{1,5},{5,9},{9,13},{13,1},{2,6},{6,10},{... | collective-permute-start | bytes 393224 | tf_op jit(solution)/shard_map/ppermute | solution.py:402
  91.1 0.8 collective-permute-done.12.refs_0_
  92.0 9.3 %collective-permute-done.13.refs_1_ = bf16[64,1024]{1,0:T(8,128)(2,1)S(1)} collective-permute-done((bf16[64,1024]{1,0:T(8,128)(2,1)S(1)}, bf16[64,1024]{1,0:T(8,128)(2,1)S(1)}, u32[]{:S(2)}, u32[]{:S(2)}) %collective-permute-start.13) | collective-permute-done | bytes 131104 | tf_op jit(solution)/shard_map/ppermute | solution.py:402
  101.3 0.7 finish.1
  (17 shorter events, 0.3 us)
Async XLA Ops:
  1.8 9.4 %collective-permute-start.2 = (bf16[72,1024]{1,0:T(8,128)(2,1)S(1)}, bf16[72,1024]{1,0:T(8,128)(2,1)S(1)}, u32[]{:S(2)}, u32[]{:S(2)}) collective-permute-start(bf16[72,1024]{1,0:T(8,128)(2,1)S(1)} %pack.1.refs_0_), channel_id=1, source_target_pairs={{0,12},{4,0},{8,4},{12,8},{1,13},{5,1},{9,5},{13,9},{2,14},{6,2},{... | collective-permute-start | bytes 442376 | tf_op jit(solution)/shard_map/ppermute | solution.py:266
  6.9 12.5 %collective-permute-start.1 = (bf16[72,1024]{1,0:T(8,128)(2,1)S(1)}, bf16[72,1024]{1,0:T(8,128)(2,1)S(1)}, u32[]{:S(2)}, u32[]{:S(2)}) collective-permute-start(bf16[72,1024]{1,0:T(8,128)(2,1)S(1)} %pack.1.refs_0_), channel_id=1, source_target_pairs={{0,8},{4,12},{8,0},{12,4},{1,9},{5,13},{9,1},{13,5},{2,10},{6,14},... | collective-permute-start | bytes 442376 | tf_op jit(solution)/shard_map/ppermute | solution.py:266
  6.9 12.5 %collective-permute-start = (bf16[72,1024]{1,0:T(8,128)(2,1)S(1)}, bf16[72,1024]{1,0:T(8,128)(2,1)S(1)}, u32[]{:S(2)}, u32[]{:S(2)}) collective-permute-start(bf16[72,1024]{1,0:T(8,128)(2,1)S(1)} %pack.1.refs_0_), channel_id=1, source_target_pairs={{0,4},{4,8},{8,12},{12,0},{1,5},{5,9},{9,13},{13,1},{2,6},{6,10},{... | collective-permute-start | bytes 442376 | tf_op jit(solution)/shard_map/ppermute | solution.py:266
  19.5 13.6 %collective-permute-start.4 = (bf16[264,1024]{1,0:T(8,128)(2,1)S(1)}, bf16[264,1024]{1,0:T(8,128)(2,1)S(1)}, u32[]{:S(2)}, u32[]{:S(2)}) collective-permute-start(bf16[264,1024]{1,0:T(8,128)(2,1)S(1)} %join.1.xa_ref), channel_id=1, source_target_pairs={{0,2},{1,3},{2,0},{3,1},{4,6},{5,7},{6,4},{7,5},{8,10},{9,11},{10,... | collective-permute-start | bytes 1622024 | tf_op jit(solution)/shard_map/ppermute | solution.py:289
  21.0 12.1 %collective-permute-start.3 = (bf16[264,1024]{1,0:T(8,128)(2,1)S(1)}, bf16[264,1024]{1,0:T(8,128)(2,1)S(1)}, u32[]{:S(2)}, u32[]{:S(2)}) collective-permute-start(bf16[264,1024]{1,0:T(8,128)(2,1)S(1)} %join.1.xa_ref), channel_id=1, source_target_pairs={{0,1},{1,0},{2,3},{3,2},{4,5},{5,4},{6,7},{7,6},{8,9},{9,8},{10,11... | collective-permute-start | bytes 1622024 | tf_op jit(solution)/shard_map/ppermute | solution.py:289
  33.1 13.6 %collective-permute-start.5 = (bf16[264,1024]{1,0:T(8,128)(2,1)S(1)}, bf16[264,1024]{1,0:T(8,128)(2,1)S(1)}, u32[]{:S(2)}, u32[]{:S(2)}) collective-permute-start(bf16[264,1024]{1,0:T(8,128)(2,1)S(1)} %collective-permute-done.4.xc_ref), channel_id=1, source_target_pairs={{0,1},{1,0},{2,3},{3,2},{4,5},{5,4},{6,7},{7,6},{8,9},{9,8},{10,11... | collective-permute-start | bytes 1622024 | tf_op jit(solution)/shard_map/ppermute | solution.py:289
  55.0 10.3 %collective-permute-start.10 = (bf16[4,192,128]{2,1,0:T(8,128)(2,1)S(1)}, bf16[4,192,128]{2,1,0:T(8,128)(2,1)S(1)}, u32[]{:S(2)}, u32[]{:S(2)}) collective-permute-start(bf16[4,192,128]{2,1,0:T(8,128)(2,1)S(1)} %shard_map.74.refs_0_), channel_id=1, source_target_pairs={{0,2},{1,3},{2,0},{3,1},{4,6},{5,7},{6,4},{7,5},{8,10},{9,11},{10,... | collective-permute-start | bytes 589832 | tf_op jit(solution)/shard_map/ppermute | solution.py:289
  64.7 9.4 %collective-permute-start.7 = (bf16[4,192,128]{2,1,0:T(8,128)(2,1)S(1)}, bf16[4,192,128]{2,1,0:T(8,128)(2,1)S(1)}, u32[]{:S(2)}, u32[]{:S(2)}) collective-permute-start(bf16[4,192,128]{2,1,0:T(8,128)(2,1)S(1)} %shard_map.73.refs_0_), channel_id=1, source_target_pairs={{0,2},{1,3},{2,0},{3,1},{4,6},{5,7},{6,4},{7,5},{8,10},{9,11},{10,... | collective-permute-start | bytes 589832 | tf_op jit(solution)/shard_map/ppermute | solution.py:289
  65.3 9.3 %collective-permute-start.9 = (bf16[4,192,128]{2,1,0:T(8,128)(2,1)S(1)}, bf16[4,192,128]{2,1,0:T(8,128)(2,1)S(1)}, u32[]{:S(2)}, u32[]{:S(2)}) collective-permute-start(bf16[4,192,128]{2,1,0:T(8,128)(2,1)S(1)} %shard_map.74.refs_0_), channel_id=1, source_target_pairs={{0,1},{1,0},{2,3},{3,2},{4,5},{5,4},{6,7},{7,6},{8,9},{9,8},{10,11... | collective-permute-start | bytes 589832 | tf_op jit(solution)/shard_map/ppermute | solution.py:289
  65.3 9.3 %collective-permute-start.11 = (bf16[4,192,128]{2,1,0:T(8,128)(2,1)S(1)}, bf16[4,192,128]{2,1,0:T(8,128)(2,1)S(1)}, u32[]{:S(2)}, u32[]{:S(2)}) collective-permute-start(bf16[4,192,128]{2,1,0:T(8,128)(2,1)S(1)} %collective-permute-done.10.refs_2_), channel_id=1, source_target_pairs={{0,1},{1,0},{2,3},{3,2},{4,5},{5,4},{6,7},{7,6},{8,9},{9,8},{10,11... | collective-permute-start | bytes 589832 | tf_op jit(solution)/shard_map/ppermute | solution.py:289
  74.0 6.5 %collective-permute-start.6 = (bf16[4,192,128]{2,1,0:T(8,128)(2,1)S(1)}, bf16[4,192,128]{2,1,0:T(8,128)(2,1)S(1)}, u32[]{:S(2)}, u32[]{:S(2)}) collective-permute-start(bf16[4,192,128]{2,1,0:T(8,128)(2,1)S(1)} %shard_map.73.refs_0_), channel_id=1, source_target_pairs={{0,1},{1,0},{2,3},{3,2},{4,5},{5,4},{6,7},{7,6},{8,9},{9,8},{10,11... | collective-permute-start | bytes 589832 | tf_op jit(solution)/shard_map/ppermute | solution.py:289
  74.1 6.4 %collective-permute-start.8 = (bf16[4,192,128]{2,1,0:T(8,128)(2,1)S(1)}, bf16[4,192,128]{2,1,0:T(8,128)(2,1)S(1)}, u32[]{:S(2)}, u32[]{:S(2)}) collective-permute-start(bf16[4,192,128]{2,1,0:T(8,128)(2,1)S(1)} %collective-permute-done.7.refs_2_), channel_id=1, source_target_pairs={{0,1},{1,0},{2,3},{3,2},{4,5},{5,4},{6,7},{7,6},{8,9},{9,8},{10,11... | collective-permute-start | bytes 589832 | tf_op jit(solution)/shard_map/ppermute | solution.py:289
  86.4 5.5 %collective-permute-start.12 = (bf16[64,1024]{1,0:T(8,128)(2,1)S(1)}, bf16[64,1024]{1,0:T(8,128)(2,1)S(1)}, u32[]{:S(2)}, u32[]{:S(2)}) collective-permute-start(bf16[64,1024]{1,0:T(8,128)(2,1)S(1)} %get-tuple-element.18), channel_id=1, source_target_pairs={{0,12},{4,0},{8,4},{12,8},{1,13},{5,1},{9,5},{13,9},{2,14},{6,2},{... | collective-permute-start | bytes 393224 | tf_op jit(solution)/shard_map/ppermute | solution.py:402
  86.9 14.4 %collective-permute-start.13 = (bf16[64,1024]{1,0:T(8,128)(2,1)S(1)}, bf16[64,1024]{1,0:T(8,128)(2,1)S(1)}, u32[]{:S(2)}, u32[]{:S(2)}) collective-permute-start(bf16[64,1024]{1,0:T(8,128)(2,1)S(1)} %get-tuple-element.19), channel_id=1, source_target_pairs={{0,8},{4,12},{8,0},{12,4},{1,9},{5,13},{9,1},{13,5},{2,10},{6,14},... | collective-permute-start | bytes 393224 | tf_op jit(solution)/shard_map/ppermute | solution.py:402
  89.2 12.1 %collective-permute-start.14 = (bf16[64,1024]{1,0:T(8,128)(2,1)S(1)}, bf16[64,1024]{1,0:T(8,128)(2,1)S(1)}, u32[]{:S(2)}, u32[]{:S(2)}) collective-permute-start(bf16[64,1024]{1,0:T(8,128)(2,1)S(1)} %get-tuple-element.20), channel_id=1, source_target_pairs={{0,4},{4,8},{8,12},{12,0},{1,5},{5,9},{9,13},{13,1},{2,6},{6,10},{... | collective-permute-start | bytes 393224 | tf_op jit(solution)/shard_map/ppermute | solution.py:402

commit v3 on v2

--- a/solution.py
+++ b/solution.py
@@ -115,83 +115,165 @@
     return jnp.where(code_row == place, 1.0, 0.0)
 
 
-def fetch_kernel(source, target, sems):
-    parts = sems.shape[0]
-    size = source.shape[0] // parts
-    copies = [
+def gate_up_copies(column, first, sources, target, sems):
+    experts, _, _, width = target.shape
+    columns = pl.ds(pl.multiple_of(column * width, 128), width)
+    return [
         pltpu.make_async_copy(
-            source.at[pl.ds(n * size, size)], target.at[pl.ds(n * size, size)], sems.at[n]
-        )
-        for n in range(parts)
+            source.at[pl.ds(first, experts), :, columns], target.at[:, n], sems.at[n]
+        )
+        for n, source in enumerate(sources)
     ]
+
+
+def down_copies(first, source, target, sems):
+    half = target.shape[0] // 2
+    return [
+        pltpu.make_async_copy(
+            source.at[pl.ds(first + n * half, half)], target.at[pl.ds(n * half, half)], sems.at[n]
+        )
+        for n in range(2)
+    ]
+
+
+def start_at_first_step(copies):
+    @pl.when(pl.program_id(0) == 0)
+    def _():
+        for copy in copies:
+            copy.start()
+
+
+def wait_at_last_step(copies):
+    @pl.when(pl.program_id(0) == pl.num_programs(0) - 1)
+    def _():
+        for copy in copies:
+            copy.wait()
+
+
+def fetch_kernel(where, gate_hbm, up_hbm, *refs):
+    *targets, sems = refs
+    copies = []
+    for n, target in enumerate(targets):
+        copies += gate_up_copies(
+            where[0] // 2, n * target.shape[0], (gate_hbm, up_hbm), target, sems.at[n]
+        )
     for copy in copies:
         copy.start()
     for copy in copies:
         copy.wait()
 
 
-def first_half_kernel(where, xa_ref, xb_ref, ga_ref, gb_ref, ua_ref, ub_ref, gate_ref, up_ref):
-    pair, units, width = ga_ref.shape
-    tokens = gate_ref.shape[2]
-    xa, xb = xa_ref[:tokens, :], xb_ref[:tokens, :]
-    for a_ref, b_ref, out_ref in ((ga_ref, gb_ref, gate_ref), (ua_ref, ub_ref, up_ref)):
-        acc = dot_rows(a_ref[...].reshape(pair * units, width), xa)
-        acc = acc + dot_rows(b_ref[...].reshape(pair * units, width), xb)
-        out_ref[...] = acc.reshape(pair, units, tokens)
+def first_half_kernel(
+    where, xa_ref, xb_ref, w_ref, gate_hbm, up_hbm, acc_ref, next_ref, x_all, sems, *, first
+):
+    step = pl.program_id(0)
+    copies = gate_up_copies(1 - where[0] // 2, first, (gate_hbm, up_hbm), next_ref, sems)
+    start_at_first_step(copies)
+    tokens, width = x_all.shape[0], xa_ref.shape[1]
+
+    @pl.when(step == 0)
+    def _():
+        for n, x_ref in enumerate((xa_ref, xb_ref)):
+            at = pl.multiple_of(where[n] % 2 * width, 128)
+            x_all[:, pl.ds(at, width)] = x_ref[:tokens, :]
+
+    pair = 2
+    _, kinds, units, depth = w_ref.shape
+    weights = w_ref[pl.ds(step * pair, pair)].reshape(pair * kinds * units, depth)
+    acc = dot_rows(weights, x_all[...])
+    acc_ref[pl.ds(step * pair, pair)] = acc.reshape(pair, kinds, units, tokens)
+    wait_at_last_step(copies)
 
 
 def second_half_kernel(
-    where, xa_ref, xb_ref, xc_ref, xd_ref, gc_ref, gd_ref, uc_ref, ud_ref,
-    gate_ref, up_ref, code_ref, weight_ref, out_ref, *, features,
+    where, xa_ref, xb_ref, near_ref, far_ref, near_own_ref, far_own_ref, w_ref, acc_ref,
+    code_ref, weight_ref, down_hbm, out_ref, next_ref, x_all, inv_ref, sems, *, features, first,
 ):
-    pair, units, width = gc_ref.shape
-    tokens = gate_ref.shape[2]
+    step = pl.program_id(0)
+    copies = down_copies(first, down_hbm, next_ref, sems)
+    start_at_first_step(copies)
+    tokens, width = x_all.shape[0], xa_ref.shape[1]
+    rows = near_own_ref.shape[0] - 8
+
+    @pl.when(step == 0)
+    def _():
+        total = jnp.zeros((1, tokens), jnp.float32)
+        for x_ref in (xa_ref, xb_ref):
+            row = x_ref[tokens:, :].astype(jnp.float32)[:1]
+            for part in range(3):
+                total = total + row[:, part * tokens : (part + 1) * tokens]
+        inv_ref[...] = total
+        others = tokens - rows
+        for n, (own_ref, x_ref) in enumerate(((near_own_ref, near_ref), (far_own_ref, far_ref)), 2):
+            at = pl.multiple_of(where[n] % 2 * width, 128)
+            x_all[:rows, pl.ds(at, width)] = own_ref[:rows, :]
+            x_all[rows:, pl.ds(at, width)] = x_ref[:others, :]
+            own_row = own_ref[rows:, :].astype(jnp.float32)[:1]
+            row = x_ref[others:, :].astype(jnp.float32)[:1]
+            for part in range(3):
+                inv_ref[:, :rows] += own_row[:, 128 * (4 + part) : 128 * (4 + part) + rows]
+                inv_ref[:, rows:] += row[:, part * others : (part + 1) * others]
+        inv_ref[...] = lax.rsqrt(inv_ref[...] / features + EPSILON)
+
+    pair = 2
+    _, kinds, units, depth = w_ref.shape
     slots = out_ref.shape[2]
-    total = jnp.zeros((1, tokens), jnp.float32)
-    for x_ref in (xa_ref, xb_ref, xc_ref, xd_ref):
-        row = x_ref[tokens:, :].astype(jnp.float32)[:1]
-        for part in range(3):
-            total = total + row[:, part * tokens : (part + 1) * tokens]
-    inv = lax.rsqrt(total / features + EPSILON)
-    xc, xd = xc_ref[:tokens, :], xd_ref[:tokens, :]
-    acts = []
-    for acc_ref, c_ref, d_ref in ((gate_ref, gc_ref, gd_ref), (up_ref, uc_ref, ud_ref)):
-        acc = acc_ref[...].reshape(pair * units, tokens)
-        acc = acc + dot_rows(c_ref[...].reshape(pair * units, width), xc)
-        acc = acc + dot_rows(d_ref[...].reshape(pair * units, width), xd)
-        acts.append(acc * inv)
-    gate, up = acts
-    hidden = gate / (1.0 + jnp.exp(-gate)) * up
+    mine = pl.ds(step * pair, pair)
+    weights = w_ref[mine].reshape(pair * kinds * units, depth)
+    acc = acc_ref[mine].reshape(pair * kinds * units, tokens)
+    acc = (acc + dot_rows(weights, x_all[...])) * inv_ref[...]
     packed = jnp.zeros((units, slots), jnp.float32)
     for n in range(pair):
-        mine = hidden[n * units : (n + 1) * units] * weight_ref[n]
+        gate = acc[(2 * n) * units : (2 * n + 1) * units]
+        up = acc[(2 * n + 1) * units : (2 * n + 2) * units]
+        hidden = gate / (1.0 + jnp.exp(-gate)) * up * weight_ref[n]
         packed = packed + dot_rows(
-            mine.astype(jnp.bfloat16), one_hot(code_ref[n], slots).astype(jnp.bfloat16)
+            hidden.astype(jnp.bfloat16), one_hot(code_ref[n], slots).astype(jnp.bfloat16)
         )
     out_ref[0] = packed.astype(jnp.bfloat16)
-
-
-def down_kernel(where, *refs, shards, first, last):
-    pieces, (code_ref, d_ref), rest = refs[:shards], refs[shards : shards + 2], refs[shards + 2 :]
-    if last:
-        before_ref, own_ref, *send_refs, joined, acc = rest
+    wait_at_last_step(copies)
+
+
+def down_kernel(where, *refs, shards, span, start, spread, keep, last):
+    refs = list(refs)
+    take = lambda n: [refs.pop(0) for _ in range(n)]
+    if spread:
+        pieces, (code_ref,) = take(shards), take(1)
     else:
-        own_ref, joined, acc = rest
+        (hidden_ref,) = take(1)
+    (d_ref,) = take(1)
+    before = take(0 if start else 1)
+    outs = take(len(refs) - (2 if spread else 1))
+    if keep:
+        kept_ref = outs.pop()
+    own_ref, *send_refs = outs
+    acc = refs[-1]
     step = pl.program_id(0)
-    units, slots = joined.shape[1:]
-    pair = code_ref.shape[0]
+    pair = 2
+    tokens = acc.shape[0]
+    features = slice(*span)
 
     @pl.when(step == 0)
     def _():
-        acc[...] = before_ref[...] if last else jnp.zeros_like(acc)
-
-    for n, piece in enumerate(pieces):
-        joined[where[n]] = piece[0]
-    packed = joined[...].reshape(shards * units, slots)
+        acc[...] = jnp.zeros_like(acc) if start else before[0][:, features]
+
+    if spread:
+        joined = refs[0]
+        units, slots = joined.shape[1:]
+        for n, piece in enumerate(pieces):
+            joined[where[n]] = piece[0]
+        packed = joined[...].reshape(shards * units, slots)
+        places = [one_hot(code_ref[n], slots).T for n in range(pair)]
+        places = jnp.concatenate(places, axis=0).astype(jnp.bfloat16)
+        hidden = dot_rows(places, packed).astype(jnp.bfloat16)
+        if keep:
+            kept_ref[step] = hidden
+    else:
+        hidden = hidden_ref[step]
     for n in range(pair):
-        spread = one_hot(code_ref[n], slots).T.astype(jnp.bfloat16)
-        hidden = dot_rows(spread, packed).astype(jnp.bfloat16)
-        acc[...] += dot_rows(hidden, d_ref[(step + first) * pair + n])
+        acc[...] += dot_rows(
+            hidden[n * tokens : (n + 1) * tokens], d_ref[step * pair + n, features, :]
+        )
 
     @pl.when(step == pl.num_programs(0) - 1)
     def _():
@@ -204,12 +286,17 @@
             own_ref[...] = acc[...]
 
 
-def finish_kernel(own_ref, *refs):
-    *pieces, out_ref = refs
-    total = own_ref[...]
-    for piece in pieces:
-        total = total + piece[...].astype(jnp.float32)
-    out_ref[...] = total.astype(jnp.bfloat16)
+def finish_kernel(*refs):
+    *groups, out_ref = refs
+    spans = out_ref.shape[1] // groups[0].shape[1]
+    each = len(groups) // spans
+    for n in range(spans):
+        own_ref, *pieces = groups[n * each : (n + 1) * each]
+        total = own_ref[...]
+        for piece in pieces:
+            total = total + piece[...].astype(jnp.float32)
+        width = own_ref.shape[1]
+        out_ref[:, n * width : (n + 1) * width] = total.astype(jnp.bfloat16)
 
 
 def params(limit=VMEM_BYTES):
@@ -265,31 +352,49 @@
     def shift(v, n):
         return lax.ppermute(v, "expert", [(i, (i + n) % blocks) for i in range(blocks)])
 
-    pieces = [packed] + [shift(packed, n) for n in range(1, blocks)]
-    down_local = pl.pallas_call(
-        fetch_kernel,
-        in_specs=[pl.BlockSpec(memory_space=pltpu.HBM)],
-        out_specs=pl.BlockSpec(memory_space=pltpu.VMEM),
-        out_shape=pltpu.VMEM(down_proj.shape, down_proj.dtype),
-        scratch_shapes=[pltpu.SemaphoreType.DMA((4,))],
-        compiler_params=params(1 << 20),
-        cost_estimate=pl.CostEstimate(
-            flops=0, bytes_accessed=4 * down_proj.size, transcendentals=0
-        ),
-        name="fetch",
-    )(in_hbm(down_proj))
-    xa = pl.pallas_call(
-        join_kernel,
-        out_shape=jax.ShapeDtypeStruct((count + 8, width), jnp.bfloat16),
-        compiler_params=params(),
-        name="join",
-    )(*pieces)
-
     def swap(v, n):
         return lax.ppermute(v, "tensor", [(i, i ^ n) for i in range(shards)])
 
+    pieces = [packed] + [shift(packed, n) for n in range(1, blocks)]
+    near_own = swap(packed, 2)
+    parts = 2
+    pairs = experts // 2 // parts
+    half = experts // parts
+    buffer = (half, 2, units, features // 2)
+    half_bytes = 4 * units * features * half
+
+    def fetched(flops, moved):
+        return pl.CostEstimate(flops=flops, bytes_accessed=moved, transcendentals=0)
+
+    in_place = pl.BlockSpec(memory_space=pltpu.VMEM)
+    stay = pl.BlockSpec(memory_space=pltpu.HBM)
+    weights = pl.pallas_call(
+        fetch_kernel,
+        grid_spec=pltpu.PrefetchScalarGridSpec(
+            num_scalar_prefetch=1,
+            grid=(1,),
+            in_specs=[stay] * 2,
+            out_specs=[in_place] * parts,
+            scratch_shapes=[pltpu.SemaphoreType.DMA((parts, 2))],
+        ),
+        out_shape=[pltpu.VMEM(buffer, gate_proj.dtype)] * parts,
+        compiler_params=params(1 << 20),
+        cost_estimate=fetched(0, 2 * parts * half_bytes),
+        name="fetch",
+    )(order, gate_hbm, up_hbm)
+
+    def join(blocks_of_rows):
+        return pl.pallas_call(
+            join_kernel,
+            out_shape=jax.ShapeDtypeStruct((len(blocks_of_rows) * rows + 8, width), jnp.bfloat16),
+            compiler_params=params(),
+        )(*blocks_of_rows)
+
+    others = join(pieces[1:])
+    xa = join(pieces)
+    near = swap(others, 2)
     xb = swap(xa, 1)
-    xc = swap(xa, 2)
+    far_own = swap(near_own, 1)
     code, weight = pl.pallas_call(
         route_kernel,
         grid_spec=pltpu.PrefetchScalarGridSpec(
@@ -304,110 +409,128 @@
         name="route",
     )(order, *pieces)
 
-    def columns(n, first=0):
-        return pl.BlockSpec((2, units, width), lambda i, w: (i + first, 0, w[n]))
-
-    x_spec = whole((count + 8, width))
-    act_shape = jax.ShapeDtypeStruct((experts, units, count), jnp.float32)
-    gate_acc, up_acc = pl.pallas_call(
-        first_half_kernel,
-        grid_spec=pltpu.PrefetchScalarGridSpec(
-            num_scalar_prefetch=1,
-            grid=(experts // 2,),
-            in_specs=[x_spec, x_spec] + [columns(0), columns(1)] * 2,
-            out_specs=[pl.BlockSpec((2, units, count), lambda i, w: (i, 0, 0))] * 2,
-        ),
-        out_shape=[act_shape] * 2,
-        compiler_params=params(12 << 20),
-        cost_estimate=pl.CostEstimate(
-            flops=2 * experts * units * count * features,
-            bytes_accessed=2 * experts * units * features,
-            transcendentals=0,
-        ),
-        name="first",
-    )(order, xa, xb, gate_hbm, gate_hbm, up_hbm, up_hbm)
-    xd = swap(xc, 1)
-
-    parts = 2
-    pairs = experts // 2 // parts
-
-    def second(part):
-        first = part * pairs
+    def first(part):
         return pl.pallas_call(
-            functools.partial(second_half_kernel, features=features),
+            functools.partial(first_half_kernel, first=part * half),
             grid_spec=pltpu.PrefetchScalarGridSpec(
                 num_scalar_prefetch=1,
                 grid=(pairs,),
-                in_specs=[x_spec] * 4
-                + [columns(2, first), columns(3, first)] * 2
-                + [pl.BlockSpec((2, units, count), lambda i, w: (i + first, 0, 0))] * 2
-                + [pl.BlockSpec((2, 1, count), lambda i, w: (i + first, 0, 0))] * 2,
-                out_specs=pl.BlockSpec((1, units, slots), lambda i, w: (i, 0, 0)),
+                in_specs=[in_place] * 3 + [stay] * 2,
+                out_specs=[in_place] * 2,
+                scratch_shapes=[
+                    pltpu.VMEM((count, features // 2), jnp.bfloat16),
+                    pltpu.SemaphoreType.DMA((2,)),
+                ],
             ),
-            out_shape=jax.ShapeDtypeStruct((pairs, units, slots), jnp.bfloat16),
-            compiler_params=params(12 << 20),
-            cost_estimate=pl.CostEstimate(
-                flops=2 * experts * units * count * features // parts,
-                bytes_accessed=2 * experts * units * features // parts,
-                transcendentals=0,
-            ),
-        )(order, xa, xb, xc, xd, gate_hbm, gate_hbm, up_hbm, up_hbm, gate_acc, up_acc, code, weight)
-
-    def down(part, pieces, before):
-        first = part * pairs
-        last = part == parts - 1
-        total = jax.ShapeDtypeStruct((count, out_width), jnp.float32)
-        if last:
-            out_shape = [jax.ShapeDtypeStruct((rows, out_width), jnp.float32)]
-            out_shape += [jax.ShapeDtypeStruct((rows, out_width), jnp.bfloat16)] * (blocks - 1)
-        else:
-            out_shape = [total]
+            out_shape=[
+                pltpu.VMEM((half, 2, units, count), jnp.float32),
+                pltpu.VMEM(buffer, gate_proj.dtype),
+            ],
+            compiler_params=params(6 << 20),
+            cost_estimate=fetched(2 * half * units * count * features, half_bytes),
+        )(order, in_vmem(xa), in_vmem(xb), in_vmem(weights[part]), gate_hbm, up_hbm)
+
+    partial = [first(part) for part in range(parts)]
+    far = swap(near, 1)
+    down_hbm = in_hbm(down_proj)
+    down_buffer = (half, out_width, hidden_units)
+
+    def second(part):
+        acc, weights = partial[part]
+        routing = pl.BlockSpec((2, 1, count), lambda i, w: (i + part * pairs, 0, 0))
         return pl.pallas_call(
-            functools.partial(down_kernel, shards=shards, first=first, last=last),
+            functools.partial(second_half_kernel, features=features, first=part * half),
             grid_spec=pltpu.PrefetchScalarGridSpec(
                 num_scalar_prefetch=1,
                 grid=(pairs,),
-                in_specs=[pl.BlockSpec((1, units, slots), lambda i, w: (i, 0, 0))] * shards
-                + [
-                    pl.BlockSpec((2, 1, count), lambda i, w: (i + first, 0, 0)),
-                    pl.BlockSpec(memory_space=pltpu.VMEM),
-                ]
-                + [whole(total.shape)] * last,
-                out_specs=[whole(s.shape) for s in out_shape],
+                in_specs=[in_place] * 8 + [routing] * 2 + [stay],
+                out_specs=[pl.BlockSpec((1, units, slots), lambda i, w: (i, 0, 0)), in_place],
                 scratch_shapes=[
-                    pltpu.VMEM((shards, units, slots), jnp.bfloat16),
-                    pltpu.VMEM(total.shape, jnp.float32),
+                    pltpu.VMEM((count, features // 2), jnp.bfloat16),
+                    pltpu.VMEM((1, count), jnp.float32),
+                    pltpu.SemaphoreType.DMA((2,)),
                 ],
             ),
+            out_shape=[
+                jax.ShapeDtypeStruct((pairs, units, slots), jnp.bfloat16),
+                pltpu.VMEM(down_buffer, down_proj.dtype),
+            ],
+            compiler_params=params(6 << 20),
+            cost_estimate=fetched(2 * half * units * count * features, half_bytes),
+        )(
+            order,
+            *[in_vmem(v) for v in (xa, xb, near, far, near_own, far_own, weights, acc)],
+            code,
+            weight,
+            down_hbm,
+        )
+
+    def down(part, pieces, down_local, before, span, keep, last):
+        wide = span[1] - span[0]
+        spread = len(pieces) > 1
+        if last:
+            out_shape = [jax.ShapeDtypeStruct((rows, wide), jnp.float32)]
+            out_shape += [jax.ShapeDtypeStruct((rows, wide), jnp.bfloat16)] * (blocks - 1)
+        else:
+            out_shape = [pltpu.VMEM((count, wide), jnp.float32)]
+        if keep:
+            out_shape += [pltpu.VMEM((pairs, 2 * count, hidden_units), jnp.bfloat16)]
+        routing = pl.BlockSpec((2, 1, count), lambda i, w: (i + part * pairs, 0, 0))
+        moved = pl.BlockSpec((1, units, slots), lambda i, w: (i, 0, 0))
+        scratch = [pltpu.VMEM((count, wide), jnp.float32)]
+        if spread:
+            scratch = [pltpu.VMEM((shards, units, slots), jnp.bfloat16)] + scratch
+        return pl.pallas_call(
+            functools.partial(
+                down_kernel,
+                shards=shards,
+                span=span,
+                start=before is None,
+                spread=spread,
+                keep=keep,
+                last=last,
+            ),
+            grid_spec=pltpu.PrefetchScalarGridSpec(
+                num_scalar_prefetch=1,
+                grid=(pairs,),
+                in_specs=([moved] * shards + [routing] if spread else [in_place])
+                + [in_place] * (1 if before is None else 2),
+                out_specs=[in_place] * len(out_shape),
+                scratch_shapes=scratch,
+            ),
             out_shape=out_shape,
-            compiler_params=params(8 << 20),
-            cost_estimate=pl.CostEstimate(
-                flops=2 * experts * count * out_width * hidden_units // parts,
-                bytes_accessed=2 * experts * out_width * hidden_units // parts,
-                transcendentals=0,
-            ),
-        )(order, *pieces, code, in_vmem(down_local), *([before] if last else []))
-
-    before = None
-    for part in range(parts):
-        mine = second(part)
+            compiler_params=params(6 << 20),
+            cost_estimate=fetched(2 * half * count * wide * hidden_units, 0),
+        )(
+            order,
+            *(list(pieces) + [code] if spread else [in_vmem(pieces[0])]),
+            in_vmem(down_local),
+            *([] if before is None else [in_vmem(before)]),
+        )
+
+    def exchange(part):
+        mine, down_local = second(part)
         across = swap(mine, 2)
-        near = swap(mine, 1)
-        pieces = [mine, near, across, swap(across, 1)]
-        before = down(part, pieces, before)
-        if part < parts - 1:
-            before = before[0]
-    own, *sends = before
-    back = [
-        lax.ppermute(v, "expert", [(i, (i - n) % blocks) for i in range(blocks)])
-        for n, v in enumerate(sends, 1)
-    ]
+        beside = swap(mine, 1)
+        return [mine, beside, across, swap(across, 1)], down_local
+
+    (total,) = down(0, *exchange(0), None, (0, out_width), False, False)
+    middle = out_width // 2
+    pieces1, down_local = exchange(1)
+    *low, kept = down(1, pieces1, down_local, total, (0, middle), True, True)
+    high = down(1, [kept], down_local, total, (middle, out_width), False, True)
+
+    def send_back(own, sends):
+        return [own] + [shift(v, -n) for n, v in enumerate(sends, 1)]
+
+    low = send_back(low[0], low[1:])
+    high = send_back(high[0], high[1:])
     return pl.pallas_call(
         finish_kernel,
         out_shape=jax.ShapeDtypeStruct((rows, out_width), jnp.bfloat16),
         compiler_params=params(),
         name="finish",
-    )(own, *back)
+    )(*low, *high)
 
 
 def slot_places(expert_ids, total):

time: 102 us -> 94.5 us (0.926)
  waiting for transfers between devices: 33 us -> 25 us
  starting transfers between devices: 15.6 us -> 22 us
  Pallas kernels: 53.2 us -> 47.1 us
    ppermute x3 -> x9, starting transfers between devices: 6.14 us -> 16.7 us  [shift(): lax.ppermute(v, 'expert', [(i, (i + n) % blocks) for i in range(blocks)])]
    ppermute x3 -> x0, waiting for transfers between devices: 10.1 us -> none  [dense_body(): lax.ppermute(v, 'expert', [(i, (i - n) % blocks) for i in range(blocks)])]
    pallas_call x7 -> x10, Pallas kernels: 50 us -> 43.9 us  [the longest x3 12.7 us: down(): pl.pallas_call(functools.partial(down_kernel, shards=shards, span=span, s...]
    ppermute x3 -> x0, starting transfers between devices: 4.7 us -> none  [dense_body(): lax.ppermute(v, 'expert', [(i, (i - n) % blocks) for i in range(blocks)])]
    ppermute x3 -> x9, waiting for transfers between devices: 11.5 us -> 16.1 us  [shift(): lax.ppermute(v, 'expert', [(i, (i + n) % blocks) for i in range(blocks)])]
    ppermute x9 -> x11, waiting for transfers between devices: 11.4 us -> 8.89 us  [swap(): return lax.ppermute(v, 'tensor', [(i, i ^ n) for i in range(shards)])]
    ppermute x9 -> x11, starting transfers between devices: 4.75 us -> 5.25 us  [swap(): return lax.ppermute(v, 'tensor', [(i, i ^ n) for i in range(shards)])]
  transfers between devices with their start and end apart: 15 -> 20, of which waited for: 5 -> 7; matrix products, arithmetic and copies ran while one was open for 0% -> 0% of each run, Pallas kernels for 36% -> 34%
where the time goes in v3:
time: 94.5 us; the launch traced here: 94.4 us
  Pallas kernels  47.1 us (50%)
  waiting for transfers between devices  25 us (26%)
  starting transfers between devices  22 us (23%)
    ppermute x9, starting transfers between devices, shift(): lax.ppermute(v, 'expert', [(i, (i + n) % blocks) for i in range(blocks)])  16.7 us
    ppermute x9, waiting for transfers between devices, shift(): lax.ppermute(v, 'expert', [(i, (i + n) % blocks) for i in range(blocks)])  16.1 us
    pallas_call x3, Pallas kernels, down(): pl.pallas_call(functools.partial(down_kernel, shards=shards, span=span, s...  12.7 us
    pallas_call x2, Pallas kernels, second(): pl.pallas_call(functools.partial(second_half_kernel, features=features, f...  11.8 us
    pallas_call x2, Pallas kernels, first(): pl.pallas_call(functools.partial(first_half_kernel, first=part * half), g...  10.5 us
    ppermute x11, waiting for transfers between devices, swap(): return lax.ppermute(v, 'tensor', [(i, i ^ n) for i in range(shards)])  8.89 us
    pallas_call x1, Pallas kernels, dense_body(): pl.pallas_call(fetch_kernel, grid_spec=pltpu.PrefetchScalarGridSpec(num_s...  8.83 us
    ppermute x11, starting transfers between devices, swap(): return lax.ppermute(v, 'tensor', [(i, i ^ n) for i in range(shards)])  5.25 us
  transfers between devices with their start and end apart: 20, of which 7 were waited for; matrix products, arithmetic and copies ran while one was open for 0% of the time, Pallas kernels for 34%

profile of v3, /device:TPU:0, one launch (start us, length us, event | category | flops | bytes accessed | tf_op | source)
XLA Modules:
  0.0 94.4 jit_solution(15815472366304186251)
XLA Ops:
  0.1 1.7 %pack.1.refs_0_ = bf16[72,1024]{1,0:T(8,128)(2,1)S(1)} custom-call(s32[5]{0:T(128)S(1)} %stack.23.where, bf16[64,1024]{1,0:T(8,128)(2,1)} %x_hbm.1, f32[1,4096]{1,0:T(1,128)} %bitcast.8, s32[8,64]{1,0:T(8,128)} %bitcast.9, f32[8,64]{1,0:T(8,128)} %bitcast.10), custom_call_target="tpu_custom_call" | custom-call | tf_op jit(solution)/shard_map/pack/pallas_call | solution.py:326
  1.8 3.1 %collective-permute-start = (bf16[72,1024]{1,0:T(8,128)(2,1)S(1)}, bf16[72,1024]{1,0:T(8,128)(2,1)S(1)}, u32[]{:S(2)}, u32[]{:S(2)}) collective-permute-start(bf16[72,1024]{1,0:T(8,128)(2,1)S(1)} %pack.1.refs_0_), channel_id=1, source_target_pairs={{0,4},{4,8},{8,12},{12,0},{1,5},{5,9},{9,13},{13,1},{2,6},{6,10},{... | collective-permute-start | bytes 442376 | tf_op jit(solution)/shard_map/ppermute | solution.py:353
  4.9 2.6 %collective-permute-start.1 = (bf16[72,1024]{1,0:T(8,128)(2,1)S(1)}, bf16[72,1024]{1,0:T(8,128)(2,1)S(1)}, u32[]{:S(2)}, u32[]{:S(2)}) collective-permute-start(bf16[72,1024]{1,0:T(8,128)(2,1)S(1)} %pack.1.refs_0_), channel_id=1, source_target_pairs={{0,8},{4,12},{8,0},{12,4},{1,9},{5,13},{9,1},{13,5},{2,10},{6,14},... | collective-permute-start | bytes 442376 | tf_op jit(solution)/shard_map/ppermute | solution.py:353
  7.5 1.3 %collective-permute-start.2 = (bf16[72,1024]{1,0:T(8,128)(2,1)S(1)}, bf16[72,1024]{1,0:T(8,128)(2,1)S(1)}, u32[]{:S(2)}, u32[]{:S(2)}) collective-permute-start(bf16[72,1024]{1,0:T(8,128)(2,1)S(1)} %pack.1.refs_0_), channel_id=1, source_target_pairs={{0,12},{4,0},{8,4},{12,8},{1,13},{5,1},{9,5},{13,9},{2,14},{6,2},{... | collective-permute-start | bytes 442376 | tf_op jit(solution)/shard_map/ppermute | solution.py:353
  8.8 2.9 %collective-permute-done.refs_1_.refs_0_ = bf16[72,1024]{1,0:T(8,128)(2,1)S(1)} collective-permute-done((bf16[72,1024]{1,0:T(8,128)(2,1)S(1)}, bf16[72,1024]{1,0:T(8,128)(2,1)S(1)}, u32[]{:S(2)}, u32[]{:S(2)}) %collective-permute-start) | collective-permute-done | bytes 147488 | tf_op jit(solution)/shard_map/ppermute | solution.py:353
  11.7 5.5 %collective-permute-done.1.refs_2_.refs_1_ = bf16[72,1024]{1,0:T(8,128)(2,1)S(1)} collective-permute-done((bf16[72,1024]{1,0:T(8,128)(2,1)S(1)}, bf16[72,1024]{1,0:T(8,128)(2,1)S(1)}, u32[]{:S(2)}, u32[]{:S(2)}) %collective-permute-start.1) | collective-permute-done | bytes 147488 | tf_op jit(solution)/shard_map/ppermute | solution.py:353
  17.4 1.5 %collective-permute-start.4 = (bf16[200,1024]{1,0:T(8,128)(2,1)S(1)}, bf16[200,1024]{1,0:T(8,128)(2,1)S(1)}, u32[]{:S(2)}, u32[]{:S(2)}) collective-permute-start(bf16[200,1024]{1,0:T(8,128)(2,1)S(1)} %shard_map.74), channel_id=1, source_target_pairs={{0,2},{1,3},{2,0},{3,1},{4,6},{5,7},{6,4},{7,5},{8,10},{9,11},{10,... | collective-permute-start | bytes 1228808 | tf_op jit(solution)/shard_map/ppermute | solution.py:356
  19.4 8.8 %fetch.1 = (bf16[8,2,192,2048]{3,2,1,0:T(8,128)(2,1)S(1)}, bf16[8,2,192,2048]{3,2,1,0:T(8,128)(2,1)S(1)}) custom-call(s32[5]{0:T(128)S(1)} %stack.23.where, bf16[16,192,4096]{2,1,0:T(8,128)(2,1)} %gate_hbm.5, bf16[16,192,4096]{2,1,0:T(8,128)(2,1)} %up_hbm.5), custom_call_target="tpu_custom_call" | custom-call | bytes 100663296 | tf_op jit(solution)/shard_map/fetch/pallas_call | solution.py:371
  28.3 0.8 route.1
  29.0 3.4 %collective-permute-done.6.near_own_ref = bf16[72,1024]{1,0:T(8,128)(2,1)S(1)} collective-permute-done((bf16[72,1024]{1,0:T(8,128)(2,1)S(1)}, bf16[72,1024]{1,0:T(8,128)(2,1)S(1)}, u32[]{:S(2)}, u32[]{:S(2)}) %collective-permute-start.6) | collective-permute-done | bytes 147488 | tf_op jit(solution)/shard_map/ppermute | solution.py:356
  33.0 5.2 %shard_map.77 = (f32[8,2,192,256]{3,2,1,0:T(8,128)S(1)}, bf16[8,2,192,2048]{3,2,1,0:T(8,128)(2,1)S(1)}) custom-call(s32[5]{0:T(128)S(1)} %stack.23.where, bf16[264,1024]{1,0:T(8,128)(2,1)S(1)} %shard_map.73.xa_ref, bf16[264,1024]{1,0:T(8,128)(2,1)S(1)} %collective-permute-done.3.xb_ref, bf16[8,2,192,2048]{3,2,1,0:T(8,128)(2,1)S(1)} %get-tuple-element.33.w_ref, ...), custom_call_target="tpu_custom_call" | custom-call | flops 3221225472 | bytes 25165824 | tf_op jit(solution)/shard_map/pallas_call | solution.py:413
  38.2 5.2 %shard_map.75 = (f32[8,2,192,256]{3,2,1,0:T(8,128)S(1)}, bf16[8,2,192,2048]{3,2,1,0:T(8,128)(2,1)S(1)}) custom-call(s32[5]{0:T(128)S(1)} %stack.23.where, bf16[264,1024]{1,0:T(8,128)(2,1)S(1)} %shard_map.73.xa_ref, bf16[264,1024]{1,0:T(8,128)(2,1)S(1)} %collective-permute-done.3.xb_ref, bf16[8,2,192,2048]{3,2,1,0:T(8,128)(2,1)S(1)} %get-tuple-element.26.w_ref, ...), custom_call_target="tpu_custom_call" | custom-call | flops 3221225472 | bytes 25165824 | tf_op jit(solution)/shard_map/pallas_call | solution.py:413
  43.4 5.9 %shard_map.78 = (bf16[4,192,128]{2,1,0:T(8,128)(2,1)S(1)}, bf16[8,1024,768]{2,1,0:T(8,128)(2,1)S(1)}) custom-call(s32[5]{0:T(128)S(1)} %stack.23.where, bf16[264,1024]{1,0:T(8,128)(2,1)S(1)} %shard_map.73.xa_ref, bf16[264,1024]{1,0:T(8,128)(2,1)S(1)} %collective-permute-done.3.xb_ref, bf16[200,1024]{1,0:T(8,128)(2,1)S(1)} %collective-permute-done.4.near_ref, ...), custom_call_target="tpu_custom_call" | custom-call | flops 3221225472 | bytes 25165824 | tf_op jit(solution)/shard_map/pallas_call | solution.py:441
  49.3 1.6 %collective-permute-start.12 = (bf16[4,192,128]{2,1,0:T(8,128)(2,1)S(1)}, bf16[4,192,128]{2,1,0:T(8,128)(2,1)S(1)}, u32[]{:S(2)}, u32[]{:S(2)}) collective-permute-start(bf16[4,192,128]{2,1,0:T(8,128)(2,1)S(1)} %get-tuple-element.36.refs_0_), channel_id=1, source_target_pairs={{0,2},{1,3},{2,0},{3,1},{4,6},{5,7},{6,4},{7,5},{8,10},{9,11},{10,... | collective-permute-start | bytes 589832 | tf_op jit(solution)/shard_map/ppermute | solution.py:356
  50.9 5.9 %shard_map.76 = (bf16[4,192,128]{2,1,0:T(8,128)(2,1)S(1)}, bf16[8,1024,768]{2,1,0:T(8,128)(2,1)S(1)}) custom-call(s32[5]{0:T(128)S(1)} %stack.23.where, bf16[264,1024]{1,0:T(8,128)(2,1)S(1)} %shard_map.73.xa_ref, bf16[264,1024]{1,0:T(8,128)(2,1)S(1)} %collective-permute-done.3.xb_ref, bf16[200,1024]{1,0:T(8,128)(2,1)S(1)} %collective-permute-done.4.near_ref, ...), custom_call_target="tpu_custom_call" | custom-call | flops 3221225472 | bytes 25165824 | tf_op jit(solution)/shard_map/pallas_call | solution.py:441
  57.9 5.5 %collective-permute-done.9.refs_2_ = bf16[4,192,128]{2,1,0:T(8,128)(2,1)S(1)} collective-permute-done((bf16[4,192,128]{2,1,0:T(8,128)(2,1)S(1)}, bf16[4,192,128]{2,1,0:T(8,128)(2,1)S(1)}, u32[]{:S(2)}, u32[]{:S(2)}) %collective-permute-start.9) | collective-permute-done | bytes 196640 | tf_op jit(solution)/shard_map/ppermute | solution.py:356
  63.4 5.7 %shard_map.79.refs_6_.refs_2_ = f32[256,1024]{1,0:T(8,128)S(1)} custom-call(s32[5]{0:T(128)S(1)} %stack.23.where, bf16[4,192,128]{2,1,0:T(8,128)(2,1)S(1)} %get-tuple-element.36.refs_0_, bf16[4,192,128]{2,1,0:T(8,128)(2,1)S(1)} %collective-permute-done.11.refs_1_, bf16[4,192,128]{2,1,0:T(8,128)(2,1)S(1)} %collective-permute-done.12.refs_2_, ...), custom_call_target="tpu_custom_call" | custom-call | flops 3221225472 | tf_op jit(solution)/shard_map/pallas_call | solution.py:483
  69.1 3.9 %shard_map.80 = (f32[64,512]{1,0:T(8,128)S(1)}, bf16[64,512]{1,0:T(8,128)(2,1)S(1)}, bf16[64,512]{1,0:T(8,128)(2,1)S(1)}, bf16[64,512]{1,0:T(8,128)(2,1)S(1)}, bf16[4,512,768]{2,1,0:T(8,128)(2,1)S(1)}) custom-call(s32[5]{0:T(128)S(1)} %stack.23.where, bf16[4,192,128]{2,1,0:T(8,128)(2,1)S(1)} %get-tuple-element.31.refs_0_, ...), custom_call_target="tpu_custom_call" | custom-call | flops 1610612736 | tf_op jit(solution)/shard_map/pallas_call | solution.py:483
  73.1 3.1 %shard_map.81 = (f32[64,512]{1,0:T(8,128)S(1)}, bf16[64,512]{1,0:T(8,128)(2,1)S(1)}, bf16[64,512]{1,0:T(8,128)(2,1)S(1)}, bf16[64,512]{1,0:T(8,128)(2,1)S(1)}) custom-call(s32[5]{0:T(128)S(1)} %stack.23.where, bf16[4,512,768]{2,1,0:T(8,128)(2,1)S(1)} %get-tuple-element.42.refs_0_, bf16[8,1024,768]{2,1,0:T(8,128)(2,1)S(1)} %get-tuple-element.32.refs_5_.refs_1_, ...), custom_call_target="tpu_custom_call" | custom-call | flops 1610612736 | tf_op jit(solution)/shard_map/pallas_call | solution.py:483
  76.1 4.7 %collective-permute-start.17 = (bf16[64,512]{1,0:T(8,128)(2,1)S(1)}, bf16[64,512]{1,0:T(8,128)(2,1)S(1)}, u32[]{:S(2)}, u32[]{:S(2)}) collective-permute-start(bf16[64,512]{1,0:T(8,128)(2,1)S(1)} %get-tuple-element.44), channel_id=1, source_target_pairs={{0,12},{4,0},{8,4},{12,8},{1,13},{5,1},{9,5},{13,9},{2,14},{6,2},{... | collective-permute-start | bytes 196616 | tf_op jit(solution)/shard_map/ppermute | solution.py:353
  81.5 3.6 %collective-permute-start.14 = (bf16[64,512]{1,0:T(8,128)(2,1)S(1)}, bf16[64,512]{1,0:T(8,128)(2,1)S(1)}, u32[]{:S(2)}, u32[]{:S(2)}) collective-permute-start(bf16[64,512]{1,0:T(8,128)(2,1)S(1)} %get-tuple-element.39), channel_id=1, source_target_pairs={{0,12},{4,0},{8,4},{12,8},{1,13},{5,1},{9,5},{13,9},{2,14},{6,2},{... | collective-permute-start | bytes 196616 | tf_op jit(solution)/shard_map/ppermute | solution.py:353
  85.8 3.1 %collective-permute-done.18.refs_6_ = bf16[64,512]{1,0:T(8,128)(2,1)S(1)} collective-permute-done((bf16[64,512]{1,0:T(8,128)(2,1)S(1)}, bf16[64,512]{1,0:T(8,128)(2,1)S(1)}, u32[]{:S(2)}, u32[]{:S(2)}) %collective-permute-start.18) | collective-permute-done | bytes 65568 | tf_op jit(solution)/shard_map/ppermute | solution.py:353
  89.1 4.5 %collective-permute-done.15.refs_2_ = bf16[64,512]{1,0:T(8,128)(2,1)S(1)} collective-permute-done((bf16[64,512]{1,0:T(8,128)(2,1)S(1)}, bf16[64,512]{1,0:T(8,128)(2,1)S(1)}, u32[]{:S(2)}, u32[]{:S(2)}) %collective-permute-start.15) | collective-permute-done | bytes 65568 | tf_op jit(solution)/shard_map/ppermute | solution.py:353
  93.6 0.7 finish.1
  (30 shorter events, 4.1 us)
Async XLA Ops:
  1.8 9.9 %collective-permute-start = (bf16[72,1024]{1,0:T(8,128)(2,1)S(1)}, bf16[72,1024]{1,0:T(8,128)(2,1)S(1)}, u32[]{:S(2)}, u32[]{:S(2)}) collective-permute-start(bf16[72,1024]{1,0:T(8,128)(2,1)S(1)} %pack.1.refs_0_), channel_id=1, source_target_pairs={{0,4},{4,8},{8,12},{12,0},{1,5},{5,9},{9,13},{13,1},{2,6},{6,10},{... | collective-permute-start | bytes 442376 | tf_op jit(solution)/shard_map/ppermute | solution.py:353
  4.9 12.3 %collective-permute-start.1 = (bf16[72,1024]{1,0:T(8,128)(2,1)S(1)}, bf16[72,1024]{1,0:T(8,128)(2,1)S(1)}, u32[]{:S(2)}, u32[]{:S(2)}) collective-permute-start(bf16[72,1024]{1,0:T(8,128)(2,1)S(1)} %pack.1.refs_0_), channel_id=1, source_target_pairs={{0,8},{4,12},{8,0},{12,4},{1,9},{5,13},{9,1},{13,5},{2,10},{6,14},... | collective-permute-start | bytes 442376 | tf_op jit(solution)/shard_map/ppermute | solution.py:353
  7.5 9.7 %collective-permute-start.2 = (bf16[72,1024]{1,0:T(8,128)(2,1)S(1)}, bf16[72,1024]{1,0:T(8,128)(2,1)S(1)}, u32[]{:S(2)}, u32[]{:S(2)}) collective-permute-start(bf16[72,1024]{1,0:T(8,128)(2,1)S(1)} %pack.1.refs_0_), channel_id=1, source_target_pairs={{0,12},{4,0},{8,4},{12,8},{1,13},{5,1},{9,5},{13,9},{2,14},{6,2},{... | collective-permute-start | bytes 442376 | tf_op jit(solution)/shard_map/ppermute | solution.py:353
  17.3 15.7 %collective-permute-start.3 = (bf16[264,1024]{1,0:T(8,128)(2,1)S(1)}, bf16[264,1024]{1,0:T(8,128)(2,1)S(1)}, u32[]{:S(2)}, u32[]{:S(2)}) collective-permute-start(bf16[264,1024]{1,0:T(8,128)(2,1)S(1)} %shard_map.73.xa_ref), channel_id=1, source_target_pairs={{0,1},{1,0},{2,3},{3,2},{4,5},{5,4},{6,7},{7,6},{8,9},{9,8},{10,11... | collective-permute-start | bytes 1622024 | tf_op jit(solution)/shard_map/ppermute | solution.py:356
  17.4 15.0 %collective-permute-start.4 = (bf16[200,1024]{1,0:T(8,128)(2,1)S(1)}, bf16[200,1024]{1,0:T(8,128)(2,1)S(1)}, u32[]{:S(2)}, u32[]{:S(2)}) collective-permute-start(bf16[200,1024]{1,0:T(8,128)(2,1)S(1)} %shard_map.74), channel_id=1, source_target_pairs={{0,2},{1,3},{2,0},{3,1},{4,6},{5,7},{6,4},{7,5},{8,10},{9,11},{10,... | collective-permute-start | bytes 1228808 | tf_op jit(solution)/shard_map/ppermute | solution.py:356
  18.9 13.5 %collective-permute-start.6 = (bf16[72,1024]{1,0:T(8,128)(2,1)S(1)}, bf16[72,1024]{1,0:T(8,128)(2,1)S(1)}, u32[]{:S(2)}, u32[]{:S(2)}) collective-permute-start(bf16[72,1024]{1,0:T(8,128)(2,1)S(1)} %pack.1.refs_0_), channel_id=1, source_target_pairs={{0,2},{1,3},{2,0},{3,1},{4,6},{5,7},{6,4},{7,5},{8,10},{9,11},{10,... | collective-permute-start | bytes 442376 | tf_op jit(solution)/shard_map/ppermute | solution.py:356
  32.4 11.0 %collective-permute-start.7 = (bf16[72,1024]{1,0:T(8,128)(2,1)S(1)}, bf16[72,1024]{1,0:T(8,128)(2,1)S(1)}, u32[]{:S(2)}, u32[]{:S(2)}) collective-permute-start(bf16[72,1024]{1,0:T(8,128)(2,1)S(1)} %collective-permute-done.6.near_own_ref), channel_id=1, source_target_pairs={{0,1},{1,0},{2,3},{3,2},{4,5},{5,4},{6,7},{7,6},{8,9},{9,8},{10,11... | collective-permute-start | bytes 442376 | tf_op jit(solution)/shard_map/ppermute | solution.py:356
  32.4 11.0 %collective-permute-start.5 = (bf16[200,1024]{1,0:T(8,128)(2,1)S(1)}, bf16[200,1024]{1,0:T(8,128)(2,1)S(1)}, u32[]{:S(2)}, u32[]{:S(2)}) collective-permute-start(bf16[200,1024]{1,0:T(8,128)(2,1)S(1)} %collective-permute-done.4.near_ref), channel_id=1, source_target_pairs={{0,1},{1,0},{2,3},{3,2},{4,5},{5,4},{6,7},{7,6},{8,9},{9,8},{10,11... | collective-permute-start | bytes 1228808 | tf_op jit(solution)/shard_map/ppermute | solution.py:356
  49.3 8.1 %collective-permute-start.12 = (bf16[4,192,128]{2,1,0:T(8,128)(2,1)S(1)}, bf16[4,192,128]{2,1,0:T(8,128)(2,1)S(1)}, u32[]{:S(2)}, u32[]{:S(2)}) collective-permute-start(bf16[4,192,128]{2,1,0:T(8,128)(2,1)S(1)} %get-tuple-element.36.refs_0_), channel_id=1, source_target_pairs={{0,2},{1,3},{2,0},{3,1},{4,6},{5,7},{6,4},{7,5},{8,10},{9,11},{10,... | collective-permute-start | bytes 589832 | tf_op jit(solution)/shard_map/ppermute | solution.py:356
  56.8 6.6 %collective-permute-start.9 = (bf16[4,192,128]{2,1,0:T(8,128)(2,1)S(1)}, bf16[4,192,128]{2,1,0:T(8,128)(2,1)S(1)}, u32[]{:S(2)}, u32[]{:S(2)}) collective-permute-start(bf16[4,192,128]{2,1,0:T(8,128)(2,1)S(1)} %get-tuple-element.31.refs_0_), channel_id=1, source_target_pairs={{0,2},{1,3},{2,0},{3,1},{4,6},{5,7},{6,4},{7,5},{8,10},{9,11},{10,... | collective-permute-start | bytes 589832 | tf_op jit(solution)/shard_map/ppermute | solution.py:356
  57.4 6.0 %collective-permute-start.11 = (bf16[4,192,128]{2,1,0:T(8,128)(2,1)S(1)}, bf16[4,192,128]{2,1,0:T(8,128)(2,1)S(1)}, u32[]{:S(2)}, u32[]{:S(2)}) collective-permute-start(bf16[4,192,128]{2,1,0:T(8,128)(2,1)S(1)} %get-tuple-element.36.refs_0_), channel_id=1, source_target_pairs={{0,1},{1,0},{2,3},{3,2},{4,5},{5,4},{6,7},{7,6},{8,9},{9,8},{10,11... | collective-permute-start | bytes 589832 | tf_op jit(solution)/shard_map/ppermute | solution.py:356
  57.4 6.0 %collective-permute-start.13 = (bf16[4,192,128]{2,1,0:T(8,128)(2,1)S(1)}, bf16[4,192,128]{2,1,0:T(8,128)(2,1)S(1)}, u32[]{:S(2)}, u32[]{:S(2)}) collective-permute-start(bf16[4,192,128]{2,1,0:T(8,128)(2,1)S(1)} %collective-permute-done.12.refs_2_), channel_id=1, source_target_pairs={{0,1},{1,0},{2,3},{3,2},{4,5},{5,4},{6,7},{7,6},{8,9},{9,8},{10,11... | collective-permute-start | bytes 589832 | tf_op jit(solution)/shard_map/ppermute | solution.py:356
  57.9 11.2 %collective-permute-start.8 = (bf16[4,192,128]{2,1,0:T(8,128)(2,1)S(1)}, bf16[4,192,128]{2,1,0:T(8,128)(2,1)S(1)}, u32[]{:S(2)}, u32[]{:S(2)}) collective-permute-start(bf16[4,192,128]{2,1,0:T(8,128)(2,1)S(1)} %get-tuple-element.31.refs_0_), channel_id=1, source_target_pairs={{0,1},{1,0},{2,3},{3,2},{4,5},{5,4},{6,7},{7,6},{8,9},{9,8},{10,11... | collective-permute-start | bytes 589832 | tf_op jit(solution)/shard_map/ppermute | solution.py:356
  63.4 5.7 %collective-permute-start.10 = (bf16[4,192,128]{2,1,0:T(8,128)(2,1)S(1)}, bf16[4,192,128]{2,1,0:T(8,128)(2,1)S(1)}, u32[]{:S(2)}, u32[]{:S(2)}) collective-permute-start(bf16[4,192,128]{2,1,0:T(8,128)(2,1)S(1)} %collective-permute-done.9.refs_2_), channel_id=1, source_target_pairs={{0,1},{1,0},{2,3},{3,2},{4,5},{5,4},{6,7},{7,6},{8,9},{9,8},{10,11... | collective-permute-start | bytes 589832 | tf_op jit(solution)/shard_map/ppermute | solution.py:356
  76.1 9.7 %collective-permute-start.17 = (bf16[64,512]{1,0:T(8,128)(2,1)S(1)}, bf16[64,512]{1,0:T(8,128)(2,1)S(1)}, u32[]{:S(2)}, u32[]{:S(2)}) collective-permute-start(bf16[64,512]{1,0:T(8,128)(2,1)S(1)} %get-tuple-element.44), channel_id=1, source_target_pairs={{0,12},{4,0},{8,4},{12,8},{1,13},{5,1},{9,5},{13,9},{2,14},{6,2},{... | collective-permute-start | bytes 196616 | tf_op jit(solution)/shard_map/ppermute | solution.py:353
  80.9 8.0 %collective-permute-start.18 = (bf16[64,512]{1,0:T(8,128)(2,1)S(1)}, bf16[64,512]{1,0:T(8,128)(2,1)S(1)}, u32[]{:S(2)}, u32[]{:S(2)}) collective-permute-start(bf16[64,512]{1,0:T(8,128)(2,1)S(1)} %get-tuple-element.45), channel_id=1, source_target_pairs={{0,8},{4,12},{8,0},{12,4},{1,9},{5,13},{9,1},{13,5},{2,10},{6,14},... | collective-permute-start | bytes 196616 | tf_op jit(solution)/shard_map/ppermute | solution.py:353
  81.3 7.6 %collective-permute-start.19 = (bf16[64,512]{1,0:T(8,128)(2,1)S(1)}, bf16[64,512]{1,0:T(8,128)(2,1)S(1)}, u32[]{:S(2)}, u32[]{:S(2)}) collective-permute-start(bf16[64,512]{1,0:T(8,128)(2,1)S(1)} %get-tuple-element.46), channel_id=1, source_target_pairs={{0,4},{4,8},{8,12},{12,0},{1,5},{5,9},{9,13},{13,1},{2,6},{6,10},{... | collective-permute-start | bytes 196616 | tf_op jit(solution)/shard_map/ppermute | solution.py:353
  81.5 7.6 %collective-permute-start.14 = (bf16[64,512]{1,0:T(8,128)(2,1)S(1)}, bf16[64,512]{1,0:T(8,128)(2,1)S(1)}, u32[]{:S(2)}, u32[]{:S(2)}) collective-permute-start(bf16[64,512]{1,0:T(8,128)(2,1)S(1)} %get-tuple-element.39), channel_id=1, source_target_pairs={{0,12},{4,0},{8,4},{12,8},{1,13},{5,1},{9,5},{13,9},{2,14},{6,2},{... | collective-permute-start | bytes 196616 | tf_op jit(solution)/shard_map/ppermute | solution.py:353
  85.1 8.5 %collective-permute-start.15 = (bf16[64,512]{1,0:T(8,128)(2,1)S(1)}, bf16[64,512]{1,0:T(8,128)(2,1)S(1)}, u32[]{:S(2)}, u32[]{:S(2)}) collective-permute-start(bf16[64,512]{1,0:T(8,128)(2,1)S(1)} %get-tuple-element.40), channel_id=1, source_target_pairs={{0,8},{4,12},{8,0},{12,4},{1,9},{5,13},{9,1},{13,5},{2,10},{6,14},... | collective-permute-start | bytes 196616 | tf_op jit(solution)/shard_map/ppermute | solution.py:353
  85.8 7.8 %collective-permute-start.16 = (bf16[64,512]{1,0:T(8,128)(2,1)S(1)}, bf16[64,512]{1,0:T(8,128)(2,1)S(1)}, u32[]{:S(2)}, u32[]{:S(2)}) collective-permute-start(bf16[64,512]{1,0:T(8,128)(2,1)S(1)} %get-tuple-element.41), channel_id=1, source_target_pairs={{0,4},{4,8},{8,12},{12,0},{1,5},{5,9},{9,13},{13,1},{2,6},{6,10},{... | collective-permute-start | bytes 196616 | tf_op jit(solution)/shard_map/ppermute | solution.py:353

commit v4 on v3

--- a/solution.py
+++ b/solution.py
@@ -163,11 +163,12 @@
         copy.wait()
 
 
-def first_half_kernel(
-    where, xa_ref, xb_ref, w_ref, gate_hbm, up_hbm, acc_ref, next_ref, x_all, sems, *, first
-):
+def first_half_kernel(where, xa_ref, xb_ref, w_ref, gate_hbm, up_hbm, *refs, first):
+    acc_ref, next_ref, x_all, sems = refs[-4:]
     step = pl.program_id(0)
-    copies = gate_up_copies(1 - where[0] // 2, first, (gate_hbm, up_hbm), next_ref, sems)
+    size = next_ref.shape[0] // 2
+    target = next_ref.at[pl.ds(first, size)]
+    copies = gate_up_copies(1 - where[0] // 2, first, (gate_hbm, up_hbm), target, sems)
     start_at_first_step(copies)
     tokens, width = x_all.shape[0], xa_ref.shape[1]
 
@@ -187,10 +188,15 @@
 
 def second_half_kernel(
     where, xa_ref, xb_ref, near_ref, far_ref, near_own_ref, far_own_ref, w_ref, acc_ref,
-    code_ref, weight_ref, down_hbm, out_ref, next_ref, x_all, inv_ref, sems, *, features, first,
+    code_ref, weight_ref, *refs, features,
 ):
+    *sources, out_ref, next_ref, x_all, inv_ref, sems = refs
     step = pl.program_id(0)
-    copies = down_copies(first, down_hbm, next_ref, sems)
+    if len(sources) > 1:
+        at = next_ref.shape[0]
+        copies = gate_up_copies(1 - where[0] // 2, at, sources, next_ref, sems)
+    else:
+        copies = down_copies(0, *sources, next_ref, sems)
     start_at_first_step(copies)
     tokens, width = x_all.shape[0], xa_ref.shape[1]
     rows = near_own_ref.shape[0] - 8
@@ -243,12 +249,18 @@
         (hidden_ref,) = take(1)
     (d_ref,) = take(1)
     before = take(0 if start else 1)
+    step = pl.program_id(0)
+    if start:
+        (down_hbm,), sems = take(1), refs.pop()
     outs = take(len(refs) - (2 if spread else 1))
+    if start:
+        next_ref = outs.pop()
+        copies = down_copies(next_ref.shape[0], down_hbm, next_ref, sems)
+        start_at_first_step(copies)
     if keep:
         kept_ref = outs.pop()
     own_ref, *send_refs = outs
     acc = refs[-1]
-    step = pl.program_id(0)
     pair = 2
     tokens = acc.shape[0]
     features = slice(*span)
@@ -285,18 +297,21 @@
         else:
             own_ref[...] = acc[...]
 
-
-def finish_kernel(*refs):
+    if start:
+        wait_at_last_step(copies)
+
+
+def finish_kernel(*refs, spans):
     *groups, out_ref = refs
-    spans = out_ref.shape[1] // groups[0].shape[1]
     each = len(groups) // spans
+    at = 0
     for n in range(spans):
         own_ref, *pieces = groups[n * each : (n + 1) * each]
         total = own_ref[...]
         for piece in pieces:
             total = total + piece[...].astype(jnp.float32)
-        width = own_ref.shape[1]
-        out_ref[:, n * width : (n + 1) * width] = total.astype(jnp.bfloat16)
+        out_ref[:, at : at + total.shape[1]] = total.astype(jnp.bfloat16)
+        at += total.shape[1]
 
 
 def params(limit=VMEM_BYTES):
@@ -409,13 +424,13 @@
         name="route",
     )(order, *pieces)
 
-    def first(part):
+    def first(part, *filling):
         return pl.pallas_call(
-            functools.partial(first_half_kernel, first=part * half),
+            functools.partial(first_half_kernel, first=part * half // 2),
             grid_spec=pltpu.PrefetchScalarGridSpec(
                 num_scalar_prefetch=1,
                 grid=(pairs,),
-                in_specs=[in_place] * 3 + [stay] * 2,
+                in_specs=[in_place] * 3 + [stay] * 2 + [in_place] * len(filling),
                 out_specs=[in_place] * 2,
                 scratch_shapes=[
                     pltpu.VMEM((count, features // 2), jnp.bfloat16),
@@ -426,24 +441,34 @@
                 pltpu.VMEM((half, 2, units, count), jnp.float32),
                 pltpu.VMEM(buffer, gate_proj.dtype),
             ],
-            compiler_params=params(6 << 20),
-            cost_estimate=fetched(2 * half * units * count * features, half_bytes),
-        )(order, in_vmem(xa), in_vmem(xb), in_vmem(weights[part]), gate_hbm, up_hbm)
-
-    partial = [first(part) for part in range(parts)]
+            compiler_params=params(7 << 20),
+            cost_estimate=fetched(2 * half * units * count * features, half_bytes // 2),
+            input_output_aliases={6: 1} if filling else {},
+        )(
+            order,
+            *[in_vmem(v) for v in (xa, xb, weights[part])],
+            gate_hbm,
+            up_hbm,
+            *[in_vmem(v) for v in filling],
+        )
+
+    acc0, filling = first(0)
+    acc1, second_weights = first(1, filling)
+    partial = [acc0, acc1]
     far = swap(near, 1)
     down_hbm = in_hbm(down_proj)
     down_buffer = (half, out_width, hidden_units)
 
-    def second(part):
-        acc, weights = partial[part]
+    def second(part, weights):
+        last = part == parts - 1
+        sources = [down_hbm] if last else [gate_hbm, up_hbm]
         routing = pl.BlockSpec((2, 1, count), lambda i, w: (i + part * pairs, 0, 0))
         return pl.pallas_call(
-            functools.partial(second_half_kernel, features=features, first=part * half),
+            functools.partial(second_half_kernel, features=features),
             grid_spec=pltpu.PrefetchScalarGridSpec(
                 num_scalar_prefetch=1,
                 grid=(pairs,),
-                in_specs=[in_place] * 8 + [routing] * 2 + [stay],
+                in_specs=[in_place] * 8 + [routing] * 2 + [stay] * len(sources),
                 out_specs=[pl.BlockSpec((1, units, slots), lambda i, w: (i, 0, 0)), in_place],
                 scratch_shapes=[
                     pltpu.VMEM((count, features // 2), jnp.bfloat16),
@@ -453,16 +478,16 @@
             ),
             out_shape=[
                 jax.ShapeDtypeStruct((pairs, units, slots), jnp.bfloat16),
-                pltpu.VMEM(down_buffer, down_proj.dtype),
+                pltpu.VMEM(down_buffer if last else buffer, down_proj.dtype),
             ],
-            compiler_params=params(6 << 20),
+            compiler_params=params(7 << 20),
             cost_estimate=fetched(2 * half * units * count * features, half_bytes),
         )(
             order,
-            *[in_vmem(v) for v in (xa, xb, near, far, near_own, far_own, weights, acc)],
+            *[in_vmem(v) for v in (xa, xb, near, far, near_own, far_own, weights, partial[part])],
             code,
             weight,
-            down_hbm,
+            *sources,
         )
 
     def down(part, pieces, down_local, before, span, keep, last):
@@ -475,11 +500,15 @@
             out_shape = [pltpu.VMEM((count, wide), jnp.float32)]
         if keep:
             out_shape += [pltpu.VMEM((pairs, 2 * count, hidden_units), jnp.bfloat16)]
+        if before is None:
+            out_shape += [pltpu.VMEM(down_buffer, down_proj.dtype)]
         routing = pl.BlockSpec((2, 1, count), lambda i, w: (i + part * pairs, 0, 0))
         moved = pl.BlockSpec((1, units, slots), lambda i, w: (i, 0, 0))
         scratch = [pltpu.VMEM((count, wide), jnp.float32)]
         if spread:
             scratch = [pltpu.VMEM((shards, units, slots), jnp.bfloat16)] + scratch
+        if before is None:
+            scratch += [pltpu.SemaphoreType.DMA((2,))]
         return pl.pallas_call(
             functools.partial(
                 down_kernel,
@@ -494,29 +523,30 @@
                 num_scalar_prefetch=1,
                 grid=(pairs,),
                 in_specs=([moved] * shards + [routing] if spread else [in_place])
-                + [in_place] * (1 if before is None else 2),
+                + [in_place] + [stay if before is None else in_place],
                 out_specs=[in_place] * len(out_shape),
                 scratch_shapes=scratch,
             ),
             out_shape=out_shape,
-            compiler_params=params(6 << 20),
+            compiler_params=params(7 << 20),
             cost_estimate=fetched(2 * half * count * wide * hidden_units, 0),
         )(
             order,
             *(list(pieces) + [code] if spread else [in_vmem(pieces[0])]),
             in_vmem(down_local),
-            *([] if before is None else [in_vmem(before)]),
-        )
-
-    def exchange(part):
-        mine, down_local = second(part)
+            down_hbm if before is None else in_vmem(before),
+        )
+
+    def exchange(part, weights):
+        mine, following = second(part, weights)
         across = swap(mine, 2)
         beside = swap(mine, 1)
-        return [mine, beside, across, swap(across, 1)], down_local
-
-    (total,) = down(0, *exchange(0), None, (0, out_width), False, False)
+        return [mine, beside, across, swap(across, 1)], following
+
+    pieces0, weights = exchange(0, second_weights)
+    pieces1, down_local = exchange(1, weights)
+    total, down_local = down(0, pieces0, down_local, None, (0, out_width), False, False)
     middle = out_width // 2
-    pieces1, down_local = exchange(1)
     *low, kept = down(1, pieces1, down_local, total, (0, middle), True, True)
     high = down(1, [kept], down_local, total, (middle, out_width), False, True)
 
@@ -526,7 +556,7 @@
     low = send_back(low[0], low[1:])
     high = send_back(high[0], high[1:])
     return pl.pallas_call(
-        finish_kernel,
+        functools.partial(finish_kernel, spans=2),
         out_shape=jax.ShapeDtypeStruct((rows, out_width), jnp.bfloat16),
         compiler_params=params(),
         name="finish",
@@ -599,6 +629,7 @@
         shards == 4
         and experts % 4 == 0
         and experts * blocks <= 256
+        and blocks == 4
         and blocks * rows <= 256
         and blocks * CAP * 2 <= 256
         and rows <= 128

time: 94.5 us -> 93.9 us (level)
  transfers between devices with their start and end apart: 20 -> 20, of which waited for: 7 -> 7; matrix products, arithmetic and copies ran while one was open for 0% -> 0% of each run, Pallas kernels for 34% -> 33%
where the time goes in v4:
time: 93.9 us; the launch traced here: 93.7 us
  Pallas kernels  46.5 us (50%)
  waiting for transfers between devices  25 us (27%)
  starting transfers between devices  22 us (23%)
    ppermute x9, starting transfers between devices, shift(): lax.ppermute(v, 'expert', [(i, (i + n) % blocks) for i in range(blocks)])  16.7 us
    ppermute x9, waiting for transfers between devices, shift(): lax.ppermute(v, 'expert', [(i, (i + n) % blocks) for i in range(blocks)])  16.1 us
    pallas_call x3, Pallas kernels, down(): pl.pallas_call(functools.partial(down_kernel, shards=shards, span=span, s...  12.7 us
    pallas_call x2, Pallas kernels, second(): pl.pallas_call(functools.partial(second_half_kernel, features=features),...  11.8 us
    pallas_call x2, Pallas kernels, first(): pl.pallas_call(functools.partial(first_half_kernel, first=part * half //...  9.76 us
    ppermute x11, waiting for transfers between devices, swap(): return lax.ppermute(v, 'tensor', [(i, i ^ n) for i in range(shards)])  8.91 us
    pallas_call x1, Pallas kernels, dense_body(): pl.pallas_call(fetch_kernel, grid_spec=pltpu.PrefetchScalarGridSpec(num_s...  8.83 us
    ppermute x11, starting transfers between devices, swap(): return lax.ppermute(v, 'tensor', [(i, i ^ n) for i in range(shards)])  5.25 us
  transfers between devices with their start and end apart: 20, of which 7 were waited for; matrix products, arithmetic and copies ran while one was open for 0% of the time, Pallas kernels for 33%

profile of v4, /device:TPU:0, one launch (start us, length us, event | category | flops | bytes accessed | tf_op | source)
XLA Modules:
  0.0 93.7 jit_solution(11424317752361040133)
XLA Ops:
  0.1 1.7 %pack.1.refs_0_ = bf16[72,1024]{1,0:T(8,128)(2,1)S(1)} custom-call(s32[5]{0:T(128)S(1)} %stack.23.where, bf16[64,1024]{1,0:T(8,128)(2,1)} %x_hbm.1, f32[1,4096]{1,0:T(1,128)} %bitcast.8, s32[8,64]{1,0:T(8,128)} %bitcast.9, f32[8,64]{1,0:T(8,128)} %bitcast.10), custom_call_target="tpu_custom_call" | custom-call | tf_op jit(solution)/shard_map/pack/pallas_call | solution.py:341
  1.8 3.1 %collective-permute-start = (bf16[72,1024]{1,0:T(8,128)(2,1)S(1)}, bf16[72,1024]{1,0:T(8,128)(2,1)S(1)}, u32[]{:S(2)}, u32[]{:S(2)}) collective-permute-start(bf16[72,1024]{1,0:T(8,128)(2,1)S(1)} %pack.1.refs_0_), channel_id=1, source_target_pairs={{0,4},{4,8},{8,12},{12,0},{1,5},{5,9},{9,13},{13,1},{2,6},{6,10},{... | collective-permute-start | bytes 442376 | tf_op jit(solution)/shard_map/ppermute | solution.py:368
  4.9 2.6 %collective-permute-start.1 = (bf16[72,1024]{1,0:T(8,128)(2,1)S(1)}, bf16[72,1024]{1,0:T(8,128)(2,1)S(1)}, u32[]{:S(2)}, u32[]{:S(2)}) collective-permute-start(bf16[72,1024]{1,0:T(8,128)(2,1)S(1)} %pack.1.refs_0_), channel_id=1, source_target_pairs={{0,8},{4,12},{8,0},{12,4},{1,9},{5,13},{9,1},{13,5},{2,10},{6,14},... | collective-permute-start | bytes 442376 | tf_op jit(solution)/shard_map/ppermute | solution.py:368
  7.5 1.3 %collective-permute-start.2 = (bf16[72,1024]{1,0:T(8,128)(2,1)S(1)}, bf16[72,1024]{1,0:T(8,128)(2,1)S(1)}, u32[]{:S(2)}, u32[]{:S(2)}) collective-permute-start(bf16[72,1024]{1,0:T(8,128)(2,1)S(1)} %pack.1.refs_0_), channel_id=1, source_target_pairs={{0,12},{4,0},{8,4},{12,8},{1,13},{5,1},{9,5},{13,9},{2,14},{6,2},{... | collective-permute-start | bytes 442376 | tf_op jit(solution)/shard_map/ppermute | solution.py:368
  8.8 2.9 %collective-permute-done.refs_1_.refs_0_ = bf16[72,1024]{1,0:T(8,128)(2,1)S(1)} collective-permute-done((bf16[72,1024]{1,0:T(8,128)(2,1)S(1)}, bf16[72,1024]{1,0:T(8,128)(2,1)S(1)}, u32[]{:S(2)}, u32[]{:S(2)}) %collective-permute-start) | collective-permute-done | bytes 147488 | tf_op jit(solution)/shard_map/ppermute | solution.py:368
  11.7 5.5 %collective-permute-done.1.refs_2_.refs_1_ = bf16[72,1024]{1,0:T(8,128)(2,1)S(1)} collective-permute-done((bf16[72,1024]{1,0:T(8,128)(2,1)S(1)}, bf16[72,1024]{1,0:T(8,128)(2,1)S(1)}, u32[]{:S(2)}, u32[]{:S(2)}) %collective-permute-start.1) | collective-permute-done | bytes 147488 | tf_op jit(solution)/shard_map/ppermute | solution.py:368
  17.4 1.5 %collective-permute-start.4 = (bf16[200,1024]{1,0:T(8,128)(2,1)S(1)}, bf16[200,1024]{1,0:T(8,128)(2,1)S(1)}, u32[]{:S(2)}, u32[]{:S(2)}) collective-permute-start(bf16[200,1024]{1,0:T(8,128)(2,1)S(1)} %shard_map.74), channel_id=1, source_target_pairs={{0,2},{1,3},{2,0},{3,1},{4,6},{5,7},{6,4},{7,5},{8,10},{9,11},{10,... | collective-permute-start | bytes 1228808 | tf_op jit(solution)/shard_map/ppermute | solution.py:371
  19.4 8.8 %fetch.1 = (bf16[8,2,192,2048]{3,2,1,0:T(8,128)(2,1)S(1)}, bf16[8,2,192,2048]{3,2,1,0:T(8,128)(2,1)S(1)}) custom-call(s32[5]{0:T(128)S(1)} %stack.23.where, bf16[16,192,4096]{2,1,0:T(8,128)(2,1)} %refs_0_.2, bf16[16,192,4096]{2,1,0:T(8,128)(2,1)} %refs_1_.1), custom_call_target="tpu_custom_call" | custom-call | bytes 100663296 | tf_op jit(solution)/shard_map/fetch/pallas_call | solution.py:386
  28.3 0.8 route.1
  29.0 3.4 %collective-permute-done.6.near_own_ref = bf16[72,1024]{1,0:T(8,128)(2,1)S(1)} collective-permute-done((bf16[72,1024]{1,0:T(8,128)(2,1)S(1)}, bf16[72,1024]{1,0:T(8,128)(2,1)S(1)}, u32[]{:S(2)}, u32[]{:S(2)}) %collective-permute-start.6) | collective-permute-done | bytes 147488 | tf_op jit(solution)/shard_map/ppermute | solution.py:371
  33.0 4.9 %shard_map.75 = (f32[8,2,192,256]{3,2,1,0:T(8,128)S(1)}, bf16[8,2,192,2048]{3,2,1,0:T(8,128)(2,1)S(1)}) custom-call(s32[5]{0:T(128)S(1)} %stack.23.where, bf16[264,1024]{1,0:T(8,128)(2,1)S(1)} %shard_map.73.xa_ref, bf16[264,1024]{1,0:T(8,128)(2,1)S(1)} %collective-permute-done.3.xb_ref, bf16[8,2,192,2048]{3,2,1,0:T(8,128)(2,1)S(1)} %get-tuple-element.29.w_ref, ...), custom_call_target="tpu_custom_call" | custom-call | flops 3221225472 | bytes 12582912 | tf_op jit(solution)/shard_map/pallas_call | solution.py:428
  37.8 4.9 %shard_map.76 = (f32[8,2,192,256]{3,2,1,0:T(8,128)S(1)}, bf16[8,2,192,2048]{3,2,1,0:T(8,128)(2,1)S(1)}) custom-call(s32[5]{0:T(128)S(1)} %stack.23.where, bf16[264,1024]{1,0:T(8,128)(2,1)S(1)} %shard_map.73.xa_ref, bf16[264,1024]{1,0:T(8,128)(2,1)S(1)} %collective-permute-done.3.xb_ref, ...), custom_call_target="tpu_custom_call", output_to_operand_aliasing={{1}: (6, {})} | custom-call | flops 3221225472 | bytes 12582912 | tf_op jit(solution)/shard_map/pallas_call | solution.py:428
  42.8 6.0 %shard_map.77 = (bf16[4,192,128]{2,1,0:T(8,128)(2,1)S(1)}, bf16[8,2,192,2048]{3,2,1,0:T(8,128)(2,1)S(1)}) custom-call(s32[5]{0:T(128)S(1)} %stack.23.where, bf16[264,1024]{1,0:T(8,128)(2,1)S(1)} %shard_map.73.xa_ref, bf16[264,1024]{1,0:T(8,128)(2,1)S(1)} %collective-permute-done.3.xb_ref, bf16[200,1024]{1,0:T(8,128)(2,1)S(1)} %collective-permute-done.4.near_ref, ...), custom_call_target="tpu_custom_call" | custom-call | flops 3221225472 | bytes 25165824 | tf_op jit(solution)/shard_map/pallas_call | solution.py:466
  48.7 1.5 %collective-permute-start.12 = (bf16[4,192,128]{2,1,0:T(8,128)(2,1)S(1)}, bf16[4,192,128]{2,1,0:T(8,128)(2,1)S(1)}, u32[]{:S(2)}, u32[]{:S(2)}) collective-permute-start(bf16[4,192,128]{2,1,0:T(8,128)(2,1)S(1)} %get-tuple-element.38.refs_0_), channel_id=1, source_target_pairs={{0,2},{1,3},{2,0},{3,1},{4,6},{5,7},{6,4},{7,5},{8,10},{9,11},{10,... | collective-permute-start | bytes 589832 | tf_op jit(solution)/shard_map/ppermute | solution.py:371
  50.3 5.9 %shard_map.78 = (bf16[4,192,128]{2,1,0:T(8,128)(2,1)S(1)}, bf16[8,1024,768]{2,1,0:T(8,128)(2,1)S(1)}) custom-call(s32[5]{0:T(128)S(1)} %stack.23.where, bf16[264,1024]{1,0:T(8,128)(2,1)S(1)} %shard_map.73.xa_ref, bf16[264,1024]{1,0:T(8,128)(2,1)S(1)} %collective-permute-done.3.xb_ref, bf16[200,1024]{1,0:T(8,128)(2,1)S(1)} %collective-permute-done.4.near_ref, ...), custom_call_target="tpu_custom_call" | custom-call | flops 3221225472 | bytes 25165824 | tf_op jit(solution)/shard_map/pallas_call | solution.py:466
  57.3 5.5 %collective-permute-done.9.refs_2_ = bf16[4,192,128]{2,1,0:T(8,128)(2,1)S(1)} collective-permute-done((bf16[4,192,128]{2,1,0:T(8,128)(2,1)S(1)}, bf16[4,192,128]{2,1,0:T(8,128)(2,1)S(1)}, u32[]{:S(2)}, u32[]{:S(2)}) %collective-permute-start.9) | collective-permute-done | bytes 196640 | tf_op jit(solution)/shard_map/ppermute | solution.py:371
  62.8 5.7 %shard_map.79 = (f32[256,1024]{1,0:T(8,128)S(1)}, bf16[8,1024,768]{2,1,0:T(8,128)(2,1)S(1)}) custom-call(s32[5]{0:T(128)S(1)} %stack.23.where, bf16[4,192,128]{2,1,0:T(8,128)(2,1)S(1)} %get-tuple-element.38.refs_0_, bf16[4,192,128]{2,1,0:T(8,128)(2,1)S(1)} %collective-permute-done.11.refs_1_, bf16[4,192,128]{2,1,0:T(8,128)(2,1)S(1)} %collective-permute-done.12.refs_2_, ...), custom_call_target="tpu_custom_call" | custom-call | flops 3221225472 | tf_op jit(solution)/shard_map/pallas_call | solution.py:512
  68.5 3.9 %shard_map.80 = (f32[64,512]{1,0:T(8,128)S(1)}, bf16[64,512]{1,0:T(8,128)(2,1)S(1)}, bf16[64,512]{1,0:T(8,128)(2,1)S(1)}, bf16[64,512]{1,0:T(8,128)(2,1)S(1)}, bf16[4,512,768]{2,1,0:T(8,128)(2,1)S(1)}) custom-call(s32[5]{0:T(128)S(1)} %stack.23.where, bf16[4,192,128]{2,1,0:T(8,128)(2,1)S(1)} %get-tuple-element.37.refs_0_, ...), custom_call_target="tpu_custom_call" | custom-call | flops 1610612736 | tf_op jit(solution)/shard_map/pallas_call | solution.py:512
  72.5 3.1 %shard_map.81 = (f32[64,512]{1,0:T(8,128)S(1)}, bf16[64,512]{1,0:T(8,128)(2,1)S(1)}, bf16[64,512]{1,0:T(8,128)(2,1)S(1)}, bf16[64,512]{1,0:T(8,128)(2,1)S(1)}) custom-call(s32[5]{0:T(128)S(1)} %stack.23.where, bf16[4,512,768]{2,1,0:T(8,128)(2,1)S(1)} %get-tuple-element.46.refs_0_, bf16[8,1024,768]{2,1,0:T(8,128)(2,1)S(1)} %get-tuple-element.40.refs_5_.refs_1_, ...), custom_call_target="tpu_custom_call" | custom-call | flops 1610612736 | tf_op jit(solution)/shard_map/pallas_call | solution.py:512
  75.5 4.7 %collective-permute-start.17 = (bf16[64,512]{1,0:T(8,128)(2,1)S(1)}, bf16[64,512]{1,0:T(8,128)(2,1)S(1)}, u32[]{:S(2)}, u32[]{:S(2)}) collective-permute-start(bf16[64,512]{1,0:T(8,128)(2,1)S(1)} %get-tuple-element.48), channel_id=1, source_target_pairs={{0,12},{4,0},{8,4},{12,8},{1,13},{5,1},{9,5},{13,9},{2,14},{6,2},{... | collective-permute-start | bytes 196616 | tf_op jit(solution)/shard_map/ppermute | solution.py:368
  80.9 3.6 %collective-permute-start.14 = (bf16[64,512]{1,0:T(8,128)(2,1)S(1)}, bf16[64,512]{1,0:T(8,128)(2,1)S(1)}, u32[]{:S(2)}, u32[]{:S(2)}) collective-permute-start(bf16[64,512]{1,0:T(8,128)(2,1)S(1)} %get-tuple-element.43), channel_id=1, source_target_pairs={{0,12},{4,0},{8,4},{12,8},{1,13},{5,1},{9,5},{13,9},{2,14},{6,2},{... | collective-permute-start | bytes 196616 | tf_op jit(solution)/shard_map/ppermute | solution.py:368
  84.5 0.8 collective-permute-start.15
  85.2 3.1 %collective-permute-done.18.refs_6_ = bf16[64,512]{1,0:T(8,128)(2,1)S(1)} collective-permute-done((bf16[64,512]{1,0:T(8,128)(2,1)S(1)}, bf16[64,512]{1,0:T(8,128)(2,1)S(1)}, u32[]{:S(2)}, u32[]{:S(2)}) %collective-permute-start.18) | collective-permute-done | bytes 65568 | tf_op jit(solution)/shard_map/ppermute | solution.py:368
  88.5 4.5 %collective-permute-done.15.refs_2_ = bf16[64,512]{1,0:T(8,128)(2,1)S(1)} collective-permute-done((bf16[64,512]{1,0:T(8,128)(2,1)S(1)}, bf16[64,512]{1,0:T(8,128)(2,1)S(1)}, u32[]{:S(2)}, u32[]{:S(2)}) %collective-permute-start.15) | collective-permute-done | bytes 65568 | tf_op jit(solution)/shard_map/ppermute | solution.py:368
  (30 shorter events, 4.1 us)
Async XLA Ops:
  1.8 9.9 %collective-permute-start = (bf16[72,1024]{1,0:T(8,128)(2,1)S(1)}, bf16[72,1024]{1,0:T(8,128)(2,1)S(1)}, u32[]{:S(2)}, u32[]{:S(2)}) collective-permute-start(bf16[72,1024]{1,0:T(8,128)(2,1)S(1)} %pack.1.refs_0_), channel_id=1, source_target_pairs={{0,4},{4,8},{8,12},{12,0},{1,5},{5,9},{9,13},{13,1},{2,6},{6,10},{... | collective-permute-start | bytes 442376 | tf_op jit(solution)/shard_map/ppermute | solution.py:368
  4.9 12.3 %collective-permute-start.1 = (bf16[72,1024]{1,0:T(8,128)(2,1)S(1)}, bf16[72,1024]{1,0:T(8,128)(2,1)S(1)}, u32[]{:S(2)}, u32[]{:S(2)}) collective-permute-start(bf16[72,1024]{1,0:T(8,128)(2,1)S(1)} %pack.1.refs_0_), channel_id=1, source_target_pairs={{0,8},{4,12},{8,0},{12,4},{1,9},{5,13},{9,1},{13,5},{2,10},{6,14},... | collective-permute-start | bytes 442376 | tf_op jit(solution)/shard_map/ppermute | solution.py:368
  7.5 9.7 %collective-permute-start.2 = (bf16[72,1024]{1,0:T(8,128)(2,1)S(1)}, bf16[72,1024]{1,0:T(8,128)(2,1)S(1)}, u32[]{:S(2)}, u32[]{:S(2)}) collective-permute-start(bf16[72,1024]{1,0:T(8,128)(2,1)S(1)} %pack.1.refs_0_), channel_id=1, source_target_pairs={{0,12},{4,0},{8,4},{12,8},{1,13},{5,1},{9,5},{13,9},{2,14},{6,2},{... | collective-permute-start | bytes 442376 | tf_op jit(solution)/shard_map/ppermute | solution.py:368
  17.3 15.7 %collective-permute-start.3 = (bf16[264,1024]{1,0:T(8,128)(2,1)S(1)}, bf16[264,1024]{1,0:T(8,128)(2,1)S(1)}, u32[]{:S(2)}, u32[]{:S(2)}) collective-permute-start(bf16[264,1024]{1,0:T(8,128)(2,1)S(1)} %shard_map.73.xa_ref), channel_id=1, source_target_pairs={{0,1},{1,0},{2,3},{3,2},{4,5},{5,4},{6,7},{7,6},{8,9},{9,8},{10,11... | collective-permute-start | bytes 1622024 | tf_op jit(solution)/shard_map/ppermute | solution.py:371
  17.4 15.0 %collective-permute-start.4 = (bf16[200,1024]{1,0:T(8,128)(2,1)S(1)}, bf16[200,1024]{1,0:T(8,128)(2,1)S(1)}, u32[]{:S(2)}, u32[]{:S(2)}) collective-permute-start(bf16[200,1024]{1,0:T(8,128)(2,1)S(1)} %shard_map.74), channel_id=1, source_target_pairs={{0,2},{1,3},{2,0},{3,1},{4,6},{5,7},{6,4},{7,5},{8,10},{9,11},{10,... | collective-permute-start | bytes 1228808 | tf_op jit(solution)/shard_map/ppermute | solution.py:371
  18.9 13.5 %collective-permute-start.6 = (bf16[72,1024]{1,0:T(8,128)(2,1)S(1)}, bf16[72,1024]{1,0:T(8,128)(2,1)S(1)}, u32[]{:S(2)}, u32[]{:S(2)}) collective-permute-start(bf16[72,1024]{1,0:T(8,128)(2,1)S(1)} %pack.1.refs_0_), channel_id=1, source_target_pairs={{0,2},{1,3},{2,0},{3,1},{4,6},{5,7},{6,4},{7,5},{8,10},{9,11},{10,... | collective-permute-start | bytes 442376 | tf_op jit(solution)/shard_map/ppermute | solution.py:371
  32.4 10.3 %collective-permute-start.7 = (bf16[72,1024]{1,0:T(8,128)(2,1)S(1)}, bf16[72,1024]{1,0:T(8,128)(2,1)S(1)}, u32[]{:S(2)}, u32[]{:S(2)}) collective-permute-start(bf16[72,1024]{1,0:T(8,128)(2,1)S(1)} %collective-permute-done.6.near_own_ref), channel_id=1, source_target_pairs={{0,1},{1,0},{2,3},{3,2},{4,5},{5,4},{6,7},{7,6},{8,9},{9,8},{10,11... | collective-permute-start | bytes 442376 | tf_op jit(solution)/shard_map/ppermute | solution.py:371
  32.4 10.3 %collective-permute-start.5 = (bf16[200,1024]{1,0:T(8,128)(2,1)S(1)}, bf16[200,1024]{1,0:T(8,128)(2,1)S(1)}, u32[]{:S(2)}, u32[]{:S(2)}) collective-permute-start(bf16[200,1024]{1,0:T(8,128)(2,1)S(1)} %collective-permute-done.4.near_ref), channel_id=1, source_target_pairs={{0,1},{1,0},{2,3},{3,2},{4,5},{5,4},{6,7},{7,6},{8,9},{9,8},{10,11... | collective-permute-start | bytes 1228808 | tf_op jit(solution)/shard_map/ppermute | solution.py:371
  48.7 8.1 %collective-permute-start.12 = (bf16[4,192,128]{2,1,0:T(8,128)(2,1)S(1)}, bf16[4,192,128]{2,1,0:T(8,128)(2,1)S(1)}, u32[]{:S(2)}, u32[]{:S(2)}) collective-permute-start(bf16[4,192,128]{2,1,0:T(8,128)(2,1)S(1)} %get-tuple-element.38.refs_0_), channel_id=1, source_target_pairs={{0,2},{1,3},{2,0},{3,1},{4,6},{5,7},{6,4},{7,5},{8,10},{9,11},{10,... | collective-permute-start | bytes 589832 | tf_op jit(solution)/shard_map/ppermute | solution.py:371
  56.2 6.6 %collective-permute-start.9 = (bf16[4,192,128]{2,1,0:T(8,128)(2,1)S(1)}, bf16[4,192,128]{2,1,0:T(8,128)(2,1)S(1)}, u32[]{:S(2)}, u32[]{:S(2)}) collective-permute-start(bf16[4,192,128]{2,1,0:T(8,128)(2,1)S(1)} %get-tuple-element.37.refs_0_), channel_id=1, source_target_pairs={{0,2},{1,3},{2,0},{3,1},{4,6},{5,7},{6,4},{7,5},{8,10},{9,11},{10,... | collective-permute-start | bytes 589832 | tf_op jit(solution)/shard_map/ppermute | solution.py:371
  56.8 6.0 %collective-permute-start.11 = (bf16[4,192,128]{2,1,0:T(8,128)(2,1)S(1)}, bf16[4,192,128]{2,1,0:T(8,128)(2,1)S(1)}, u32[]{:S(2)}, u32[]{:S(2)}) collective-permute-start(bf16[4,192,128]{2,1,0:T(8,128)(2,1)S(1)} %get-tuple-element.38.refs_0_), channel_id=1, source_target_pairs={{0,1},{1,0},{2,3},{3,2},{4,5},{5,4},{6,7},{7,6},{8,9},{9,8},{10,11... | collective-permute-start | bytes 589832 | tf_op jit(solution)/shard_map/ppermute | solution.py:371
  56.8 6.0 %collective-permute-start.13 = (bf16[4,192,128]{2,1,0:T(8,128)(2,1)S(1)}, bf16[4,192,128]{2,1,0:T(8,128)(2,1)S(1)}, u32[]{:S(2)}, u32[]{:S(2)}) collective-permute-start(bf16[4,192,128]{2,1,0:T(8,128)(2,1)S(1)} %collective-permute-done.12.refs_2_), channel_id=1, source_target_pairs={{0,1},{1,0},{2,3},{3,2},{4,5},{5,4},{6,7},{7,6},{8,9},{9,8},{10,11... | collective-permute-start | bytes 589832 | tf_op jit(solution)/shard_map/ppermute | solution.py:371
  57.3 11.2 %collective-permute-start.8 = (bf16[4,192,128]{2,1,0:T(8,128)(2,1)S(1)}, bf16[4,192,128]{2,1,0:T(8,128)(2,1)S(1)}, u32[]{:S(2)}, u32[]{:S(2)}) collective-permute-start(bf16[4,192,128]{2,1,0:T(8,128)(2,1)S(1)} %get-tuple-element.37.refs_0_), channel_id=1, source_target_pairs={{0,1},{1,0},{2,3},{3,2},{4,5},{5,4},{6,7},{7,6},{8,9},{9,8},{10,11... | collective-permute-start | bytes 589832 | tf_op jit(solution)/shard_map/ppermute | solution.py:371
  62.8 5.7 %collective-permute-start.10 = (bf16[4,192,128]{2,1,0:T(8,128)(2,1)S(1)}, bf16[4,192,128]{2,1,0:T(8,128)(2,1)S(1)}, u32[]{:S(2)}, u32[]{:S(2)}) collective-permute-start(bf16[4,192,128]{2,1,0:T(8,128)(2,1)S(1)} %collective-permute-done.9.refs_2_), channel_id=1, source_target_pairs={{0,1},{1,0},{2,3},{3,2},{4,5},{5,4},{6,7},{7,6},{8,9},{9,8},{10,11... | collective-permute-start | bytes 589832 | tf_op jit(solution)/shard_map/ppermute | solution.py:371
  75.5 9.7 %collective-permute-start.17 = (bf16[64,512]{1,0:T(8,128)(2,1)S(1)}, bf16[64,512]{1,0:T(8,128)(2,1)S(1)}, u32[]{:S(2)}, u32[]{:S(2)}) collective-permute-start(bf16[64,512]{1,0:T(8,128)(2,1)S(1)} %get-tuple-element.48), channel_id=1, source_target_pairs={{0,12},{4,0},{8,4},{12,8},{1,13},{5,1},{9,5},{13,9},{2,14},{6,2},{... | collective-permute-start | bytes 196616 | tf_op jit(solution)/shard_map/ppermute | solution.py:368
  80.3 8.0 %collective-permute-start.18 = (bf16[64,512]{1,0:T(8,128)(2,1)S(1)}, bf16[64,512]{1,0:T(8,128)(2,1)S(1)}, u32[]{:S(2)}, u32[]{:S(2)}) collective-permute-start(bf16[64,512]{1,0:T(8,128)(2,1)S(1)} %get-tuple-element.49), channel_id=1, source_target_pairs={{0,8},{4,12},{8,0},{12,4},{1,9},{5,13},{9,1},{13,5},{2,10},{6,14},... | collective-permute-start | bytes 196616 | tf_op jit(solution)/shard_map/ppermute | solution.py:368
  80.7 7.7 %collective-permute-start.19 = (bf16[64,512]{1,0:T(8,128)(2,1)S(1)}, bf16[64,512]{1,0:T(8,128)(2,1)S(1)}, u32[]{:S(2)}, u32[]{:S(2)}) collective-permute-start(bf16[64,512]{1,0:T(8,128)(2,1)S(1)} %get-tuple-element.50), channel_id=1, source_target_pairs={{0,4},{4,8},{8,12},{12,0},{1,5},{5,9},{9,13},{13,1},{2,6},{6,10},{... | collective-permute-start | bytes 196616 | tf_op jit(solution)/shard_map/ppermute | solution.py:368
  80.9 7.6 %collective-permute-start.14 = (bf16[64,512]{1,0:T(8,128)(2,1)S(1)}, bf16[64,512]{1,0:T(8,128)(2,1)S(1)}, u32[]{:S(2)}, u32[]{:S(2)}) collective-permute-start(bf16[64,512]{1,0:T(8,128)(2,1)S(1)} %get-tuple-element.43), channel_id=1, source_target_pairs={{0,12},{4,0},{8,4},{12,8},{1,13},{5,1},{9,5},{13,9},{2,14},{6,2},{... | collective-permute-start | bytes 196616 | tf_op jit(solution)/shard_map/ppermute | solution.py:368
  84.5 8.5 %collective-permute-start.15 = (bf16[64,512]{1,0:T(8,128)(2,1)S(1)}, bf16[64,512]{1,0:T(8,128)(2,1)S(1)}, u32[]{:S(2)}, u32[]{:S(2)}) collective-permute-start(bf16[64,512]{1,0:T(8,128)(2,1)S(1)} %get-tuple-element.44), channel_id=1, source_target_pairs={{0,8},{4,12},{8,0},{12,4},{1,9},{5,13},{9,1},{13,5},{2,10},{6,14},... | collective-permute-start | bytes 196616 | tf_op jit(solution)/shard_map/ppermute | solution.py:368
  85.2 7.8 %collective-permute-start.16 = (bf16[64,512]{1,0:T(8,128)(2,1)S(1)}, bf16[64,512]{1,0:T(8,128)(2,1)S(1)}, u32[]{:S(2)}, u32[]{:S(2)}) collective-permute-start(bf16[64,512]{1,0:T(8,128)(2,1)S(1)} %get-tuple-element.45), channel_id=1, source_target_pairs={{0,4},{4,8},{8,12},{12,0},{1,5},{5,9},{9,13},{13,1},{2,6},{6,10},{... | collective-permute-start | bytes 196616 | tf_op jit(solution)/shard_map/ppermute | solution.py:368

commit v5 on v4

--- a/solution.py
+++ b/solution.py
@@ -179,10 +179,11 @@
             x_all[:, pl.ds(at, width)] = x_ref[:tokens, :]
 
     pair = 2
-    _, kinds, units, depth = w_ref.shape
-    weights = w_ref[pl.ds(step * pair, pair)].reshape(pair * kinds * units, depth)
-    acc = dot_rows(weights, x_all[...])
-    acc_ref[pl.ds(step * pair, pair)] = acc.reshape(pair, kinds, units, tokens)
+    experts, kinds, units, depth = w_ref.shape
+    for e in range(0, experts, pair):
+        weights = w_ref[e : e + pair].reshape(pair * kinds * units, depth)
+        acc = dot_rows(weights, x_all[...])
+        acc_ref[e : e + pair] = acc.reshape(pair, kinds, units, tokens)
     wait_at_last_step(copies)
 
 
@@ -190,7 +191,7 @@
     where, xa_ref, xb_ref, near_ref, far_ref, near_own_ref, far_own_ref, w_ref, acc_ref,
     code_ref, weight_ref, *refs, features,
 ):
-    *sources, out_ref, next_ref, x_all, inv_ref, sems = refs
+    *sources, out_ref, next_ref, x_all, inv_ref, raw, sems = refs
     step = pl.program_id(0)
     if len(sources) > 1:
         at = next_ref.shape[0]
@@ -224,19 +225,30 @@
     pair = 2
     _, kinds, units, depth = w_ref.shape
     slots = out_ref.shape[2]
-    mine = pl.ds(step * pair, pair)
-    weights = w_ref[mine].reshape(pair * kinds * units, depth)
-    acc = acc_ref[mine].reshape(pair * kinds * units, tokens)
-    acc = (acc + dot_rows(weights, x_all[...])) * inv_ref[...]
-    packed = jnp.zeros((units, slots), jnp.float32)
-    for n in range(pair):
-        gate = acc[(2 * n) * units : (2 * n + 1) * units]
-        up = acc[(2 * n + 1) * units : (2 * n + 2) * units]
-        hidden = gate / (1.0 + jnp.exp(-gate)) * up * weight_ref[n]
-        packed = packed + dot_rows(
-            hidden.astype(jnp.bfloat16), one_hot(code_ref[n], slots).astype(jnp.bfloat16)
-        )
-    out_ref[0] = packed.astype(jnp.bfloat16)
+
+    def finish_pair(n, slot):
+        acc = raw[slot] * inv_ref[...]
+        packed = jnp.zeros((units, slots), jnp.float32)
+        for m in range(pair):
+            gate = acc[(2 * m) * units : (2 * m + 1) * units]
+            up = acc[(2 * m + 1) * units : (2 * m + 2) * units]
+            hidden = gate / (1.0 + jnp.exp(-gate)) * up * weight_ref[pair * n + m]
+            packed = packed + dot_rows(
+                hidden.astype(jnp.bfloat16),
+                one_hot(code_ref[pair * n + m], slots).astype(jnp.bfloat16),
+            )
+        out_ref[n] = packed.astype(jnp.bfloat16)
+
+    pairs = raw.shape[0]
+    at = step * pairs
+    for n in range(pairs + 1):
+        if n < pairs:
+            mine = pl.ds((at + n) * pair, pair)
+            weights = w_ref[mine].reshape(pair * kinds * units, depth)
+            acc = acc_ref[mine].reshape(pair * kinds * units, tokens)
+            raw[n] = acc + dot_rows(weights, x_all[...])
+        if n > 0:
+            finish_pair(at + n - 1, n - 1)
     wait_at_last_step(copies)
 
 
@@ -269,23 +281,25 @@
     def _():
         acc[...] = jnp.zeros_like(acc) if start else before[0][:, features]
 
-    if spread:
-        joined = refs[0]
-        units, slots = joined.shape[1:]
-        for n, piece in enumerate(pieces):
-            joined[where[n]] = piece[0]
-        packed = joined[...].reshape(shards * units, slots)
-        places = [one_hot(code_ref[n], slots).T for n in range(pair)]
-        places = jnp.concatenate(places, axis=0).astype(jnp.bfloat16)
-        hidden = dot_rows(places, packed).astype(jnp.bfloat16)
-        if keep:
-            kept_ref[step] = hidden
-    else:
-        hidden = hidden_ref[step]
-    for n in range(pair):
-        acc[...] += dot_rows(
-            hidden[n * tokens : (n + 1) * tokens], d_ref[step * pair + n, features, :]
-        )
+    groups = 2
+    hidden = []
+    for g in range(groups):
+        if spread:
+            joined = refs[0]
+            units, slots = joined.shape[2:]
+            for n, piece in enumerate(pieces):
+                joined[g, where[n]] = piece[g]
+            packed = joined[g].reshape(shards * units, slots)
+            places = [one_hot(code_ref[pair * g + n], slots).T for n in range(pair)]
+            places = jnp.concatenate(places, axis=0).astype(jnp.bfloat16)
+            both = dot_rows(places, packed).astype(jnp.bfloat16)
+            if keep:
+                kept_ref[step * groups + g] = both
+        else:
+            both = hidden_ref[step * groups + g]
+        hidden += [both[n * tokens : (n + 1) * tokens] for n in range(pair)]
+    weights = [d_ref[step * pair * groups + n, features, :] for n in range(pair * groups)]
+    acc[...] += dot_rows(jnp.concatenate(hidden, axis=1), jnp.concatenate(weights, axis=1))
 
     @pl.when(step == pl.num_programs(0) - 1)
     def _():
@@ -429,7 +443,7 @@
             functools.partial(first_half_kernel, first=part * half // 2),
             grid_spec=pltpu.PrefetchScalarGridSpec(
                 num_scalar_prefetch=1,
-                grid=(pairs,),
+                grid=(1,),
                 in_specs=[in_place] * 3 + [stay] * 2 + [in_place] * len(filling),
                 out_specs=[in_place] * 2,
                 scratch_shapes=[
@@ -441,7 +455,7 @@
                 pltpu.VMEM((half, 2, units, count), jnp.float32),
                 pltpu.VMEM(buffer, gate_proj.dtype),
             ],
-            compiler_params=params(7 << 20),
+            compiler_params=params(10 << 20),
             cost_estimate=fetched(2 * half * units * count * features, half_bytes // 2),
             input_output_aliases={6: 1} if filling else {},
         )(
@@ -462,17 +476,18 @@
     def second(part, weights):
         last = part == parts - 1
         sources = [down_hbm] if last else [gate_hbm, up_hbm]
-        routing = pl.BlockSpec((2, 1, count), lambda i, w: (i + part * pairs, 0, 0))
+        routing = pl.BlockSpec((half, 1, count), lambda i, w: (part, 0, 0))
         return pl.pallas_call(
             functools.partial(second_half_kernel, features=features),
             grid_spec=pltpu.PrefetchScalarGridSpec(
                 num_scalar_prefetch=1,
-                grid=(pairs,),
+                grid=(pairs // 2,),
                 in_specs=[in_place] * 8 + [routing] * 2 + [stay] * len(sources),
-                out_specs=[pl.BlockSpec((1, units, slots), lambda i, w: (i, 0, 0)), in_place],
+                out_specs=[whole((pairs, units, slots)), in_place],
                 scratch_shapes=[
                     pltpu.VMEM((count, features // 2), jnp.bfloat16),
                     pltpu.VMEM((1, count), jnp.float32),
+                    pltpu.VMEM((2, 4 * units, count), jnp.float32),
                     pltpu.SemaphoreType.DMA((2,)),
                 ],
             ),
@@ -480,7 +495,7 @@
                 jax.ShapeDtypeStruct((pairs, units, slots), jnp.bfloat16),
                 pltpu.VMEM(down_buffer if last else buffer, down_proj.dtype),
             ],
-            compiler_params=params(7 << 20),
+            compiler_params=params(10 << 20),
             cost_estimate=fetched(2 * half * units * count * features, half_bytes),
         )(
             order,
@@ -502,11 +517,12 @@
             out_shape += [pltpu.VMEM((pairs, 2 * count, hidden_units), jnp.bfloat16)]
         if before is None:
             out_shape += [pltpu.VMEM(down_buffer, down_proj.dtype)]
-        routing = pl.BlockSpec((2, 1, count), lambda i, w: (i + part * pairs, 0, 0))
-        moved = pl.BlockSpec((1, units, slots), lambda i, w: (i, 0, 0))
+        steps = pairs // 2
+        routing = pl.BlockSpec((4, 1, count), lambda i, w: (i + part * steps, 0, 0))
+        moved = pl.BlockSpec((2, units, slots), lambda i, w: (i, 0, 0))
         scratch = [pltpu.VMEM((count, wide), jnp.float32)]
         if spread:
-            scratch = [pltpu.VMEM((shards, units, slots), jnp.bfloat16)] + scratch
+            scratch = [pltpu.VMEM((2, shards, units, slots), jnp.bfloat16)] + scratch
         if before is None:
             scratch += [pltpu.SemaphoreType.DMA((2,))]
         return pl.pallas_call(
@@ -521,14 +537,14 @@
             ),
             grid_spec=pltpu.PrefetchScalarGridSpec(
                 num_scalar_prefetch=1,
-                grid=(pairs,),
+                grid=(steps,),
                 in_specs=([moved] * shards + [routing] if spread else [in_place])
                 + [in_place] + [stay if before is None else in_place],
                 out_specs=[in_place] * len(out_shape),
                 scratch_shapes=scratch,
             ),
             out_shape=out_shape,
-            compiler_params=params(7 << 20),
+            compiler_params=params(10 << 20),
             cost_estimate=fetched(2 * half * count * wide * hidden_units, 0),
         )(
             order,
@@ -627,7 +643,7 @@
     experts = gate_proj.shape[0]
     fits = (
         shards == 4
-        and experts % 4 == 0
+        and experts % 8 == 0
         and experts * blocks <= 256
         and blocks == 4
         and blocks * rows <= 256

time: 93.9 us -> 90 us (0.958)
  Pallas kernels: 46.5 us -> 42.6 us
    pallas_call x2, Pallas kernels: 9.76 us -> 8.27 us  [first(): pl.pallas_call(functools.partial(first_half_kernel, first=part * half //...]
    pallas_call x3, Pallas kernels: 12.7 us -> 11.4 us  [down(): pl.pallas_call(functools.partial(down_kernel, shards=shards, span=span, s...]
    pallas_call x2, Pallas kernels: 11.8 us -> 10.7 us  [second(): pl.pallas_call(functools.partial(second_half_kernel, features=features),...]
  transfers between devices with their start and end apart: 20 -> 20, of which waited for: 7 -> 7; matrix products, arithmetic and copies ran while one was open for 0% -> 0% of each run, Pallas kernels for 33% -> 32%
where the time goes in v5:
time: 90 us; the launch traced here: 89.9 us
  Pallas kernels  42.6 us (47%)
  waiting for transfers between devices  25 us (28%)
  starting transfers between devices  22 us (24%)
    ppermute x9, starting transfers between devices, shift(): lax.ppermute(v, 'expert', [(i, (i + n) % blocks) for i in range(blocks)])  16.7 us
    ppermute x9, waiting for transfers between devices, shift(): lax.ppermute(v, 'expert', [(i, (i + n) % blocks) for i in range(blocks)])  16.1 us
    pallas_call x3, Pallas kernels, down(): pl.pallas_call(functools.partial(down_kernel, shards=shards, span=span, s...  11.4 us
    pallas_call x2, Pallas kernels, second(): pl.pallas_call(functools.partial(second_half_kernel, features=features),...  10.7 us
    ppermute x11, waiting for transfers between devices, swap(): return lax.ppermute(v, 'tensor', [(i, i ^ n) for i in range(shards)])  8.9 us
    pallas_call x1, Pallas kernels, dense_body(): pl.pallas_call(fetch_kernel, grid_spec=pltpu.PrefetchScalarGridSpec(num_s...  8.83 us
    pallas_call x2, Pallas kernels, first(): pl.pallas_call(functools.partial(first_half_kernel, first=part * half //...  8.27 us
    ppermute x11, starting transfers between devices, swap(): return lax.ppermute(v, 'tensor', [(i, i ^ n) for i in range(shards)])  5.25 us
  transfers between devices with their start and end apart: 20, of which 7 were waited for; matrix products, arithmetic and copies ran while one was open for 0% of the time, Pallas kernels for 32%

profile of v5, /device:TPU:0, one launch (start us, length us, event | category | flops | bytes accessed | tf_op | source)
XLA Modules:
  0.0 89.9 jit_solution(4571655606812006712)
XLA Ops:
  0.1 1.7 %pack.1.refs_0_ = bf16[72,1024]{1,0:T(8,128)(2,1)S(1)} custom-call(s32[5]{0:T(128)S(1)} %stack.23.where, bf16[64,1024]{1,0:T(8,128)(2,1)} %x_hbm.1, f32[1,4096]{1,0:T(1,128)} %bitcast.8, s32[8,64]{1,0:T(8,128)} %bitcast.9, f32[8,64]{1,0:T(8,128)} %bitcast.10), custom_call_target="tpu_custom_call" | custom-call | tf_op jit(solution)/shard_map/pack/pallas_call | solution.py:355
  1.8 3.1 %collective-permute-start = (bf16[72,1024]{1,0:T(8,128)(2,1)S(1)}, bf16[72,1024]{1,0:T(8,128)(2,1)S(1)}, u32[]{:S(2)}, u32[]{:S(2)}) collective-permute-start(bf16[72,1024]{1,0:T(8,128)(2,1)S(1)} %pack.1.refs_0_), channel_id=1, source_target_pairs={{0,4},{4,8},{8,12},{12,0},{1,5},{5,9},{9,13},{13,1},{2,6},{6,10},{... | collective-permute-start | bytes 442376 | tf_op jit(solution)/shard_map/ppermute | solution.py:382
  4.9 2.6 %collective-permute-start.1 = (bf16[72,1024]{1,0:T(8,128)(2,1)S(1)}, bf16[72,1024]{1,0:T(8,128)(2,1)S(1)}, u32[]{:S(2)}, u32[]{:S(2)}) collective-permute-start(bf16[72,1024]{1,0:T(8,128)(2,1)S(1)} %pack.1.refs_0_), channel_id=1, source_target_pairs={{0,8},{4,12},{8,0},{12,4},{1,9},{5,13},{9,1},{13,5},{2,10},{6,14},... | collective-permute-start | bytes 442376 | tf_op jit(solution)/shard_map/ppermute | solution.py:382
  7.5 1.3 %collective-permute-start.2 = (bf16[72,1024]{1,0:T(8,128)(2,1)S(1)}, bf16[72,1024]{1,0:T(8,128)(2,1)S(1)}, u32[]{:S(2)}, u32[]{:S(2)}) collective-permute-start(bf16[72,1024]{1,0:T(8,128)(2,1)S(1)} %pack.1.refs_0_), channel_id=1, source_target_pairs={{0,12},{4,0},{8,4},{12,8},{1,13},{5,1},{9,5},{13,9},{2,14},{6,2},{... | collective-permute-start | bytes 442376 | tf_op jit(solution)/shard_map/ppermute | solution.py:382
  8.8 2.9 %collective-permute-done.refs_1_.refs_0_ = bf16[72,1024]{1,0:T(8,128)(2,1)S(1)} collective-permute-done((bf16[72,1024]{1,0:T(8,128)(2,1)S(1)}, bf16[72,1024]{1,0:T(8,128)(2,1)S(1)}, u32[]{:S(2)}, u32[]{:S(2)}) %collective-permute-start) | collective-permute-done | bytes 147488 | tf_op jit(solution)/shard_map/ppermute | solution.py:382
  11.7 5.5 %collective-permute-done.1.refs_2_.refs_1_ = bf16[72,1024]{1,0:T(8,128)(2,1)S(1)} collective-permute-done((bf16[72,1024]{1,0:T(8,128)(2,1)S(1)}, bf16[72,1024]{1,0:T(8,128)(2,1)S(1)}, u32[]{:S(2)}, u32[]{:S(2)}) %collective-permute-start.1) | collective-permute-done | bytes 147488 | tf_op jit(solution)/shard_map/ppermute | solution.py:382
  17.4 1.5 %collective-permute-start.4 = (bf16[200,1024]{1,0:T(8,128)(2,1)S(1)}, bf16[200,1024]{1,0:T(8,128)(2,1)S(1)}, u32[]{:S(2)}, u32[]{:S(2)}) collective-permute-start(bf16[200,1024]{1,0:T(8,128)(2,1)S(1)} %shard_map.74), channel_id=1, source_target_pairs={{0,2},{1,3},{2,0},{3,1},{4,6},{5,7},{6,4},{7,5},{8,10},{9,11},{10,... | collective-permute-start | bytes 1228808 | tf_op jit(solution)/shard_map/ppermute | solution.py:385
  19.4 8.8 %fetch.1 = (bf16[8,2,192,2048]{3,2,1,0:T(8,128)(2,1)S(1)}, bf16[8,2,192,2048]{3,2,1,0:T(8,128)(2,1)S(1)}) custom-call(s32[5]{0:T(128)S(1)} %stack.23.where, bf16[16,192,4096]{2,1,0:T(8,128)(2,1)} %refs_0_.2, bf16[16,192,4096]{2,1,0:T(8,128)(2,1)} %refs_1_.1), custom_call_target="tpu_custom_call" | custom-call | bytes 100663296 | tf_op jit(solution)/shard_map/fetch/pallas_call | solution.py:400
  28.3 0.8 route.1
  29.0 3.4 %collective-permute-done.6.near_own_ref = bf16[72,1024]{1,0:T(8,128)(2,1)S(1)} collective-permute-done((bf16[72,1024]{1,0:T(8,128)(2,1)S(1)}, bf16[72,1024]{1,0:T(8,128)(2,1)S(1)}, u32[]{:S(2)}, u32[]{:S(2)}) %collective-permute-start.6) | collective-permute-done | bytes 147488 | tf_op jit(solution)/shard_map/ppermute | solution.py:385
  33.0 4.1 %shard_map.75 = (f32[8,2,192,256]{3,2,1,0:T(8,128)S(1)}, bf16[8,2,192,2048]{3,2,1,0:T(8,128)(2,1)S(1)}) custom-call(s32[5]{0:T(128)S(1)} %stack.23.where, bf16[264,1024]{1,0:T(8,128)(2,1)S(1)} %shard_map.73.xa_ref, bf16[264,1024]{1,0:T(8,128)(2,1)S(1)} %collective-permute-done.3.xb_ref, bf16[8,2,192,2048]{3,2,1,0:T(8,128)(2,1)S(1)} %get-tuple-element.29.w_ref, ...), custom_call_target="tpu_custom_call" | custom-call | flops 3221225472 | bytes 12582912 | tf_op jit(solution)/shard_map/pallas_call | solution.py:442
  37.1 4.1 %shard_map.76 = (f32[8,2,192,256]{3,2,1,0:T(8,128)S(1)}, bf16[8,2,192,2048]{3,2,1,0:T(8,128)(2,1)S(1)}) custom-call(s32[5]{0:T(128)S(1)} %stack.23.where, bf16[264,1024]{1,0:T(8,128)(2,1)S(1)} %shard_map.73.xa_ref, bf16[264,1024]{1,0:T(8,128)(2,1)S(1)} %collective-permute-done.3.xb_ref, ...), custom_call_target="tpu_custom_call", output_to_operand_aliasing={{1}: (6, {})} | custom-call | flops 3221225472 | bytes 12582912 | tf_op jit(solution)/shard_map/pallas_call | solution.py:442
  41.3 5.5 %shard_map.77 = (bf16[4,192,128]{2,1,0:T(8,128)(2,1)S(1)}, bf16[8,2,192,2048]{3,2,1,0:T(8,128)(2,1)S(1)}) custom-call(s32[5]{0:T(128)S(1)} %stack.23.where, bf16[264,1024]{1,0:T(8,128)(2,1)S(1)} %shard_map.73.xa_ref, bf16[264,1024]{1,0:T(8,128)(2,1)S(1)} %collective-permute-done.3.xb_ref, bf16[200,1024]{1,0:T(8,128)(2,1)S(1)} %collective-permute-done.4.near_ref, ...), custom_call_target="tpu_custom_call" | custom-call | flops 3221225472 | bytes 25165824 | tf_op jit(solution)/shard_map/pallas_call | solution.py:480
  46.8 1.6 %collective-permute-start.12 = (bf16[4,192,128]{2,1,0:T(8,128)(2,1)S(1)}, bf16[4,192,128]{2,1,0:T(8,128)(2,1)S(1)}, u32[]{:S(2)}, u32[]{:S(2)}) collective-permute-start(bf16[4,192,128]{2,1,0:T(8,128)(2,1)S(1)} %get-tuple-element.38.refs_0_), channel_id=1, source_target_pairs={{0,2},{1,3},{2,0},{3,1},{4,6},{5,7},{6,4},{7,5},{8,10},{9,11},{10,... | collective-permute-start | bytes 589832 | tf_op jit(solution)/shard_map/ppermute | solution.py:385
  48.3 5.2 %shard_map.78 = (bf16[4,192,128]{2,1,0:T(8,128)(2,1)S(1)}, bf16[8,1024,768]{2,1,0:T(8,128)(2,1)S(1)}) custom-call(s32[5]{0:T(128)S(1)} %stack.23.where, bf16[264,1024]{1,0:T(8,128)(2,1)S(1)} %shard_map.73.xa_ref, bf16[264,1024]{1,0:T(8,128)(2,1)S(1)} %collective-permute-done.3.xb_ref, bf16[200,1024]{1,0:T(8,128)(2,1)S(1)} %collective-permute-done.4.near_ref, ...), custom_call_target="tpu_custom_call" | custom-call | flops 3221225472 | bytes 25165824 | tf_op jit(solution)/shard_map/pallas_call | solution.py:480
  54.7 5.5 %collective-permute-done.9.refs_2_ = bf16[4,192,128]{2,1,0:T(8,128)(2,1)S(1)} collective-permute-done((bf16[4,192,128]{2,1,0:T(8,128)(2,1)S(1)}, bf16[4,192,128]{2,1,0:T(8,128)(2,1)S(1)}, u32[]{:S(2)}, u32[]{:S(2)}) %collective-permute-start.9) | collective-permute-done | bytes 196640 | tf_op jit(solution)/shard_map/ppermute | solution.py:385
  60.2 5.3 %shard_map.79 = (f32[256,1024]{1,0:T(8,128)S(1)}, bf16[8,1024,768]{2,1,0:T(8,128)(2,1)S(1)}) custom-call(s32[5]{0:T(128)S(1)} %stack.23.where, bf16[4,192,128]{2,1,0:T(8,128)(2,1)S(1)} %get-tuple-element.38.refs_0_, bf16[4,192,128]{2,1,0:T(8,128)(2,1)S(1)} %collective-permute-done.11.refs_1_, bf16[4,192,128]{2,1,0:T(8,128)(2,1)S(1)} %collective-permute-done.12.refs_2_, ...), custom_call_target="tpu_custom_call" | custom-call | flops 3221225472 | tf_op jit(solution)/shard_map/pallas_call | solution.py:528
  65.5 3.5 %shard_map.80 = (f32[64,512]{1,0:T(8,128)S(1)}, bf16[64,512]{1,0:T(8,128)(2,1)S(1)}, bf16[64,512]{1,0:T(8,128)(2,1)S(1)}, bf16[64,512]{1,0:T(8,128)(2,1)S(1)}, bf16[4,512,768]{2,1,0:T(8,128)(2,1)S(1)}) custom-call(s32[5]{0:T(128)S(1)} %stack.23.where, bf16[4,192,128]{2,1,0:T(8,128)(2,1)S(1)} %get-tuple-element.37.refs_0_, ...), custom_call_target="tpu_custom_call" | custom-call | flops 1610612736 | tf_op jit(solution)/shard_map/pallas_call | solution.py:528
  69.0 2.7 %shard_map.81 = (f32[64,512]{1,0:T(8,128)S(1)}, bf16[64,512]{1,0:T(8,128)(2,1)S(1)}, bf16[64,512]{1,0:T(8,128)(2,1)S(1)}, bf16[64,512]{1,0:T(8,128)(2,1)S(1)}) custom-call(s32[5]{0:T(128)S(1)} %stack.23.where, bf16[4,512,768]{2,1,0:T(8,128)(2,1)S(1)} %get-tuple-element.46.refs_0_, bf16[8,1024,768]{2,1,0:T(8,128)(2,1)S(1)} %get-tuple-element.40.refs_5_.refs_1_, ...), custom_call_target="tpu_custom_call" | custom-call | flops 1610612736 | tf_op jit(solution)/shard_map/pallas_call | solution.py:528
  71.7 4.7 %collective-permute-start.17 = (bf16[64,512]{1,0:T(8,128)(2,1)S(1)}, bf16[64,512]{1,0:T(8,128)(2,1)S(1)}, u32[]{:S(2)}, u32[]{:S(2)}) collective-permute-start(bf16[64,512]{1,0:T(8,128)(2,1)S(1)} %get-tuple-element.48), channel_id=1, source_target_pairs={{0,12},{4,0},{8,4},{12,8},{1,13},{5,1},{9,5},{13,9},{2,14},{6,2},{... | collective-permute-start | bytes 196616 | tf_op jit(solution)/shard_map/ppermute | solution.py:382
  77.1 3.6 %collective-permute-start.14 = (bf16[64,512]{1,0:T(8,128)(2,1)S(1)}, bf16[64,512]{1,0:T(8,128)(2,1)S(1)}, u32[]{:S(2)}, u32[]{:S(2)}) collective-permute-start(bf16[64,512]{1,0:T(8,128)(2,1)S(1)} %get-tuple-element.43), channel_id=1, source_target_pairs={{0,12},{4,0},{8,4},{12,8},{1,13},{5,1},{9,5},{13,9},{2,14},{6,2},{... | collective-permute-start | bytes 196616 | tf_op jit(solution)/shard_map/ppermute | solution.py:382
  80.6 0.7 collective-permute-start.15
  81.4 3.1 %collective-permute-done.18.refs_6_ = bf16[64,512]{1,0:T(8,128)(2,1)S(1)} collective-permute-done((bf16[64,512]{1,0:T(8,128)(2,1)S(1)}, bf16[64,512]{1,0:T(8,128)(2,1)S(1)}, u32[]{:S(2)}, u32[]{:S(2)}) %collective-permute-start.18) | collective-permute-done | bytes 65568 | tf_op jit(solution)/shard_map/ppermute | solution.py:382
  84.6 4.5 %collective-permute-done.15.refs_2_ = bf16[64,512]{1,0:T(8,128)(2,1)S(1)} collective-permute-done((bf16[64,512]{1,0:T(8,128)(2,1)S(1)}, bf16[64,512]{1,0:T(8,128)(2,1)S(1)}, u32[]{:S(2)}, u32[]{:S(2)}) %collective-permute-start.15) | collective-permute-done | bytes 65568 | tf_op jit(solution)/shard_map/ppermute | solution.py:382
  (30 shorter events, 4.1 us)
Async XLA Ops:
  1.8 9.9 %collective-permute-start = (bf16[72,1024]{1,0:T(8,128)(2,1)S(1)}, bf16[72,1024]{1,0:T(8,128)(2,1)S(1)}, u32[]{:S(2)}, u32[]{:S(2)}) collective-permute-start(bf16[72,1024]{1,0:T(8,128)(2,1)S(1)} %pack.1.refs_0_), channel_id=1, source_target_pairs={{0,4},{4,8},{8,12},{12,0},{1,5},{5,9},{9,13},{13,1},{2,6},{6,10},{... | collective-permute-start | bytes 442376 | tf_op jit(solution)/shard_map/ppermute | solution.py:382
  4.9 12.3 %collective-permute-start.1 = (bf16[72,1024]{1,0:T(8,128)(2,1)S(1)}, bf16[72,1024]{1,0:T(8,128)(2,1)S(1)}, u32[]{:S(2)}, u32[]{:S(2)}) collective-permute-start(bf16[72,1024]{1,0:T(8,128)(2,1)S(1)} %pack.1.refs_0_), channel_id=1, source_target_pairs={{0,8},{4,12},{8,0},{12,4},{1,9},{5,13},{9,1},{13,5},{2,10},{6,14},... | collective-permute-start | bytes 442376 | tf_op jit(solution)/shard_map/ppermute | solution.py:382
  7.5 9.7 %collective-permute-start.2 = (bf16[72,1024]{1,0:T(8,128)(2,1)S(1)}, bf16[72,1024]{1,0:T(8,128)(2,1)S(1)}, u32[]{:S(2)}, u32[]{:S(2)}) collective-permute-start(bf16[72,1024]{1,0:T(8,128)(2,1)S(1)} %pack.1.refs_0_), channel_id=1, source_target_pairs={{0,12},{4,0},{8,4},{12,8},{1,13},{5,1},{9,5},{13,9},{2,14},{6,2},{... | collective-permute-start | bytes 442376 | tf_op jit(solution)/shard_map/ppermute | solution.py:382
  17.3 15.7 %collective-permute-start.3 = (bf16[264,1024]{1,0:T(8,128)(2,1)S(1)}, bf16[264,1024]{1,0:T(8,128)(2,1)S(1)}, u32[]{:S(2)}, u32[]{:S(2)}) collective-permute-start(bf16[264,1024]{1,0:T(8,128)(2,1)S(1)} %shard_map.73.xa_ref), channel_id=1, source_target_pairs={{0,1},{1,0},{2,3},{3,2},{4,5},{5,4},{6,7},{7,6},{8,9},{9,8},{10,11... | collective-permute-start | bytes 1622024 | tf_op jit(solution)/shard_map/ppermute | solution.py:385
  17.4 15.0 %collective-permute-start.4 = (bf16[200,1024]{1,0:T(8,128)(2,1)S(1)}, bf16[200,1024]{1,0:T(8,128)(2,1)S(1)}, u32[]{:S(2)}, u32[]{:S(2)}) collective-permute-start(bf16[200,1024]{1,0:T(8,128)(2,1)S(1)} %shard_map.74), channel_id=1, source_target_pairs={{0,2},{1,3},{2,0},{3,1},{4,6},{5,7},{6,4},{7,5},{8,10},{9,11},{10,... | collective-permute-start | bytes 1228808 | tf_op jit(solution)/shard_map/ppermute | solution.py:385
  18.9 13.5 %collective-permute-start.6 = (bf16[72,1024]{1,0:T(8,128)(2,1)S(1)}, bf16[72,1024]{1,0:T(8,128)(2,1)S(1)}, u32[]{:S(2)}, u32[]{:S(2)}) collective-permute-start(bf16[72,1024]{1,0:T(8,128)(2,1)S(1)} %pack.1.refs_0_), channel_id=1, source_target_pairs={{0,2},{1,3},{2,0},{3,1},{4,6},{5,7},{6,4},{7,5},{8,10},{9,11},{10,... | collective-permute-start | bytes 442376 | tf_op jit(solution)/shard_map/ppermute | solution.py:385
  32.4 8.8 %collective-permute-start.7 = (bf16[72,1024]{1,0:T(8,128)(2,1)S(1)}, bf16[72,1024]{1,0:T(8,128)(2,1)S(1)}, u32[]{:S(2)}, u32[]{:S(2)}) collective-permute-start(bf16[72,1024]{1,0:T(8,128)(2,1)S(1)} %collective-permute-done.6.near_own_ref), channel_id=1, source_target_pairs={{0,1},{1,0},{2,3},{3,2},{4,5},{5,4},{6,7},{7,6},{8,9},{9,8},{10,11... | collective-permute-start | bytes 442376 | tf_op jit(solution)/shard_map/ppermute | solution.py:385
  32.4 8.8 %collective-permute-start.5 = (bf16[200,1024]{1,0:T(8,128)(2,1)S(1)}, bf16[200,1024]{1,0:T(8,128)(2,1)S(1)}, u32[]{:S(2)}, u32[]{:S(2)}) collective-permute-start(bf16[200,1024]{1,0:T(8,128)(2,1)S(1)} %collective-permute-done.4.near_ref), channel_id=1, source_target_pairs={{0,1},{1,0},{2,3},{3,2},{4,5},{5,4},{6,7},{7,6},{8,9},{9,8},{10,11... | collective-permute-start | bytes 1228808 | tf_op jit(solution)/shard_map/ppermute | solution.py:385
  46.8 7.4 %collective-permute-start.12 = (bf16[4,192,128]{2,1,0:T(8,128)(2,1)S(1)}, bf16[4,192,128]{2,1,0:T(8,128)(2,1)S(1)}, u32[]{:S(2)}, u32[]{:S(2)}) collective-permute-start(bf16[4,192,128]{2,1,0:T(8,128)(2,1)S(1)} %get-tuple-element.38.refs_0_), channel_id=1, source_target_pairs={{0,2},{1,3},{2,0},{3,1},{4,6},{5,7},{6,4},{7,5},{8,10},{9,11},{10,... | collective-permute-start | bytes 589832 | tf_op jit(solution)/shard_map/ppermute | solution.py:385
  53.6 6.6 %collective-permute-start.9 = (bf16[4,192,128]{2,1,0:T(8,128)(2,1)S(1)}, bf16[4,192,128]{2,1,0:T(8,128)(2,1)S(1)}, u32[]{:S(2)}, u32[]{:S(2)}) collective-permute-start(bf16[4,192,128]{2,1,0:T(8,128)(2,1)S(1)} %get-tuple-element.37.refs_0_), channel_id=1, source_target_pairs={{0,2},{1,3},{2,0},{3,1},{4,6},{5,7},{6,4},{7,5},{8,10},{9,11},{10,... | collective-permute-start | bytes 589832 | tf_op jit(solution)/shard_map/ppermute | solution.py:385
  54.2 6.0 %collective-permute-start.11 = (bf16[4,192,128]{2,1,0:T(8,128)(2,1)S(1)}, bf16[4,192,128]{2,1,0:T(8,128)(2,1)S(1)}, u32[]{:S(2)}, u32[]{:S(2)}) collective-permute-start(bf16[4,192,128]{2,1,0:T(8,128)(2,1)S(1)} %get-tuple-element.38.refs_0_), channel_id=1, source_target_pairs={{0,1},{1,0},{2,3},{3,2},{4,5},{5,4},{6,7},{7,6},{8,9},{9,8},{10,11... | collective-permute-start | bytes 589832 | tf_op jit(solution)/shard_map/ppermute | solution.py:385
  54.2 6.0 %collective-permute-start.13 = (bf16[4,192,128]{2,1,0:T(8,128)(2,1)S(1)}, bf16[4,192,128]{2,1,0:T(8,128)(2,1)S(1)}, u32[]{:S(2)}, u32[]{:S(2)}) collective-permute-start(bf16[4,192,128]{2,1,0:T(8,128)(2,1)S(1)} %collective-permute-done.12.refs_2_), channel_id=1, source_target_pairs={{0,1},{1,0},{2,3},{3,2},{4,5},{5,4},{6,7},{7,6},{8,9},{9,8},{10,11... | collective-permute-start | bytes 589832 | tf_op jit(solution)/shard_map/ppermute | solution.py:385
  54.7 10.8 %collective-permute-start.8 = (bf16[4,192,128]{2,1,0:T(8,128)(2,1)S(1)}, bf16[4,192,128]{2,1,0:T(8,128)(2,1)S(1)}, u32[]{:S(2)}, u32[]{:S(2)}) collective-permute-start(bf16[4,192,128]{2,1,0:T(8,128)(2,1)S(1)} %get-tuple-element.37.refs_0_), channel_id=1, source_target_pairs={{0,1},{1,0},{2,3},{3,2},{4,5},{5,4},{6,7},{7,6},{8,9},{9,8},{10,11... | collective-permute-start | bytes 589832 | tf_op jit(solution)/shard_map/ppermute | solution.py:385
  60.2 5.3 %collective-permute-start.10 = (bf16[4,192,128]{2,1,0:T(8,128)(2,1)S(1)}, bf16[4,192,128]{2,1,0:T(8,128)(2,1)S(1)}, u32[]{:S(2)}, u32[]{:S(2)}) collective-permute-start(bf16[4,192,128]{2,1,0:T(8,128)(2,1)S(1)} %collective-permute-done.9.refs_2_), channel_id=1, source_target_pairs={{0,1},{1,0},{2,3},{3,2},{4,5},{5,4},{6,7},{7,6},{8,9},{9,8},{10,11... | collective-permute-start | bytes 589832 | tf_op jit(solution)/shard_map/ppermute | solution.py:385
  71.7 9.7 %collective-permute-start.17 = (bf16[64,512]{1,0:T(8,128)(2,1)S(1)}, bf16[64,512]{1,0:T(8,128)(2,1)S(1)}, u32[]{:S(2)}, u32[]{:S(2)}) collective-permute-start(bf16[64,512]{1,0:T(8,128)(2,1)S(1)} %get-tuple-element.48), channel_id=1, source_target_pairs={{0,12},{4,0},{8,4},{12,8},{1,13},{5,1},{9,5},{13,9},{2,14},{6,2},{... | collective-permute-start | bytes 196616 | tf_op jit(solution)/shard_map/ppermute | solution.py:382
  76.4 8.0 %collective-permute-start.18 = (bf16[64,512]{1,0:T(8,128)(2,1)S(1)}, bf16[64,512]{1,0:T(8,128)(2,1)S(1)}, u32[]{:S(2)}, u32[]{:S(2)}) collective-permute-start(bf16[64,512]{1,0:T(8,128)(2,1)S(1)} %get-tuple-element.49), channel_id=1, source_target_pairs={{0,8},{4,12},{8,0},{12,4},{1,9},{5,13},{9,1},{13,5},{2,10},{6,14},... | collective-permute-start | bytes 196616 | tf_op jit(solution)/shard_map/ppermute | solution.py:382
  76.8 7.6 %collective-permute-start.19 = (bf16[64,512]{1,0:T(8,128)(2,1)S(1)}, bf16[64,512]{1,0:T(8,128)(2,1)S(1)}, u32[]{:S(2)}, u32[]{:S(2)}) collective-permute-start(bf16[64,512]{1,0:T(8,128)(2,1)S(1)} %get-tuple-element.50), channel_id=1, source_target_pairs={{0,4},{4,8},{8,12},{12,0},{1,5},{5,9},{9,13},{13,1},{2,6},{6,10},{... | collective-permute-start | bytes 196616 | tf_op jit(solution)/shard_map/ppermute | solution.py:382
  77.1 7.6 %collective-permute-start.14 = (bf16[64,512]{1,0:T(8,128)(2,1)S(1)}, bf16[64,512]{1,0:T(8,128)(2,1)S(1)}, u32[]{:S(2)}, u32[]{:S(2)}) collective-permute-start(bf16[64,512]{1,0:T(8,128)(2,1)S(1)} %get-tuple-element.43), channel_id=1, source_target_pairs={{0,12},{4,0},{8,4},{12,8},{1,13},{5,1},{9,5},{13,9},{2,14},{6,2},{... | collective-permute-start | bytes 196616 | tf_op jit(solution)/shard_map/ppermute | solution.py:382
  80.6 8.5 %collective-permute-start.15 = (bf16[64,512]{1,0:T(8,128)(2,1)S(1)}, bf16[64,512]{1,0:T(8,128)(2,1)S(1)}, u32[]{:S(2)}, u32[]{:S(2)}) collective-permute-start(bf16[64,512]{1,0:T(8,128)(2,1)S(1)} %get-tuple-element.44), channel_id=1, source_target_pairs={{0,8},{4,12},{8,0},{12,4},{1,9},{5,13},{9,1},{13,5},{2,10},{6,14},... | collective-permute-start | bytes 196616 | tf_op jit(solution)/shard_map/ppermute | solution.py:382
  81.4 7.8 %collective-permute-start.16 = (bf16[64,512]{1,0:T(8,128)(2,1)S(1)}, bf16[64,512]{1,0:T(8,128)(2,1)S(1)}, u32[]{:S(2)}, u32[]{:S(2)}) collective-permute-start(bf16[64,512]{1,0:T(8,128)(2,1)S(1)} %get-tuple-element.45), channel_id=1, source_target_pairs={{0,4},{4,8},{8,12},{12,0},{1,5},{5,9},{9,13},{13,1},{2,6},{6,10},{... | collective-permute-start | bytes 196616 | tf_op jit(solution)/shard_map/ppermute | solution.py:382

commit v6 on v5

--- a/solution.py
+++ b/solution.py
@@ -281,7 +281,7 @@
     def _():
         acc[...] = jnp.zeros_like(acc) if start else before[0][:, features]
 
-    groups = 2
+    groups = d_ref.shape[0] // pair if last else 2
     hidden = []
     for g in range(groups):
         if spread:
@@ -517,12 +517,13 @@
             out_shape += [pltpu.VMEM((pairs, 2 * count, hidden_units), jnp.bfloat16)]
         if before is None:
             out_shape += [pltpu.VMEM(down_buffer, down_proj.dtype)]
-        steps = pairs // 2
-        routing = pl.BlockSpec((4, 1, count), lambda i, w: (i + part * steps, 0, 0))
-        moved = pl.BlockSpec((2, units, slots), lambda i, w: (i, 0, 0))
+        steps = 1 if last else pairs // 2
+        each = pairs // steps
+        routing = pl.BlockSpec((2 * each, 1, count), lambda i, w: (i + part * steps, 0, 0))
+        moved = pl.BlockSpec((each, units, slots), lambda i, w: (i, 0, 0))
         scratch = [pltpu.VMEM((count, wide), jnp.float32)]
         if spread:
-            scratch = [pltpu.VMEM((2, shards, units, slots), jnp.bfloat16)] + scratch
+            scratch = [pltpu.VMEM((each, shards, units, slots), jnp.bfloat16)] + scratch
         if before is None:
             scratch += [pltpu.SemaphoreType.DMA((2,))]
         return pl.pallas_call(

time: 90 us -> 89.4 us (level)
  no operation moved by 1% of the time
where the time goes in v6:
time: 89.4 us; the launch traced here: 89.3 us
  Pallas kernels  42 us (47%)
  waiting for transfers between devices  25 us (28%)
  starting transfers between devices  22 us (25%)
    ppermute x9, starting transfers between devices, shift(): lax.ppermute(v, 'expert', [(i, (i + n) % blocks) for i in range(blocks)])  16.7 us
    ppermute x9, waiting for transfers between devices, shift(): lax.ppermute(v, 'expert', [(i, (i + n) % blocks) for i in range(blocks)])  16.1 us
    pallas_call x3, Pallas kernels, down(): pl.pallas_call(functools.partial(down_kernel, shards=shards, span=span, s...  10.8 us
    pallas_call x2, Pallas kernels, second(): pl.pallas_call(functools.partial(second_half_kernel, features=features),...  10.7 us
    ppermute x11, waiting for transfers between devices, swap(): return lax.ppermute(v, 'tensor', [(i, i ^ n) for i in range(shards)])  8.9 us
    pallas_call x1, Pallas kernels, dense_body(): pl.pallas_call(fetch_kernel, grid_spec=pltpu.PrefetchScalarGridSpec(num_s...  8.83 us
    pallas_call x2, Pallas kernels, first(): pl.pallas_call(functools.partial(first_half_kernel, first=part * half //...  8.27 us
    ppermute x11, starting transfers between devices, swap(): return lax.ppermute(v, 'tensor', [(i, i ^ n) for i in range(shards)])  5.25 us
  transfers between devices with their start and end apart: 20, of which 7 were waited for; matrix products, arithmetic and copies ran while one was open for 0% of the time, Pallas kernels for 32%

profile of v6, /device:TPU:0, one launch (start us, length us, event | category | flops | bytes accessed | tf_op | source)
XLA Modules:
  0.0 89.3 jit_solution(6366004497836054905)
XLA Ops:
  0.1 1.7 %pack.1.refs_0_ = bf16[72,1024]{1,0:T(8,128)(2,1)S(1)} custom-call(s32[5]{0:T(128)S(1)} %stack.23.where, bf16[64,1024]{1,0:T(8,128)(2,1)} %x_hbm.1, f32[1,4096]{1,0:T(1,128)} %bitcast.8, s32[8,64]{1,0:T(8,128)} %bitcast.9, f32[8,64]{1,0:T(8,128)} %bitcast.10), custom_call_target="tpu_custom_call" | custom-call | tf_op jit(solution)/shard_map/pack/pallas_call | solution.py:355
  1.8 3.1 %collective-permute-start = (bf16[72,1024]{1,0:T(8,128)(2,1)S(1)}, bf16[72,1024]{1,0:T(8,128)(2,1)S(1)}, u32[]{:S(2)}, u32[]{:S(2)}) collective-permute-start(bf16[72,1024]{1,0:T(8,128)(2,1)S(1)} %pack.1.refs_0_), channel_id=1, source_target_pairs={{0,4},{4,8},{8,12},{12,0},{1,5},{5,9},{9,13},{13,1},{2,6},{6,10},{... | collective-permute-start | bytes 442376 | tf_op jit(solution)/shard_map/ppermute | solution.py:382
  4.9 2.6 %collective-permute-start.1 = (bf16[72,1024]{1,0:T(8,128)(2,1)S(1)}, bf16[72,1024]{1,0:T(8,128)(2,1)S(1)}, u32[]{:S(2)}, u32[]{:S(2)}) collective-permute-start(bf16[72,1024]{1,0:T(8,128)(2,1)S(1)} %pack.1.refs_0_), channel_id=1, source_target_pairs={{0,8},{4,12},{8,0},{12,4},{1,9},{5,13},{9,1},{13,5},{2,10},{6,14},... | collective-permute-start | bytes 442376 | tf_op jit(solution)/shard_map/ppermute | solution.py:382
  7.5 1.3 %collective-permute-start.2 = (bf16[72,1024]{1,0:T(8,128)(2,1)S(1)}, bf16[72,1024]{1,0:T(8,128)(2,1)S(1)}, u32[]{:S(2)}, u32[]{:S(2)}) collective-permute-start(bf16[72,1024]{1,0:T(8,128)(2,1)S(1)} %pack.1.refs_0_), channel_id=1, source_target_pairs={{0,12},{4,0},{8,4},{12,8},{1,13},{5,1},{9,5},{13,9},{2,14},{6,2},{... | collective-permute-start | bytes 442376 | tf_op jit(solution)/shard_map/ppermute | solution.py:382
  8.8 2.9 %collective-permute-done.refs_1_.refs_0_ = bf16[72,1024]{1,0:T(8,128)(2,1)S(1)} collective-permute-done((bf16[72,1024]{1,0:T(8,128)(2,1)S(1)}, bf16[72,1024]{1,0:T(8,128)(2,1)S(1)}, u32[]{:S(2)}, u32[]{:S(2)}) %collective-permute-start) | collective-permute-done | bytes 147488 | tf_op jit(solution)/shard_map/ppermute | solution.py:382
  11.7 5.5 %collective-permute-done.1.refs_2_.refs_1_ = bf16[72,1024]{1,0:T(8,128)(2,1)S(1)} collective-permute-done((bf16[72,1024]{1,0:T(8,128)(2,1)S(1)}, bf16[72,1024]{1,0:T(8,128)(2,1)S(1)}, u32[]{:S(2)}, u32[]{:S(2)}) %collective-permute-start.1) | collective-permute-done | bytes 147488 | tf_op jit(solution)/shard_map/ppermute | solution.py:382
  17.4 1.5 %collective-permute-start.4 = (bf16[200,1024]{1,0:T(8,128)(2,1)S(1)}, bf16[200,1024]{1,0:T(8,128)(2,1)S(1)}, u32[]{:S(2)}, u32[]{:S(2)}) collective-permute-start(bf16[200,1024]{1,0:T(8,128)(2,1)S(1)} %shard_map.74), channel_id=1, source_target_pairs={{0,2},{1,3},{2,0},{3,1},{4,6},{5,7},{6,4},{7,5},{8,10},{9,11},{10,... | collective-permute-start | bytes 1228808 | tf_op jit(solution)/shard_map/ppermute | solution.py:385
  19.4 8.8 %fetch.1 = (bf16[8,2,192,2048]{3,2,1,0:T(8,128)(2,1)S(1)}, bf16[8,2,192,2048]{3,2,1,0:T(8,128)(2,1)S(1)}) custom-call(s32[5]{0:T(128)S(1)} %stack.23.where, bf16[16,192,4096]{2,1,0:T(8,128)(2,1)} %refs_0_.2, bf16[16,192,4096]{2,1,0:T(8,128)(2,1)} %refs_1_.1), custom_call_target="tpu_custom_call" | custom-call | bytes 100663296 | tf_op jit(solution)/shard_map/fetch/pallas_call | solution.py:400
  28.3 0.8 route.1
  29.0 3.4 %collective-permute-done.6.near_own_ref = bf16[72,1024]{1,0:T(8,128)(2,1)S(1)} collective-permute-done((bf16[72,1024]{1,0:T(8,128)(2,1)S(1)}, bf16[72,1024]{1,0:T(8,128)(2,1)S(1)}, u32[]{:S(2)}, u32[]{:S(2)}) %collective-permute-start.6) | collective-permute-done | bytes 147488 | tf_op jit(solution)/shard_map/ppermute | solution.py:385
  33.0 4.1 %shard_map.75 = (f32[8,2,192,256]{3,2,1,0:T(8,128)S(1)}, bf16[8,2,192,2048]{3,2,1,0:T(8,128)(2,1)S(1)}) custom-call(s32[5]{0:T(128)S(1)} %stack.23.where, bf16[264,1024]{1,0:T(8,128)(2,1)S(1)} %shard_map.73.xa_ref, bf16[264,1024]{1,0:T(8,128)(2,1)S(1)} %collective-permute-done.3.xb_ref, bf16[8,2,192,2048]{3,2,1,0:T(8,128)(2,1)S(1)} %get-tuple-element.29.w_ref, ...), custom_call_target="tpu_custom_call" | custom-call | flops 3221225472 | bytes 12582912 | tf_op jit(solution)/shard_map/pallas_call | solution.py:442
  37.1 4.1 %shard_map.76 = (f32[8,2,192,256]{3,2,1,0:T(8,128)S(1)}, bf16[8,2,192,2048]{3,2,1,0:T(8,128)(2,1)S(1)}) custom-call(s32[5]{0:T(128)S(1)} %stack.23.where, bf16[264,1024]{1,0:T(8,128)(2,1)S(1)} %shard_map.73.xa_ref, bf16[264,1024]{1,0:T(8,128)(2,1)S(1)} %collective-permute-done.3.xb_ref, ...), custom_call_target="tpu_custom_call", output_to_operand_aliasing={{1}: (6, {})} | custom-call | flops 3221225472 | bytes 12582912 | tf_op jit(solution)/shard_map/pallas_call | solution.py:442
  41.3 5.5 %shard_map.77 = (bf16[4,192,128]{2,1,0:T(8,128)(2,1)S(1)}, bf16[8,2,192,2048]{3,2,1,0:T(8,128)(2,1)S(1)}) custom-call(s32[5]{0:T(128)S(1)} %stack.23.where, bf16[264,1024]{1,0:T(8,128)(2,1)S(1)} %shard_map.73.xa_ref, bf16[264,1024]{1,0:T(8,128)(2,1)S(1)} %collective-permute-done.3.xb_ref, bf16[200,1024]{1,0:T(8,128)(2,1)S(1)} %collective-permute-done.4.near_ref, ...), custom_call_target="tpu_custom_call" | custom-call | flops 3221225472 | bytes 25165824 | tf_op jit(solution)/shard_map/pallas_call | solution.py:480
  46.8 1.6 %collective-permute-start.12 = (bf16[4,192,128]{2,1,0:T(8,128)(2,1)S(1)}, bf16[4,192,128]{2,1,0:T(8,128)(2,1)S(1)}, u32[]{:S(2)}, u32[]{:S(2)}) collective-permute-start(bf16[4,192,128]{2,1,0:T(8,128)(2,1)S(1)} %get-tuple-element.38.refs_0_), channel_id=1, source_target_pairs={{0,2},{1,3},{2,0},{3,1},{4,6},{5,7},{6,4},{7,5},{8,10},{9,11},{10,... | collective-permute-start | bytes 589832 | tf_op jit(solution)/shard_map/ppermute | solution.py:385
  48.3 5.2 %shard_map.78 = (bf16[4,192,128]{2,1,0:T(8,128)(2,1)S(1)}, bf16[8,1024,768]{2,1,0:T(8,128)(2,1)S(1)}) custom-call(s32[5]{0:T(128)S(1)} %stack.23.where, bf16[264,1024]{1,0:T(8,128)(2,1)S(1)} %shard_map.73.xa_ref, bf16[264,1024]{1,0:T(8,128)(2,1)S(1)} %collective-permute-done.3.xb_ref, bf16[200,1024]{1,0:T(8,128)(2,1)S(1)} %collective-permute-done.4.near_ref, ...), custom_call_target="tpu_custom_call" | custom-call | flops 3221225472 | bytes 25165824 | tf_op jit(solution)/shard_map/pallas_call | solution.py:480
  54.7 5.5 %collective-permute-done.9.refs_2_ = bf16[4,192,128]{2,1,0:T(8,128)(2,1)S(1)} collective-permute-done((bf16[4,192,128]{2,1,0:T(8,128)(2,1)S(1)}, bf16[4,192,128]{2,1,0:T(8,128)(2,1)S(1)}, u32[]{:S(2)}, u32[]{:S(2)}) %collective-permute-start.9) | collective-permute-done | bytes 196640 | tf_op jit(solution)/shard_map/ppermute | solution.py:385
  60.2 5.3 %shard_map.79 = (f32[256,1024]{1,0:T(8,128)S(1)}, bf16[8,1024,768]{2,1,0:T(8,128)(2,1)S(1)}) custom-call(s32[5]{0:T(128)S(1)} %stack.23.where, bf16[4,192,128]{2,1,0:T(8,128)(2,1)S(1)} %get-tuple-element.38.refs_0_, bf16[4,192,128]{2,1,0:T(8,128)(2,1)S(1)} %collective-permute-done.11.refs_1_, bf16[4,192,128]{2,1,0:T(8,128)(2,1)S(1)} %collective-permute-done.12.refs_2_, ...), custom_call_target="tpu_custom_call" | custom-call | flops 3221225472 | tf_op jit(solution)/shard_map/pallas_call | solution.py:529
  65.5 3.2 %shard_map.80 = (f32[64,512]{1,0:T(8,128)S(1)}, bf16[64,512]{1,0:T(8,128)(2,1)S(1)}, bf16[64,512]{1,0:T(8,128)(2,1)S(1)}, bf16[64,512]{1,0:T(8,128)(2,1)S(1)}, bf16[4,512,768]{2,1,0:T(8,128)(2,1)S(1)}) custom-call(s32[5]{0:T(128)S(1)} %stack.23.where, bf16[4,192,128]{2,1,0:T(8,128)(2,1)S(1)} %get-tuple-element.37.refs_0_, ...), custom_call_target="tpu_custom_call" | custom-call | flops 1610612736 | tf_op jit(solution)/shard_map/pallas_call | solution.py:529
  68.7 2.4 %shard_map.81 = (f32[64,512]{1,0:T(8,128)S(1)}, bf16[64,512]{1,0:T(8,128)(2,1)S(1)}, bf16[64,512]{1,0:T(8,128)(2,1)S(1)}, bf16[64,512]{1,0:T(8,128)(2,1)S(1)}) custom-call(s32[5]{0:T(128)S(1)} %stack.23.where, bf16[4,512,768]{2,1,0:T(8,128)(2,1)S(1)} %get-tuple-element.46.refs_0_, bf16[8,1024,768]{2,1,0:T(8,128)(2,1)S(1)} %get-tuple-element.40.refs_5_.refs_1_, ...), custom_call_target="tpu_custom_call" | custom-call | flops 1610612736 | tf_op jit(solution)/shard_map/pallas_call | solution.py:529
  71.1 4.7 %collective-permute-start.17 = (bf16[64,512]{1,0:T(8,128)(2,1)S(1)}, bf16[64,512]{1,0:T(8,128)(2,1)S(1)}, u32[]{:S(2)}, u32[]{:S(2)}) collective-permute-start(bf16[64,512]{1,0:T(8,128)(2,1)S(1)} %get-tuple-element.48), channel_id=1, source_target_pairs={{0,12},{4,0},{8,4},{12,8},{1,13},{5,1},{9,5},{13,9},{2,14},{6,2},{... | collective-permute-start | bytes 196616 | tf_op jit(solution)/shard_map/ppermute | solution.py:382
  76.4 3.6 %collective-permute-start.14 = (bf16[64,512]{1,0:T(8,128)(2,1)S(1)}, bf16[64,512]{1,0:T(8,128)(2,1)S(1)}, u32[]{:S(2)}, u32[]{:S(2)}) collective-permute-start(bf16[64,512]{1,0:T(8,128)(2,1)S(1)} %get-tuple-element.43), channel_id=1, source_target_pairs={{0,12},{4,0},{8,4},{12,8},{1,13},{5,1},{9,5},{13,9},{2,14},{6,2},{... | collective-permute-start | bytes 196616 | tf_op jit(solution)/shard_map/ppermute | solution.py:382
  80.0 0.7 collective-permute-start.15
  80.8 3.1 %collective-permute-done.18.refs_6_ = bf16[64,512]{1,0:T(8,128)(2,1)S(1)} collective-permute-done((bf16[64,512]{1,0:T(8,128)(2,1)S(1)}, bf16[64,512]{1,0:T(8,128)(2,1)S(1)}, u32[]{:S(2)}, u32[]{:S(2)}) %collective-permute-start.18) | collective-permute-done | bytes 65568 | tf_op jit(solution)/shard_map/ppermute | solution.py:382
  84.0 4.5 %collective-permute-done.15.refs_2_ = bf16[64,512]{1,0:T(8,128)(2,1)S(1)} collective-permute-done((bf16[64,512]{1,0:T(8,128)(2,1)S(1)}, bf16[64,512]{1,0:T(8,128)(2,1)S(1)}, u32[]{:S(2)}, u32[]{:S(2)}) %collective-permute-start.15) | collective-permute-done | bytes 65568 | tf_op jit(solution)/shard_map/ppermute | solution.py:382
  (30 shorter events, 4.1 us)
Async XLA Ops:
  1.8 9.9 %collective-permute-start = (bf16[72,1024]{1,0:T(8,128)(2,1)S(1)}, bf16[72,1024]{1,0:T(8,128)(2,1)S(1)}, u32[]{:S(2)}, u32[]{:S(2)}) collective-permute-start(bf16[72,1024]{1,0:T(8,128)(2,1)S(1)} %pack.1.refs_0_), channel_id=1, source_target_pairs={{0,4},{4,8},{8,12},{12,0},{1,5},{5,9},{9,13},{13,1},{2,6},{6,10},{... | collective-permute-start | bytes 442376 | tf_op jit(solution)/shard_map/ppermute | solution.py:382
  4.9 12.3 %collective-permute-start.1 = (bf16[72,1024]{1,0:T(8,128)(2,1)S(1)}, bf16[72,1024]{1,0:T(8,128)(2,1)S(1)}, u32[]{:S(2)}, u32[]{:S(2)}) collective-permute-start(bf16[72,1024]{1,0:T(8,128)(2,1)S(1)} %pack.1.refs_0_), channel_id=1, source_target_pairs={{0,8},{4,12},{8,0},{12,4},{1,9},{5,13},{9,1},{13,5},{2,10},{6,14},... | collective-permute-start | bytes 442376 | tf_op jit(solution)/shard_map/ppermute | solution.py:382
  7.5 9.7 %collective-permute-start.2 = (bf16[72,1024]{1,0:T(8,128)(2,1)S(1)}, bf16[72,1024]{1,0:T(8,128)(2,1)S(1)}, u32[]{:S(2)}, u32[]{:S(2)}) collective-permute-start(bf16[72,1024]{1,0:T(8,128)(2,1)S(1)} %pack.1.refs_0_), channel_id=1, source_target_pairs={{0,12},{4,0},{8,4},{12,8},{1,13},{5,1},{9,5},{13,9},{2,14},{6,2},{... | collective-permute-start | bytes 442376 | tf_op jit(solution)/shard_map/ppermute | solution.py:382
  17.3 15.7 %collective-permute-start.3 = (bf16[264,1024]{1,0:T(8,128)(2,1)S(1)}, bf16[264,1024]{1,0:T(8,128)(2,1)S(1)}, u32[]{:S(2)}, u32[]{:S(2)}) collective-permute-start(bf16[264,1024]{1,0:T(8,128)(2,1)S(1)} %shard_map.73.xa_ref), channel_id=1, source_target_pairs={{0,1},{1,0},{2,3},{3,2},{4,5},{5,4},{6,7},{7,6},{8,9},{9,8},{10,11... | collective-permute-start | bytes 1622024 | tf_op jit(solution)/shard_map/ppermute | solution.py:385
  17.4 15.0 %collective-permute-start.4 = (bf16[200,1024]{1,0:T(8,128)(2,1)S(1)}, bf16[200,1024]{1,0:T(8,128)(2,1)S(1)}, u32[]{:S(2)}, u32[]{:S(2)}) collective-permute-start(bf16[200,1024]{1,0:T(8,128)(2,1)S(1)} %shard_map.74), channel_id=1, source_target_pairs={{0,2},{1,3},{2,0},{3,1},{4,6},{5,7},{6,4},{7,5},{8,10},{9,11},{10,... | collective-permute-start | bytes 1228808 | tf_op jit(solution)/shard_map/ppermute | solution.py:385
  18.9 13.5 %collective-permute-start.6 = (bf16[72,1024]{1,0:T(8,128)(2,1)S(1)}, bf16[72,1024]{1,0:T(8,128)(2,1)S(1)}, u32[]{:S(2)}, u32[]{:S(2)}) collective-permute-start(bf16[72,1024]{1,0:T(8,128)(2,1)S(1)} %pack.1.refs_0_), channel_id=1, source_target_pairs={{0,2},{1,3},{2,0},{3,1},{4,6},{5,7},{6,4},{7,5},{8,10},{9,11},{10,... | collective-permute-start | bytes 442376 | tf_op jit(solution)/shard_map/ppermute | solution.py:385
  32.4 8.8 %collective-permute-start.7 = (bf16[72,1024]{1,0:T(8,128)(2,1)S(1)}, bf16[72,1024]{1,0:T(8,128)(2,1)S(1)}, u32[]{:S(2)}, u32[]{:S(2)}) collective-permute-start(bf16[72,1024]{1,0:T(8,128)(2,1)S(1)} %collective-permute-done.6.near_own_ref), channel_id=1, source_target_pairs={{0,1},{1,0},{2,3},{3,2},{4,5},{5,4},{6,7},{7,6},{8,9},{9,8},{10,11... | collective-permute-start | bytes 442376 | tf_op jit(solution)/shard_map/ppermute | solution.py:385
  32.4 8.8 %collective-permute-start.5 = (bf16[200,1024]{1,0:T(8,128)(2,1)S(1)}, bf16[200,1024]{1,0:T(8,128)(2,1)S(1)}, u32[]{:S(2)}, u32[]{:S(2)}) collective-permute-start(bf16[200,1024]{1,0:T(8,128)(2,1)S(1)} %collective-permute-done.4.near_ref), channel_id=1, source_target_pairs={{0,1},{1,0},{2,3},{3,2},{4,5},{5,4},{6,7},{7,6},{8,9},{9,8},{10,11... | collective-permute-start | bytes 1228808 | tf_op jit(solution)/shard_map/ppermute | solution.py:385
  46.8 7.4 %collective-permute-start.12 = (bf16[4,192,128]{2,1,0:T(8,128)(2,1)S(1)}, bf16[4,192,128]{2,1,0:T(8,128)(2,1)S(1)}, u32[]{:S(2)}, u32[]{:S(2)}) collective-permute-start(bf16[4,192,128]{2,1,0:T(8,128)(2,1)S(1)} %get-tuple-element.38.refs_0_), channel_id=1, source_target_pairs={{0,2},{1,3},{2,0},{3,1},{4,6},{5,7},{6,4},{7,5},{8,10},{9,11},{10,... | collective-permute-start | bytes 589832 | tf_op jit(solution)/shard_map/ppermute | solution.py:385
  53.6 6.6 %collective-permute-start.9 = (bf16[4,192,128]{2,1,0:T(8,128)(2,1)S(1)}, bf16[4,192,128]{2,1,0:T(8,128)(2,1)S(1)}, u32[]{:S(2)}, u32[]{:S(2)}) collective-permute-start(bf16[4,192,128]{2,1,0:T(8,128)(2,1)S(1)} %get-tuple-element.37.refs_0_), channel_id=1, source_target_pairs={{0,2},{1,3},{2,0},{3,1},{4,6},{5,7},{6,4},{7,5},{8,10},{9,11},{10,... | collective-permute-start | bytes 589832 | tf_op jit(solution)/shard_map/ppermute | solution.py:385
  54.2 6.0 %collective-permute-start.11 = (bf16[4,192,128]{2,1,0:T(8,128)(2,1)S(1)}, bf16[4,192,128]{2,1,0:T(8,128)(2,1)S(1)}, u32[]{:S(2)}, u32[]{:S(2)}) collective-permute-start(bf16[4,192,128]{2,1,0:T(8,128)(2,1)S(1)} %get-tuple-element.38.refs_0_), channel_id=1, source_target_pairs={{0,1},{1,0},{2,3},{3,2},{4,5},{5,4},{6,7},{7,6},{8,9},{9,8},{10,11... | collective-permute-start | bytes 589832 | tf_op jit(solution)/shard_map/ppermute | solution.py:385
  54.2 6.0 %collective-permute-start.13 = (bf16[4,192,128]{2,1,0:T(8,128)(2,1)S(1)}, bf16[4,192,128]{2,1,0:T(8,128)(2,1)S(1)}, u32[]{:S(2)}, u32[]{:S(2)}) collective-permute-start(bf16[4,192,128]{2,1,0:T(8,128)(2,1)S(1)} %collective-permute-done.12.refs_2_), channel_id=1, source_target_pairs={{0,1},{1,0},{2,3},{3,2},{4,5},{5,4},{6,7},{7,6},{8,9},{9,8},{10,11... | collective-permute-start | bytes 589832 | tf_op jit(solution)/shard_map/ppermute | solution.py:385
  54.7 10.8 %collective-permute-start.8 = (bf16[4,192,128]{2,1,0:T(8,128)(2,1)S(1)}, bf16[4,192,128]{2,1,0:T(8,128)(2,1)S(1)}, u32[]{:S(2)}, u32[]{:S(2)}) collective-permute-start(bf16[4,192,128]{2,1,0:T(8,128)(2,1)S(1)} %get-tuple-element.37.refs_0_), channel_id=1, source_target_pairs={{0,1},{1,0},{2,3},{3,2},{4,5},{5,4},{6,7},{7,6},{8,9},{9,8},{10,11... | collective-permute-start | bytes 589832 | tf_op jit(solution)/shard_map/ppermute | solution.py:385
  60.2 5.3 %collective-permute-start.10 = (bf16[4,192,128]{2,1,0:T(8,128)(2,1)S(1)}, bf16[4,192,128]{2,1,0:T(8,128)(2,1)S(1)}, u32[]{:S(2)}, u32[]{:S(2)}) collective-permute-start(bf16[4,192,128]{2,1,0:T(8,128)(2,1)S(1)} %collective-permute-done.9.refs_2_), channel_id=1, source_target_pairs={{0,1},{1,0},{2,3},{3,2},{4,5},{5,4},{6,7},{7,6},{8,9},{9,8},{10,11... | collective-permute-start | bytes 589832 | tf_op jit(solution)/shard_map/ppermute | solution.py:385
  71.1 9.7 %collective-permute-start.17 = (bf16[64,512]{1,0:T(8,128)(2,1)S(1)}, bf16[64,512]{1,0:T(8,128)(2,1)S(1)}, u32[]{:S(2)}, u32[]{:S(2)}) collective-permute-start(bf16[64,512]{1,0:T(8,128)(2,1)S(1)} %get-tuple-element.48), channel_id=1, source_target_pairs={{0,12},{4,0},{8,4},{12,8},{1,13},{5,1},{9,5},{13,9},{2,14},{6,2},{... | collective-permute-start | bytes 196616 | tf_op jit(solution)/shard_map/ppermute | solution.py:382
  75.8 8.0 %collective-permute-start.18 = (bf16[64,512]{1,0:T(8,128)(2,1)S(1)}, bf16[64,512]{1,0:T(8,128)(2,1)S(1)}, u32[]{:S(2)}, u32[]{:S(2)}) collective-permute-start(bf16[64,512]{1,0:T(8,128)(2,1)S(1)} %get-tuple-element.49), channel_id=1, source_target_pairs={{0,8},{4,12},{8,0},{12,4},{1,9},{5,13},{9,1},{13,5},{2,10},{6,14},... | collective-permute-start | bytes 196616 | tf_op jit(solution)/shard_map/ppermute | solution.py:382
  76.2 7.6 %collective-permute-start.19 = (bf16[64,512]{1,0:T(8,128)(2,1)S(1)}, bf16[64,512]{1,0:T(8,128)(2,1)S(1)}, u32[]{:S(2)}, u32[]{:S(2)}) collective-permute-start(bf16[64,512]{1,0:T(8,128)(2,1)S(1)} %get-tuple-element.50), channel_id=1, source_target_pairs={{0,4},{4,8},{8,12},{12,0},{1,5},{5,9},{9,13},{13,1},{2,6},{6,10},{... | collective-permute-start | bytes 196616 | tf_op jit(solution)/shard_map/ppermute | solution.py:382
  76.4 7.6 %collective-permute-start.14 = (bf16[64,512]{1,0:T(8,128)(2,1)S(1)}, bf16[64,512]{1,0:T(8,128)(2,1)S(1)}, u32[]{:S(2)}, u32[]{:S(2)}) collective-permute-start(bf16[64,512]{1,0:T(8,128)(2,1)S(1)} %get-tuple-element.43), channel_id=1, source_target_pairs={{0,12},{4,0},{8,4},{12,8},{1,13},{5,1},{9,5},{13,9},{2,14},{6,2},{... | collective-permute-start | bytes 196616 | tf_op jit(solution)/shard_map/ppermute | solution.py:382
  80.0 8.5 %collective-permute-start.15 = (bf16[64,512]{1,0:T(8,128)(2,1)S(1)}, bf16[64,512]{1,0:T(8,128)(2,1)S(1)}, u32[]{:S(2)}, u32[]{:S(2)}) collective-permute-start(bf16[64,512]{1,0:T(8,128)(2,1)S(1)} %get-tuple-element.44), channel_id=1, source_target_pairs={{0,8},{4,12},{8,0},{12,4},{1,9},{5,13},{9,1},{13,5},{2,10},{6,14},... | collective-permute-start | bytes 196616 | tf_op jit(solution)/shard_map/ppermute | solution.py:382
  80.8 7.8 %collective-permute-start.16 = (bf16[64,512]{1,0:T(8,128)(2,1)S(1)}, bf16[64,512]{1,0:T(8,128)(2,1)S(1)}, u32[]{:S(2)}, u32[]{:S(2)}) collective-permute-start(bf16[64,512]{1,0:T(8,128)(2,1)S(1)} %get-tuple-element.45), channel_id=1, source_target_pairs={{0,4},{4,8},{8,12},{12,0},{1,5},{5,9},{9,13},{13,1},{2,6},{6,10},{... | collective-permute-start | bytes 196616 | tf_op jit(solution)/shard_map/ppermute | solution.py:382
